TPU v7x, 32 devices: a whole 2x2x4 slice. The times are simulated.
32 devices in a mesh: dp: 8 (over z, y), tm: 4 (over x, core).
Axes of the slice: x: 2, y: 2, z: 4, core: 2. Of those that a mesh axis runs over, the one named last changes fastest.
Arguments:
- currents: bfloat16 [8, 32, 128, 1280], P('dp', 'tm'), may hold values from -4 to 4, as said below
- mixing: float32 [32, 32], replicated, may hold values from -1 to 1, as said below
- threshold: float32 [32], replicated, may hold values from -4 to 4, as said below
- weight: bfloat16 [1280, 1280], replicated, may hold values from -0.15625 to 0.15625
- bias: float32 [1280], replicated, may hold values from -3 to 3
- cotangent: bfloat16 [8, 32, 128, 1280], P('dp', 'tm'), may hold values from -6 to 6
Outputs:
- output: bfloat16 [8, 32, 128, 1280], P('dp', 'tm')
- current_grad: bfloat16 [8, 32, 128, 1280], P('dp', 'tm')
- weight_grad: bfloat16 [1280, 1280], P(('dp', 'tm'))
- mixing_grad: float32 [32, 32], replicated
- threshold_grad: float32 [32], replicated
- bias_grad: float32 [1280], replicated
Inputs may be any that keep to these rules, and one draw needn't show every extreme that they name: `currents`: every entry is a multiple of 1/16. `mixing`: every entry is a multiple of 1/16. threshold: every entry is an odd multiple of 1/512, so that every membrane value (a multiple of 1/256) lies at least 1/512 from its threshold.
All inputs are finite; a program needn't handle non-finite values.
Results may differ from a plain program's by a relative error of at most 0.0049.
Values may be sent and summed in bfloat16 or wider, within the bound.
No kernel may reach another device: no remote copies, remote signals or barrier semaphores. Data moves between devices by JAX's collectives and lax.ppermute only.
A program may use at most 128 MiB of HBM per device.

v0:
```python
import jax
import jax.numpy as jnp
from jax import lax
from jax.sharding import PartitionSpec as P


def neuron_forward(currents, mixing, threshold):
    highest = lax.Precision.HIGHEST
    wide_cur = currents.astype(jnp.float32)
    membrane = jnp.einsum("tj,ijnd->itnd", mixing, wide_cur, precision=highest)
    shifted = membrane - threshold[None, :, None, None]
    spikes = (shifted > 0).astype(jnp.bfloat16)
    sigmoid_val = jax.nn.sigmoid(shifted)
    surrogate = sigmoid_val * (1.0 - sigmoid_val)
    return (wide_cur, spikes, surrogate)


def neuron_backward(spike_grad, surrogate, mixing, wide_cur):
    highest = lax.Precision.HIGHEST
    membrane_grad = spike_grad.astype(jnp.float32) * surrogate
    input_grad = jnp.einsum("tj,itnd->ijnd", mixing, membrane_grad, precision=highest).astype(
        jnp.bfloat16
    )
    mixing_term = jnp.einsum("itnd,ijnd->tj", membrane_grad, wide_cur, precision=highest)
    threshold_term = -jnp.sum(membrane_grad, axis=(0, 2, 3))
    return (input_grad, mixing_term, threshold_term)


def body(currents, mixing, threshold, weight, bias, cotangent):
    shape = cotangent.shape
    width = shape[3]
    tok_cur = lax.all_to_all(currents, "tm", split_axis=2, concat_axis=1, tiled=True)
    wide_cur, tok_spikes, surrogate = neuron_forward(tok_cur, mixing, threshold)
    spikes = lax.all_to_all(tok_spikes, "tm", split_axis=1, concat_axis=2, tiled=True)
    spike_rows = spikes.reshape(-1, width)
    grad_rows = cotangent.reshape(-1, width)
    output = (
        (jnp.dot(spike_rows, weight, preferred_element_type=jnp.float32) + bias)
        .astype(jnp.bfloat16)
        .reshape(shape)
    )
    spike_grad = (
        jnp.einsum("re,de->rd", grad_rows, weight, preferred_element_type=jnp.float32)
        .astype(jnp.bfloat16)
        .reshape(shape)
    )
    weight_term = jnp.einsum("rd,re->de", spike_rows, grad_rows, preferred_element_type=jnp.float32)
    bias_term = jnp.sum(grad_rows.astype(jnp.float32), axis=0)
    tok_grad = lax.all_to_all(spike_grad, "tm", split_axis=2, concat_axis=1, tiled=True)
    tok_cgrad, mixing_term, threshold_term = neuron_backward(tok_grad, surrogate, mixing, wide_cur)
    current_grad = lax.all_to_all(tok_cgrad, "tm", split_axis=1, concat_axis=2, tiled=True)
    weight_sum = lax.psum_scatter(weight_term, ("dp", "tm"), scatter_dimension=0, tiled=True)
    mixing_grad, threshold_grad, bias_grad = lax.psum(
        (mixing_term, threshold_term, bias_term), ("dp", "tm")
    )
    return (
        output,
        current_grad,
        weight_sum.astype(jnp.bfloat16),
        mixing_grad,
        threshold_grad,
        bias_grad,
    )


def solution(mesh):
    return jax.shard_map(
        body,
        mesh=mesh,
        in_specs=(P("dp", "tm", None, None), P(), P(), P(), P(), P("dp", "tm", None, None)),
        out_specs=(
            P("dp", "tm", None, None),
            P("dp", "tm", None, None),
            P(("dp", "tm"), None),
            P(),
            P(),
            P(),
        ),
        check_vma=False,
    )
```

profile of v0, /device:TPU:0, one launch (start us, length us, event | category | flops | bytes accessed | tf_op | source)
XLA Modules:
  0.0 300.1 jit_solution(4259585015621780677)
XLA Ops:
  7.2 0.0 copy-start
  7.2 1.9 copy-done
  9.1 5.3 %convolution_convert_fusion = bf16[1024,1280]{1,0:T(8,128)(2,1)S(1)} fusion(bf16[1024,1280]{1,0:T(8,128)(2,1)} %bitcast.77, bf16[1280,1280]{1,0:T(8,128)(2,1)S(1)} %copy-done), kind=kOutput, calls=%fused_computation.12 | convolution fusion | flops 3356753920 | bytes 8519680 | tf_op jit(solution)/shard_map/re,de->rd/dot_general | solution.py:43
  14.4 2.9 copy.33
  17.4 4.5 %all-to-all-start.2 = ((bf16[1,8,128,1280]{3,1,0,2:T(8,128)(2,1)}), bf16[1,8,128,1280]{3,1,0,2:T(8,128)(2,1)}, u32[]{:S(2)}, u32[]{:S(2)}) async-start(bf16[1,8,128,1280]{3,1,0,2:T(8,128)(2,1)} %copy.33), calls=%async_computation.2 | async-start | bytes 5242880 | tf_op jit(solution)/shard_map/all_to_all | solution.py:49
  21.9 4.7 %copy.29 = bf16[1,8,128,1280]{3,1,0,2:T(8,128)(2,1)} copy(bf16[1,8,128,1280]{3,2,1,0:T(8,128)(2,1)} %param.6) | data formatting | bytes 5242880 | tf_op args[0]
  26.6 27.3 %all-to-all-done.2 = bf16[1,8,128,1280]{3,1,0,2:T(8,128)(2,1)} async-done(((bf16[1,8,128,1280]{3,1,0,2:T(8,128)(2,1)}), bf16[1,8,128,1280]{3,1,0,2:T(8,128)(2,1)}, u32[]{:S(2)}, u32[]{:S(2)}) %all-to-all-start.2) | async-done | bytes 2621472 | tf_op jit(solution)/shard_map/all_to_all | solution.py:49
  53.9 4.6 %all-to-all-start = ((bf16[1,8,128,1280]{3,1,0,2:T(8,128)(2,1)}), bf16[1,8,128,1280]{3,1,0,2:T(8,128)(2,1)}, u32[]{:S(2)}, u32[]{:S(2)}) async-start(bf16[1,8,128,1280]{3,1,0,2:T(8,128)(2,1)} %copy.29), calls=%async_computation | async-start | bytes 5242880 | tf_op jit(solution)/shard_map/all_to_all | solution.py:32
  58.5 0.0 reduce-scatter.2.cloned.1.call-start
  58.5 2.2 copy.34
  60.7 0.0 copy-start.4
  60.8 0.0 copy-start.5
  60.8 3.0 convert_bitcast_fusion
  63.7 26.1 %all-to-all-done = bf16[1,8,128,1280]{3,1,0,2:T(8,128)(2,1)} async-done(((bf16[1,8,128,1280]{3,1,0,2:T(8,128)(2,1)}), bf16[1,8,128,1280]{3,1,0,2:T(8,128)(2,1)}, u32[]{:S(2)}, u32[]{:S(2)}) %all-to-all-start) | async-done | bytes 2621472 | tf_op jit(solution)/shard_map/all_to_all | solution.py:32
  89.8 0.0 copy-done.4
  89.8 0.0 copy-done.5
  89.8 10.1 %fusion.24 = (f32[32]{0:T(128)S(1)}, f32[1,32,32,1280]{3,1,2,0:T(8,128)}, f32[32,1280,32]{1,2,0:T(8,128)S(1)}) fusion(f32[32]{0:T(128)S(1)} %copy-done.5, f32[1,4,8,32,1280]{4,3,1,2,0:T(8,128)} %convert_bitcast_fusion, f32[32,32]{1,0:T(8,128)S(1)} %copy-done.4, bf16[1,8,4,32,1280]{4,1,3,2,0:T(8,128)(2,1)} %bitcast), kind=kOutput, calls=%fused_computation.23 | convolution fusion | flops 513802208 | bytes 18354432 | tf_op jit(solution)/shard_map/tj,ijnd->itnd/dot_general | solution.py:10
  100.0 0.8 fusion.11
  100.8 1.4 copy.31
  102.2 33.8 %all_to_all.57 = bf16[1,32,32,1280]{3,2,0,1:T(8,128)(2,1)S(1)} all-to-all(bf16[1,32,32,1280]{3,2,0,1:T(8,128)(2,1)S(1)} %copy.31), channel_id=1, replica_groups=mesh['dp'=8,'tm'=4] {'tm'}, dimensions={1} | all-to-all | bytes 5242880 | tf_op jit(solution)/shard_map/all_to_all | solution.py:34
  136.0 0.0 copy-start.1
  136.0 0.2 copy.32
  136.2 0.0 copy-start.2
  136.3 1.5 copy-done.2
  137.7 1.0 copy-done.1
  138.7 5.6 %fusion.26 = f32[1280,1280]{1,0:T(8,128)} fusion(bf16[1024,1280]{1,0:T(8,128)(2,1)S(1)} %bitcast.79, bf16[1024,1280]{1,0:T(8,128)(2,1)S(1)} %bitcast.78), kind=kOutput, calls=%fused_computation.24 | convolution fusion | flops 3355443200 | bytes 11796480 | tf_op jit(solution)/shard_map/rd,re->de/dot_general | solution.py:47
  144.3 0.0 reduce-scatter.2.cloned.1.call-update
  144.3 7.1 %fusion.8 = bf16[1,32,32,1280]{3,1,2,0:T(8,128)(2,1)S(1)} fusion(f32[1,32,32,1280]{3,1,2,0:T(8,128)} %get-tuple-element.10, f32[32,32]{1,0:T(8,128)S(1)} %copy-done.4), kind=kOutput, calls=%fused_computation.13 | convolution fusion | flops 504627200 | bytes 7868416 | tf_op jit(solution)/shard_map/tj,itnd->ijnd/dot_general | solution.py:21
  151.4 2.9 copy.37
  154.3 4.6 %all-to-all-start.3 = ((bf16[1,32,32,1280]{3,2,0,1:T(8,128)(2,1)}), bf16[1,32,32,1280]{3,2,0,1:T(8,128)(2,1)}, u32[]{:S(2)}, u32[]{:S(2)}) async-start(bf16[1,32,32,1280]{3,2,0,1:T(8,128)(2,1)} %copy.37), calls=%async_computation.3 | async-start | bytes 5242880 | tf_op jit(solution)/shard_map/all_to_all | solution.py:51
  158.9 2.2 convert_reduce_fusion
  161.1 5.8 %fusion.17 = f32[32,32]{1,0:T(8,128)S(1)} fusion(bf16[1,8,4,32,1280]{4,1,3,2,0:T(8,128)(2,1)} %bitcast, f32[1,32,32,1280]{3,1,2,0:T(8,128)} %get-tuple-element.10), kind=kOutput, calls=%fused_computation.20 | convolution fusion | flops 503316480 | bytes 7868416 | tf_op jit(solution)/shard_map/itnd,ijnd->tj/dot_general | solution.py:24
  166.9 89.1 %all-reduce = (f32[32,32]{1,0:T(8,128)}, f32[32]{0:T(128)}, f32[1280]{0:T(1024)}) all-reduce(f32[32,32]{1,0:T(8,128)S(1)} %fusion.17, f32[32]{0:T(128)S(1)} %neg.8, f32[1280]{0:T(1024)S(1)} %convert_reduce_fusion), channel_id=1, replica_groups=mesh['dp'=8,'tm'=4] {'dp','tm'}, use_global_device_ids=true, to_apply=%region_1.0 | all-reduce | flops 2336 | bytes 18688 | tf_op jit(solution)/shard_map/psum | solution.py:53
  256.1 0.0 all-to-all-done.3
  256.1 0.0 copy-start.3
  256.1 0.0 copy-start.6
  256.1 3.6 %copy.38 = bf16[1,8,4,32,1280]{4,3,2,1,0:T(8,128)(2,1)} copy(bf16[1,8,4,32,1280]{4,3,1,2,0:T(8,128)(2,1)} %bitcast.21) | data formatting | bytes 5242880 | tf_op jit(solution)/shard_map/all_to_all | solution.py:51
  259.7 0.0 copy-done.3
  259.7 0.0 copy-done.6
  259.7 4.8 %add_convert_fusion = bf16[1024,1280]{1,0:T(8,128)(2,1)} fusion(bf16[1024,1280]{1,0:T(8,128)(2,1)S(1)} %bitcast.80, bf16[1280,1280]{1,0:T(8,128)(2,1)S(1)} %copy-done, f32[1280]{0:T(1024)S(1)} %copy-done.6), kind=kOutput, calls=%fused_computation.9 | convolution fusion | flops 3358064640 | bytes 8524800 | tf_op jit(solution)/shard_map/dot_general | solution.py:38
  264.5 27.2 %reduce-scatter.2.cloned.1.call-done = f32[40,1280]{1,0:T(8,128)} async-done(((f32[1280,1280]{1,0:T(8,128)}), f32[40,1280]{1,0:T(8,128)}) %reduce-scatter.2.cloned.1.call-update) | async-done | bytes 204816 | tf_op jit(solution)/shard_map/reduce_scatter | solution.py:52
  291.7 1.6 convert_element_type.60
  (1 shorter events, 0.0 us)
Async XLA Ops:
  7.2 1.9 copy-start
  17.4 36.5 %all-to-all-start.2 = ((bf16[1,8,128,1280]{3,1,0,2:T(8,128)(2,1)}), bf16[1,8,128,1280]{3,1,0,2:T(8,128)(2,1)}, u32[]{:S(2)}, u32[]{:S(2)}) async-start(bf16[1,8,128,1280]{3,1,0,2:T(8,128)(2,1)} %copy.33), calls=%async_computation.2 | async-start | bytes 5242880 | tf_op jit(solution)/shard_map/all_to_all | solution.py:49
  53.9 35.9 %all-to-all-start = ((bf16[1,8,128,1280]{3,1,0,2:T(8,128)(2,1)}), bf16[1,8,128,1280]{3,1,0,2:T(8,128)(2,1)}, u32[]{:S(2)}, u32[]{:S(2)}) async-start(bf16[1,8,128,1280]{3,1,0,2:T(8,128)(2,1)} %copy.29), calls=%async_computation | async-start | bytes 5242880 | tf_op jit(solution)/shard_map/all_to_all | solution.py:32
  58.5 233.2 %reduce-scatter.2.cloned.1.call-start = ((), (), s32[]{:S(2)}) async-start(), calls=%async_computation.5 | async-start | bytes 6758400 | tf_op jit(solution)/shard_map/reduce_scatter | solution.py:52
  60.7 29.1 %copy-start.4 = (f32[32,32]{1,0:T(8,128)S(1)}, f32[32,32]{1,0:T(8,128)}, u32[]{:S(2)}) copy-start(f32[32,32]{1,0:T(8,128)} %param.7) | copy-start | bytes 12292
  60.8 29.1 %copy-start.5 = (f32[32]{0:T(128)S(1)}, f32[32]{0:T(128)}, u32[]{:S(2)}) copy-start(f32[32]{0:T(128)} %param.8) | copy-start | bytes 388
  136.0 2.7 copy-start.1
  136.2 1.5 copy-start.2
  154.3 101.7 %all-to-all-start.3 = ((bf16[1,32,32,1280]{3,2,0,1:T(8,128)(2,1)}), bf16[1,32,32,1280]{3,2,0,1:T(8,128)(2,1)}, u32[]{:S(2)}, u32[]{:S(2)}) async-start(bf16[1,32,32,1280]{3,2,0,1:T(8,128)(2,1)} %copy.37), calls=%async_computation.3 | async-start | bytes 5242880 | tf_op jit(solution)/shard_map/all_to_all | solution.py:51
  256.1 3.6 %copy-start.3 = (bf16[1,8,4,32,1280]{4,3,2,1,0:T(8,128)(2,1)S(1)}, bf16[1,8,4,32,1280]{4,3,2,1,0:T(8,128)(2,1)}, u32[]{:S(2)}) copy-start(bf16[1,8,4,32,1280]{4,3,2,1,0:T(8,128)(2,1)} %copy-done.2) | copy-start | bytes 7864324
  256.1 3.6 %copy-start.6 = (f32[1280]{0:T(1024)S(1)}, f32[1280]{0:T(1024)}, u32[]{:S(2)}) copy-start(f32[1280]{0:T(1024)} %param.10) | copy-start | bytes 15364
Sparse Core Ops, SparseCore 0:
  144.4 147.2 reduce-scatter.1
where the time goes:
time: 301 us; the launch traced here: 300 us
  blocking collectives  123 us (41%)
  waiting for transfers between devices  80.6 us (27%)
  matrix products  38.7 us (13%)
  local copies, waits for them, and re-layouts  22.4 us (7%)
  between operations  14.2 us (5%)
  starting transfers between devices  13.7 us (5%)
  other arithmetic  7.52 us (2%)
    psum x1, blocking collectives, body(): lax.psum((mixing_term, threshold_term, bias_term), ('dp', 'tm'))  89.1 us
    all_to_all x1, blocking collectives, body(): lax.all_to_all(tok_spikes, 'tm', split_axis=1, concat_axis=2, tiled=True)  33.8 us
    all_to_all x1, waiting for transfers between devices, body(): lax.all_to_all(spike_grad, 'tm', split_axis=2, concat_axis=1, tiled=True)  27.3 us
    reduce_scatter x1, waiting for transfers between devices, body(): lax.psum_scatter(weight_term, ('dp', 'tm'), scatter_dimension=0, tiled=True)  27.2 us
    all_to_all x1, waiting for transfers between devices, body(): lax.all_to_all(currents, 'tm', split_axis=2, concat_axis=1, tiled=True)  26.1 us
    dot_general x1, matrix products, neuron_forward(): membrane = jnp.einsum('tj,ijnd->itnd', mixing, wide_cur, precision=highest)  10.1 us
    unnamed x15, local copies, waits for them, and re-layouts  9.07 us
    dot_general x1, matrix products, neuron_backward(): jnp.einsum('tj,itnd->ijnd', mixing, membrane_grad, precision=highest)  7.08 us
  transfers between devices with their start and end apart: 4, of which 3 were waited for; matrix products, arithmetic and copies ran while one was open for 12% of the time, Pallas kernels for 0%

commit v1 on v0

v1 whole, which is shorter than its diff:
```python
import functools

import jax
import jax.numpy as jnp
from jax import lax
from jax.experimental import pallas as pl
from jax.experimental.pallas import tpu as pltpu
from jax.sharding import PartitionSpec as P

GROUP = 16
CHUNKS = (32, 32, 32, 32)


def xor_permute(value, axis, size, mask):
    return lax.ppermute(value, axis, [(i, i ^ mask) for i in range(size)])


def forward_kernel(parts, kron_ref, thr_ref, sg_ref, *refs):
    sources = refs[:parts]
    spikes_ref, mg_ref, cross_ref, tsum_ref = refs[-4:]
    steps, group, width = mg_ref.shape
    rows = steps * group

    @pl.when(pl.program_id(0) == 0)
    def _():
        cross_ref[...] = jnp.zeros_like(cross_ref)
        tsum_ref[...] = jnp.zeros_like(tsum_ref)

    kron = kron_ref[...]
    thr = thr_ref[...]
    tile = 256
    for at in range(0, width, tile):
        cur = jnp.concatenate(
            [s[:, :, at : at + tile].reshape(rows, tile) for s in sources], axis=0
        )
        membrane = jnp.dot(kron, cur, preferred_element_type=jnp.float32)
        shifted = membrane - thr
        spikes_ref[:, :, at : at + tile] = (
            jnp.where(shifted > 0, 1.0, 0.0).astype(jnp.bfloat16).reshape(steps, group, tile)
        )
        small = jnp.exp(-jnp.abs(shifted))
        part = 1.0 / (1.0 + small)
        surrogate = small * part * part
        sg = sg_ref[:, :, at : at + tile].reshape(rows, tile).astype(jnp.float32)
        mg = sg * surrogate
        high = mg.astype(jnp.bfloat16)
        low = (mg - high.astype(jnp.float32)).astype(jnp.bfloat16)
        mg_ref[:, :, at : at + tile] = high.reshape(steps, group, tile)
        contract = (((1,), (1,)), ((), ()))
        cross_ref[...] += lax.dot_general(
            high, cur, contract, preferred_element_type=jnp.float32
        ) + lax.dot_general(low, cur, contract, preferred_element_type=jnp.float32)
        total = mg[:, :128]
        for piece in range(128, tile, 128):
            total = total + mg[:, piece : piece + 128]
        tsum_ref[...] += total


def backward_kernel(parts, kron_ref, *refs):
    sources = refs[:parts]
    out_ref = refs[-1]
    steps, group, width = out_ref.shape
    rows = steps * group
    kron = kron_ref[...]
    tile = 256
    for at in range(0, width, tile):
        mg = jnp.concatenate(
            [s[:, :, at : at + tile].reshape(rows, tile) for s in sources], axis=0
        )
        grad = jnp.dot(kron, mg, preferred_element_type=jnp.float32)
        out_ref[:, :, at : at + tile] = grad.astype(jnp.bfloat16).reshape(steps, group, tile)


def forward_chunk(start, size, kron, thr, spike_grad, sources, spikes):
    steps, tokens, width = spike_grad.shape
    parts = len(sources)
    rows = steps * GROUP
    first = start // GROUP
    whole = pl.BlockSpec((steps, GROUP, width), lambda g: (0, g + first, 0))
    piece = pl.BlockSpec((steps, GROUP, width), lambda g: (0, g, 0))
    fixed = lambda shape: pl.BlockSpec(shape, lambda g: (0, 0))
    args = [kron, thr, spike_grad, *sources]
    specs = [fixed(kron.shape), fixed(thr.shape), whole, whole, whole] + [piece] * (parts - 2)
    aliases = {}
    if spikes is not None:
        aliases = {len(args): 0}
        args.append(spikes)
        specs.append(pl.BlockSpec(memory_space=pl.ANY))
    return pl.pallas_call(
        functools.partial(forward_kernel, parts),
        grid=(size // GROUP,),
        in_specs=specs,
        out_specs=(whole, piece, fixed((rows, parts * rows)), fixed((rows, 128))),
        out_shape=(
            jax.ShapeDtypeStruct((steps, tokens, width), jnp.bfloat16),
            jax.ShapeDtypeStruct((steps, size, width), jnp.bfloat16),
            jax.ShapeDtypeStruct((rows, parts * rows), jnp.float32),
            jax.ShapeDtypeStruct((rows, 128), jnp.float32),
        ),
        input_output_aliases=aliases,
        cost_estimate=pl.CostEstimate(
            flops=6 * rows * parts * rows * width * (size // GROUP),
            bytes_accessed=2 * (parts + 3) * steps * size * width,
            transcendentals=2 * steps * size * width,
        ),
        name="forward_chunk",
    )(*args)


def backward_chunk(start, kron, sources, grad, tokens):
    steps, size, width = sources[0].shape
    first = start // GROUP
    piece = pl.BlockSpec((steps, GROUP, width), lambda g: (0, g, 0))
    args = [kron, *sources]
    specs = [pl.BlockSpec(kron.shape, lambda g: (0, 0))] + [piece] * len(sources)
    aliases = {}
    if grad is not None:
        aliases = {len(args): 0}
        args.append(grad)
        specs.append(pl.BlockSpec(memory_space=pl.ANY))
    return pl.pallas_call(
        functools.partial(backward_kernel, len(sources)),
        grid=(size // GROUP,),
        in_specs=specs,
        out_specs=pl.BlockSpec((steps, GROUP, width), lambda g: (0, g + first, 0)),
        out_shape=jax.ShapeDtypeStruct((steps, tokens, width), jnp.bfloat16),
        input_output_aliases=aliases,
        cost_estimate=pl.CostEstimate(
            flops=2 * len(sources) * (steps * GROUP) ** 2 * width * (size // GROUP),
            bytes_accessed=2 * (len(sources) + 1) * steps * size * width,
            transcendentals=0,
        ),
        name="backward_chunk",
    )(*args)


def iota2(shape, dim):
    return lax.broadcasted_iota(jnp.int32, shape, dim)


def selectors(me, parts, steps):
    rows, cols, total = steps * GROUP, parts * steps * GROUP, parts * steps
    shift, depth = GROUP.bit_length() - 1, (steps * GROUP).bit_length() - 1
    own = me * steps + lax.shift_right_logical(iota2((rows, total), 0), shift)
    left = own == iota2((rows, total), 1)
    at = iota2((total, cols), 1)
    source = jnp.bitwise_xor(me, lax.shift_right_logical(at, depth))
    step = jnp.bitwise_and(lax.shift_right_logical(at, shift), steps - 1)
    right = source * steps + step == iota2((total, cols), 0)
    same = jnp.bitwise_and(iota2((rows, cols), 0), GROUP - 1) == jnp.bitwise_and(
        iota2((rows, cols), 1), GROUP - 1
    )
    return left, right, same


def kron_kernel(parts, steps, me_ref, mixing_ref, thr_ref, fwd_ref, bwd_ref, rows_ref):
    left, right, same = selectors(me_ref[0], parts, steps)
    mixing = mixing_ref[...].astype(jnp.bfloat16)
    one = lambda m: jnp.where(m, 1.0, 0.0).astype(jnp.bfloat16)
    dot = functools.partial(lax.dot_general, preferred_element_type=jnp.float32)
    for ref, dims in ((fwd_ref, (1, 0)), (bwd_ref, (1, 1))):
        first = dot(one(left), mixing, (((1,), (dims[1],)), ((), ()))).astype(jnp.bfloat16)
        wide = dot(first, one(right), (((1,), (0,)), ((), ())))
        ref[...] = jnp.where(same, wide, 0.0).astype(jnp.bfloat16)
    thr = jnp.broadcast_to(thr_ref[...], left.shape)
    rows_ref[...] = jnp.sum(jnp.where(left, thr, 0.0), axis=1, keepdims=True)


def build_krons(me, mixing, threshold, parts, steps):
    rows = steps * GROUP
    vmem = pl.BlockSpec(memory_space=pltpu.VMEM)
    wide = jax.ShapeDtypeStruct((rows, parts * rows), jnp.bfloat16)
    return pl.pallas_call(
        functools.partial(kron_kernel, parts, steps),
        in_specs=[pl.BlockSpec(memory_space=pltpu.SMEM), vmem, vmem],
        out_specs=(vmem, vmem, vmem),
        out_shape=(wide, wide, jax.ShapeDtypeStruct((rows, 1), jnp.float32)),
        name="build_krons",
    )(me.reshape(1), mixing, threshold.reshape(1, -1))


def sums_kernel(parts, steps, count, me_ref, bias_ref, *refs):
    crosses, tsums, out_ref = refs[:count], refs[count : 2 * count], refs[-1]
    left, right, same = selectors(me_ref[0], parts, steps)
    exact = functools.partial(
        lax.dot_general, precision=lax.Precision.HIGHEST, preferred_element_type=jnp.float32
    )
    one = lambda m: jnp.where(m, 1.0, 0.0)
    cross, tsum = crosses[0][...], tsums[0][...]
    for c, t in zip(crosses[1:], tsums[1:]):
        cross, tsum = cross + c[...], tsum + t[...]
    cross = jnp.where(same, cross, 0.0)
    narrow = exact(cross, one(right), (((1,), (1,)), ((), ())))
    total = parts * steps
    lane = iota2((narrow.shape[0], 128), 1)
    row_sum = -jnp.sum(tsum, axis=1, keepdims=True)
    block = jnp.concatenate(
        [narrow, jnp.zeros((narrow.shape[0], 128 - total), jnp.float32)], axis=1
    ) + jnp.where(lane == total, row_sum, 0.0)
    out_ref[:total, :] = exact(one(left), block, (((0,), (0,)), ((), ())))
    out_ref[total:, :] = bias_ref[...]


def pack_sums(me, bias_rows, crosses, tsums, parts, steps):
    vmem = pl.BlockSpec(memory_space=pltpu.VMEM)
    rows = parts * steps + bias_rows.shape[0]
    return pl.pallas_call(
        functools.partial(sums_kernel, parts, steps, len(crosses)),
        in_specs=[pl.BlockSpec(memory_space=pltpu.SMEM)] + [vmem] * (1 + 2 * len(crosses)),
        out_specs=vmem,
        out_shape=jax.ShapeDtypeStruct((rows, 128), jnp.float32),
        name="pack_sums",
    )(me.reshape(1), bias_rows, *crosses, *tsums)


def after(value, *earlier):
    return lax.optimization_barrier((value, *earlier))[0]


def body(ndp, ntm, currents, mixing, threshold, weight, bias, cotangent):
    _, steps, tokens, width = currents.shape
    me = lax.axis_index("tm")
    bits = lambda n: n.bit_length() - 1
    own = currents[0]
    spans = [(sum(CHUNKS[:i]), n) for i, n in enumerate(CHUNKS)]
    far = range(2, ntm, 2)

    cuts = [own[:, s : s + n] for s, n in spans]
    across = [[xor_permute(cut, "tm", ntm, k) for k in far] for cut in cuts]
    sibling = xor_permute(own, "tm", ntm, 1)
    kron_fwd, kron_bwd, thr_rows = build_krons(me, mixing, threshold, ntm, steps)

    grad_rows = cotangent.reshape(-1, width)
    spike_grad = (
        jnp.einsum("re,de->rd", grad_rows, weight, preferred_element_type=jnp.float32)
        .astype(jnp.bfloat16)
        .reshape(steps, tokens, width)
    )
    bias_term = jnp.sum(grad_rows.astype(jnp.float32), axis=0)

    def pass_on(values, token):
        found = []
        for value in values:
            value = after(value, token)
            found += [value, xor_permute(value, "tm", ntm, 1)]
        return found

    spikes, token = None, spike_grad
    crosses, tsums, mgs, mg_across, mg_sibling = [], [], [], [], []
    for (s, n), got in zip(spans, across):
        spikes, mg, cross, tsum = forward_chunk(
            s, n, kron_fwd, thr_rows, spike_grad, [own, sibling] + pass_on(got, token), spikes
        )
        token = tsum
        crosses.append(cross)
        tsums.append(tsum)
        mgs.append(mg)
        mg_across.append([xor_permute(mg, "tm", ntm, k) for k in far])
        mg_sibling.append(xor_permute(mg, "tm", ntm, 1))

    spike_rows = spikes.reshape(-1, width)
    weight_term = jnp.einsum("rd,re->de", spike_rows, grad_rows, preferred_element_type=jnp.float32)
    sums = pack_sums(me, bias_term.reshape(-1, 128), crosses, tsums, ntm, steps)

    bdp, btm = bits(ndp), bits(ntm)
    shard = width // (ndp * ntm)
    names = [("dp", b) for b in range(bdp - 1, -1, -1)] + [("tm", b) for b in range(btm - 1, -1, -1)]
    sizes = {"dp": ndp, "tm": ntm}
    y, zs, xs = ("dp", 0), [("dp", b) for b in range(1, bdp)], [("tm", b) for b in range(1, btm)]

    def halve(value, left, bit, dtype):
        axis, b = bit
        place = left.index(bit)
        beta = (lax.axis_index(axis) >> b) & 1
        keep = lax.dynamic_index_in_dim(value, beta, place, keepdims=False)
        send = lax.dynamic_index_in_dim(value, 1 - beta, place, keepdims=False)
        got = xor_permute(send.astype(dtype), axis, sizes[axis], 1 << b)
        return keep + got.astype(jnp.float32), [x for x in left if x != bit]

    value = weight_term.reshape((2,) * (bdp + btm) + (shard, width))
    value, left = halve(value, names, ("tm", 0), jnp.float32)
    half = width // 2
    done = []
    for part, route in ((value[..., :half], [y] + zs), (value[..., half:], zs + [y])):
        rest = left
        for bit in route:
            part, rest = halve(part, rest, bit, jnp.bfloat16)
        done.append(part)
    value = jnp.concatenate(done, axis=-1)
    for bit in xs:
        value, rest = halve(value, rest, bit, jnp.bfloat16)
    weight_grad = value.astype(jnp.bfloat16)

    for axis, b in [("tm", 0), y] + zs + xs:
        sums = sums + xor_permute(sums, axis, sizes[axis], 1 << b)
    total = ntm * steps
    mixing_grad, threshold_grad = sums[:total, :total], sums[:total, total]
    bias_grad = sums[total:].reshape(-1)

    output = (
        (jnp.dot(spike_rows, weight, preferred_element_type=jnp.float32) + bias)
        .astype(jnp.bfloat16)
        .reshape(cotangent.shape)
    )

    grad, token = None, output
    for (s, n), mg, got, near in zip(spans, mgs, mg_across, mg_sibling):
        grad = backward_chunk(s, kron_bwd, [mg, near] + pass_on(got, token), grad, tokens)
        token = output
    return (output, grad[None], weight_grad, mixing_grad, threshold_grad, bias_grad)


def solution(mesh):
    return jax.shard_map(
        functools.partial(body, mesh.shape["dp"], mesh.shape["tm"]),
        mesh=mesh,
        in_specs=(P("dp", "tm", None, None), P(), P(), P(), P(), P("dp", "tm", None, None)),
        out_specs=(
            P("dp", "tm", None, None),
            P("dp", "tm", None, None),
            P(("dp", "tm"), None),
            P(),
            P(),
            P(),
        ),
        check_vma=False,
    )
```

time: 301 us -> 210 us (0.70)
  blocking collectives: 123 us -> 0 us
  Pallas kernels: 0 us -> 39.4 us
  matrix products: 38.7 us -> 15.8 us
  waiting for transfers between devices: 80.6 us -> 101 us
  starting transfers between devices: 13.7 us -> 29.1 us
  between operations: 14.2 us -> 0.9 us
  local copies, waits for them, and re-layouts: 22.4 us -> 15.3 us
    ppermute x0 -> x34, waiting for transfers between devices: none -> 101 us  [xor_permute(): return lax.ppermute(value, axis, [(i, i ^ mask) for i in range(size)])]
    psum x1 -> x0, blocking collectives: 89.1 us -> none  [body(): lax.psum((mixing_term, threshold_term, bias_term), ('dp', 'tm'))]
    all_to_all x3 -> x0, waiting for transfers between devices: 53.4 us -> none  [the longest x1 27.3 us: body(): lax.all_to_all(spike_grad, 'tm', split_axis=2, concat_axis=1, tiled=True)]
    pallas_call x0 -> x10, Pallas kernels: none -> 39.4 us  [the longest x4 23.8 us: forward_chunk(): pl.pallas_call(functools.partial(forward_kernel, parts), grid=(size // GR...]
    all_to_all x1 -> x0, blocking collectives: 33.8 us -> none  [body(): lax.all_to_all(tok_spikes, 'tm', split_axis=1, concat_axis=2, tiled=True)]
    ppermute x0 -> x34, starting transfers between devices: none -> 29.1 us  [xor_permute(): return lax.ppermute(value, axis, [(i, i ^ mask) for i in range(size)])]
    reduce_scatter x1 -> x0, waiting for transfers between devices: 27.2 us -> none  [body(): lax.psum_scatter(weight_term, ('dp', 'tm'), scatter_dimension=0, tiled=True)]
    dot_general x3 -> x0, matrix products: 23 us -> none  [the longest x1 10.1 us: neuron_forward(): membrane = jnp.einsum('tj,ijnd->itnd', mixing, wide_cur, precision=highest)]
  transfers between devices with their start and end apart: 4 -> 34, of which waited for: 3 -> 18; matrix products, arithmetic and copies ran while one was open for 12% -> 10% of each run, Pallas kernels for 0% -> 16%
where the time goes in v1:
time: 210 us
  waiting for transfers between devices  101 us (48%)
  Pallas kernels  39.4 us (19%)
  starting transfers between devices  29.1 us (14%)
  matrix products  15.8 us (8%)
  local copies, waits for them, and re-layouts  15.3 us (7%)
  other arithmetic  7.63 us (4%)
    ppermute x34, waiting for transfers between devices, xor_permute(): return lax.ppermute(value, axis, [(i, i ^ mask) for i in range(size)])  101 us
    ppermute x34, starting transfers between devices, xor_permute(): return lax.ppermute(value, axis, [(i, i ^ mask) for i in range(size)])  29.1 us
    pallas_call x4, Pallas kernels, forward_chunk(): pl.pallas_call(functools.partial(forward_kernel, parts), grid=(size // GR...  23.8 us
    pallas_call x4, Pallas kernels, backward_chunk(): pl.pallas_call(functools.partial(backward_kernel, len(sources)), grid=(si...  11.3 us
    dot_general x1, matrix products, body(): jnp.einsum('rd,re->de', spike_rows, grad_rows, preferred_element_type=jnp...  6.17 us
    dot_general x1, matrix products, body(): jnp.einsum('re,de->rd', grad_rows, weight, preferred_element_type=jnp.flo...  4.85 us
    dot_general x1, matrix products, body(): jnp.dot(spike_rows, weight, preferred_element_type=jnp.float32) + bias  4.83 us
    dot_general x1, local copies, waits for them, and re-layouts, body(): jnp.einsum('rd,re->de', spike_rows, grad_rows, preferred_element_type=jnp...  4.39 us
  transfers between devices with their start and end apart: 34, of which 18 were waited for; matrix products, arithmetic and copies ran while one was open for 10% of the time, Pallas kernels for 16%

profile of v1, /device:TPU:0, one launch (start us, length us, event | category | flops | bytes accessed | tf_op | source)
XLA Modules:
  0.0 209.6 jit_solution(5623857741420377511)
XLA Ops:
  1.2 3.3 %fusion.15 = (bf16[8,32,1280]{2,1,0:T(8,128)(2,1)S(1)}, bf16[8,32,1280]{2,1,0:T(8,128)(2,1)}, bf16[8,32,1280]{2,1,0:T(8,128)(2,1)}, bf16[8,32,1280]{2,1,0:T(8,128)(2,1)}) fusion(bf16[8,128,1280]{2,1,0:T(8,128)(2,1)} %bitcast.63), kind=kLoop, calls=%fused_computation.40 | loop fusion | bytes 5242880 | tf_op jit(solution)/shard_map/slice | solution.py:228
  4.4 2.4 %collective-permute-start.4 = (bf16[8,32,1280]{2,1,0:T(8,128)(2,1)S(1)}, bf16[8,32,1280]{2,1,0:T(8,128)(2,1)}, u32[]{:S(2)}, u32[]{:S(2)}) collective-permute-start(bf16[8,32,1280]{2,1,0:T(8,128)(2,1)S(1)} %get-tuple-element.62), channel_id=1, source_target_pairs={{0,2},{1,3},{2,0},{3,1},{4,6},{5,7},{6,4},{7,5},{8,10},{9,11},{10,... | collective-permute-start | bytes 1966088 | tf_op jit(solution)/shard_map/ppermute | solution.py:15
  6.8 4.8 %convolution_convert_fusion = bf16[1024,1280]{1,0:T(8,128)(2,1)} fusion(bf16[1024,1280]{1,0:T(8,128)(2,1)S(1)} %bitcast.76, bf16[1280,1280]{1,0:T(8,128)(2,1)S(1)} %copy-done), kind=kOutput, calls=%fused_computation.2 | convolution fusion | flops 3356753920 | bytes 8519680 | tf_op jit(solution)/shard_map/re,de->rd/dot_general | solution.py:235
  11.7 10.8 %collective-permute-done.4.refs_2_ = bf16[8,32,1280]{2,1,0:T(8,128)(2,1)} collective-permute-done((bf16[8,32,1280]{2,1,0:T(8,128)(2,1)S(1)}, bf16[8,32,1280]{2,1,0:T(8,128)(2,1)}, u32[]{:S(2)}, u32[]{:S(2)}) %collective-permute-start.4) | collective-permute-done | bytes 655392 | tf_op jit(solution)/shard_map/ppermute | solution.py:15
  22.6 1.7 collective-permute-start.3
  24.3 1.8 build_krons.1
  26.1 6.0 %forward_chunk.4 = (bf16[8,128,1280]{2,1,0:T(8,128)(2,1)}, bf16[8,32,1280]{2,1,0:T(8,128)(2,1)}, f32[128,512]{1,0:T(8,128)}, f32[128,128]{1,0:T(8,128)}) custom-call(bf16[128,512]{1,0:T(8,128)(2,1)} %get-tuple-element.33.kron_ref, f32[128,1]{1,0:T(8,128)} %get-tuple-element.34.thr_ref, bf16[8,128,1280]{2,1,0:T(8,128)(2,1)} %bitcast.69, ...), custom_call_target="tpu_custom_call" | custom-call | flops 1006632960 | bytes 4587520 | tf_op jit(solution)/shard_map/forward_chunk/pallas_call | solution.py:89
  32.1 7.9 %collective-permute-done.3.refs_2_ = bf16[8,32,1280]{2,1,0:T(8,128)(2,1)} collective-permute-done((bf16[8,32,1280]{2,1,0:T(8,128)(2,1)}, bf16[8,32,1280]{2,1,0:T(8,128)(2,1)}, u32[]{:S(2)}, u32[]{:S(2)}) %collective-permute-start.3) | collective-permute-done | bytes 655392 | tf_op jit(solution)/shard_map/ppermute | solution.py:15
  40.0 1.7 collective-permute-start.2
  42.5 5.9 %forward_chunk.5 = (bf16[8,128,1280]{2,1,0:T(8,128)(2,1)}, bf16[8,32,1280]{2,1,0:T(8,128)(2,1)}, f32[128,512]{1,0:T(8,128)}, f32[128,128]{1,0:T(8,128)}) custom-call(bf16[128,512]{1,0:T(8,128)(2,1)} %get-tuple-element.33.kron_ref, f32[128,1]{1,0:T(8,128)} %get-tuple-element.34.thr_ref, ...), custom_call_target="tpu_custom_call", output_to_operand_aliasing={{0}: (7, {})} | custom-call | flops 1006632960 | bytes 4587520 | tf_op jit(solution)/shard_map/forward_chunk/pallas_call | solution.py:89
  48.4 9.1 %collective-permute-done.2.refs_2_ = bf16[8,32,1280]{2,1,0:T(8,128)(2,1)} collective-permute-done((bf16[8,32,1280]{2,1,0:T(8,128)(2,1)}, bf16[8,32,1280]{2,1,0:T(8,128)(2,1)}, u32[]{:S(2)}, u32[]{:S(2)}) %collective-permute-start.2) | collective-permute-done | bytes 655392 | tf_op jit(solution)/shard_map/ppermute | solution.py:15
  57.5 1.7 collective-permute-start.1
  59.9 5.9 %forward_chunk.6 = (bf16[8,128,1280]{2,1,0:T(8,128)(2,1)}, bf16[8,32,1280]{2,1,0:T(8,128)(2,1)}, f32[128,512]{1,0:T(8,128)}, f32[128,128]{1,0:T(8,128)}) custom-call(bf16[128,512]{1,0:T(8,128)(2,1)} %get-tuple-element.33.kron_ref, f32[128,1]{1,0:T(8,128)} %get-tuple-element.34.thr_ref, ...), custom_call_target="tpu_custom_call", output_to_operand_aliasing={{0}: (7, {})} | custom-call | flops 1006632960 | bytes 4587520 | tf_op jit(solution)/shard_map/forward_chunk/pallas_call | solution.py:89
  65.9 9.1 %collective-permute-done.1.refs_2_ = bf16[8,32,1280]{2,1,0:T(8,128)(2,1)} collective-permute-done((bf16[8,32,1280]{2,1,0:T(8,128)(2,1)}, bf16[8,32,1280]{2,1,0:T(8,128)(2,1)}, u32[]{:S(2)}, u32[]{:S(2)}) %collective-permute-start.1) | collective-permute-done | bytes 655392 | tf_op jit(solution)/shard_map/ppermute | solution.py:15
  74.9 2.4 %collective-permute-done.8.refs_3_ = bf16[8,32,1280]{2,1,0:T(8,128)(2,1)} collective-permute-done((bf16[8,32,1280]{2,1,0:T(8,128)(2,1)}, bf16[8,32,1280]{2,1,0:T(8,128)(2,1)}, u32[]{:S(2)}, u32[]{:S(2)}) %collective-permute-start.8) | collective-permute-done | bytes 655392 | tf_op jit(solution)/shard_map/ppermute | solution.py:15
  77.4 5.9 %forward_chunk.7 = (bf16[8,128,1280]{2,1,0:T(8,128)(2,1)}, bf16[8,32,1280]{2,1,0:T(8,128)(2,1)}, f32[128,512]{1,0:T(8,128)}, f32[128,128]{1,0:T(8,128)}) custom-call(bf16[128,512]{1,0:T(8,128)(2,1)} %get-tuple-element.33.kron_ref, f32[128,1]{1,0:T(8,128)} %get-tuple-element.34.thr_ref, ...), custom_call_target="tpu_custom_call", output_to_operand_aliasing={{0}: (7, {})} | custom-call | flops 1006632960 | bytes 4587520 | tf_op jit(solution)/shard_map/forward_chunk/pallas_call | solution.py:89
  83.3 4.4 %copy.19 = bf16[1280,1024]{1,0:T(8,128)(2,1)} copy(bf16[1280,1024]{0,1:T(8,128)(2,1)} %bitcast.73) | data formatting | bytes 5242880 | tf_op jit(solution)/shard_map/rd,re->de/dot_general | solution.py:262
  87.7 6.2 %fusion.16 = f32[2,2,2,2,2,40,1280]{6,5,4,3,2,1,0:T(8,128)S(1)} fusion(bf16[2,2,2,2,2,40,1024]{6,5,4,3,2,1,0:T(8,128)(2,1)} %bitcast.77, bf16[1024,1280,1,1,1,1,1]{1,0,6,5,4,3,2:T(8,128)(2,1)} %bitcast.75), kind=kOutput, calls=%fused_computation.41 | convolution fusion | flops 3355443200 | bytes 11796480 | tf_op jit(solution)/shard_map/rd,re->de/dot_general | solution.py:262
  93.9 2.1 %dynamic-slice_bitcast_fusion = f32[2,2,2,2,40,1280]{5,4,3,2,1,0:T(8,128)} fusion(f32[2,2,2,2,2,40,1280]{6,5,4,3,2,1,0:T(8,128)S(1)} %fusion.16, s32[]{:T(128)S(6)} %select_n.44), kind=kLoop, calls=%fused_computation.4 | loop fusion | bytes 6553604 | tf_op jit(solution)/shard_map/jit(dynamic_index_in_dim)/squeeze | solution.py:276
  96.0 2.0 copy-done.2
  99.1 2.5 %pack_sums.1 = f32[42,128]{1,0:T(8,128)} custom-call(s32[1]{0:T(128)} %bitcast.me_ref, f32[10,128]{1,0:T(8,128)} %bitcast.78, f32[128,512]{1,0:T(8,128)} %get-tuple-element.55.refs_0_, f32[128,512]{1,0:T(8,128)} %get-tuple-element.56.refs_1_, f32[128,512]{1,0:T(8,128)} %get-tuple-element.57.refs_2_, f32[128,512]{1,0:T(8,128)} %get-tuple-element.58.refs_3_, ...), custom_call_target="tpu_custom_call" | custom-call | tf_op jit(solution)/shard_map/pack_sums/pallas_call | solution.py:207
  102.0 2.1 collective-permute-done.29
  104.8 1.8 collective-permute-start.30
  106.6 2.1 collective-permute-done.30
  108.7 1.8 collective-permute-start.31
  110.5 2.0 collective-permute-done.31
  112.5 2.8 %collective-permute-start.32 = (f32[42,128]{1,0:T(8,128)S(1)}, f32[42,128]{1,0:T(8,128)S(1)}, u32[]{:S(2)}, u32[]{:S(2)}) collective-permute-start(f32[42,128]{1,0:T(8,128)S(1)} %add.117), channel_id=1, source_target_pairs={{0,16},{4,20},{8,24},{12,28},{16,0},{20,4},{24,8},{28,12},{1,17},{... | collective-permute-start | bytes 64520 | tf_op jit(solution)/shard_map/ppermute | solution.py:15
  115.3 1.5 collective-permute-start.19
  117.4 1.5 collective-permute-start.13
  119.5 3.3 %bitcast_add_fusion = f32[2,2,2,2,40,1280]{5,4,3,2,1,0:T(8,128)S(1)} fusion(f32[2,2,2,2,40,1280]{5,4,3,2,1,0:T(8,128)} %collective-permute-done.21, f32[2,2,2,2,2,40,1280]{6,5,4,3,2,1,0:T(8,128)} %copy-done.2, s32[]{:T(128)S(6)} %select_n.43), kind=kLoop, calls=%fused_computation.3 | loop fusion | flops 819200 | bytes 9830404 | tf_op jit(solution)/shard_map/add | solution.py:278
  123.2 1.6 collective-permute-start.22
  124.8 4.8 %add_convert_fusion = bf16[1024,1280]{1,0:T(8,128)(2,1)} fusion(bf16[1024,1280]{1,0:T(8,128)(2,1)S(1)} %bitcast.74, bf16[1280,1280]{1,0:T(8,128)(2,1)S(1)} %copy-done, f32[1280]{0:T(1024)S(1)} %copy-done.14), kind=kOutput, calls=%fused_computation.1 | convolution fusion | flops 3358064640 | bytes 8524800 | tf_op jit(solution)/shard_map/dot_general | solution.py:301
  129.6 3.6 %collective-permute-done.19.refs_2_ = bf16[8,32,1280]{2,1,0:T(8,128)(2,1)S(1)} collective-permute-done((bf16[8,32,1280]{2,1,0:T(8,128)(2,1)}, bf16[8,32,1280]{2,1,0:T(8,128)(2,1)S(1)}, u32[]{:S(2)}, u32[]{:S(2)}) %collective-permute-start.19) | collective-permute-done | bytes 655392 | tf_op jit(solution)/shard_map/ppermute | solution.py:15
  133.2 14.0 %collective-permute-done.16.refs_2_ = bf16[8,32,1280]{2,1,0:T(8,128)(2,1)S(1)} collective-permute-done((bf16[8,32,1280]{2,1,0:T(8,128)(2,1)}, bf16[8,32,1280]{2,1,0:T(8,128)(2,1)S(1)}, u32[]{:S(2)}, u32[]{:S(2)}) %collective-permute-start.16) | collective-permute-done | bytes 655392 | tf_op jit(solution)/shard_map/ppermute | solution.py:15
  147.3 11.6 %collective-permute-done.13.refs_2_ = bf16[8,32,1280]{2,1,0:T(8,128)(2,1)} collective-permute-done((bf16[8,32,1280]{2,1,0:T(8,128)(2,1)}, bf16[8,32,1280]{2,1,0:T(8,128)(2,1)}, u32[]{:S(2)}, u32[]{:S(2)}) %collective-permute-start.13) | collective-permute-done | bytes 655392 | tf_op jit(solution)/shard_map/ppermute | solution.py:15
  158.9 1.5 collective-permute-start.10
  160.4 1.6 collective-permute-start.25
  163.4 6.8 %collective-permute-done.25 = bf16[2,2,2,40,640]{4,3,2,1,0:T(8,128)(2,1)S(1)} collective-permute-done((bf16[2,2,2,40,640]{4,3,2,1,0:T(8,128)(2,1)S(1)}, bf16[2,2,2,40,640]{4,3,2,1,0:T(8,128)(2,1)S(1)}, u32[]{:S(2)}, u32[]{:S(2)}) %collective-permute-start.25) | collective-permute-done | bytes 409632 | tf_op jit(solution)/shard_map/ppermute | solution.py:15
  170.3 2.0 collective-permute-start.23
  172.4 5.2 %collective-permute-done.23 = bf16[2,2,40,640]{3,2,1,0:T(8,128)(2,1)S(1)} collective-permute-done((bf16[2,2,40,640]{3,2,1,0:T(8,128)(2,1)S(1)}, bf16[2,2,40,640]{3,2,1,0:T(8,128)(2,1)S(1)}, u32[]{:S(2)}, u32[]{:S(2)}) %collective-permute-start.23) | collective-permute-done | bytes 204832 | tf_op jit(solution)/shard_map/ppermute | solution.py:15
  177.6 10.4 %collective-permute-done.26 = bf16[2,2,40,640]{3,2,1,0:T(8,128)(2,1)S(1)} collective-permute-done((bf16[2,2,40,640]{3,2,1,0:T(8,128)(2,1)S(1)}, bf16[2,2,40,640]{3,2,1,0:T(8,128)(2,1)S(1)}, u32[]{:S(2)}, u32[]{:S(2)}) %collective-permute-start.26) | collective-permute-done | bytes 204832 | tf_op jit(solution)/shard_map/ppermute | solution.py:15
  188.1 1.6 collective-permute-start.27
  190.9 2.6 %collective-permute-done.24 = bf16[2,40,640]{2,1,0:T(8,128)(2,1)S(1)} collective-permute-done((bf16[2,40,640]{2,1,0:T(8,128)(2,1)S(1)}, bf16[2,40,640]{2,1,0:T(8,128)(2,1)S(1)}, u32[]{:S(2)}, u32[]{:S(2)}) %collective-permute-start.24) | collective-permute-done | bytes 102432 | tf_op jit(solution)/shard_map/ppermute | solution.py:15
  196.7 2.8 %backward_chunk.4.refs_4_ = bf16[8,128,1280]{2,1,0:T(8,128)(2,1)} custom-call(bf16[128,512]{1,0:T(8,128)(2,1)} %get-tuple-element.46.kron_ref, bf16[8,32,1280]{2,1,0:T(8,128)(2,1)} %get-tuple-element.53.refs_0_, bf16[8,32,1280]{2,1,0:T(8,128)(2,1)} %copy-done.10, bf16[8,32,1280]{2,1,0:T(8,128)(2,1)} %copy-done.8, bf16[8,32,1280]{2,1,0:T(8,128)(2,1)} %copy-done.13), custom_call_target="tpu_custom_call" | custom-call | flops 335544320 | bytes 3276800 | tf_op jit(solution)/shard_map/backward_chunk/pallas_call | solution.py:121
  199.5 2.8 %backward_chunk.5.refs_4_ = bf16[8,128,1280]{2,1,0:T(8,128)(2,1)} custom-call(bf16[128,512]{1,0:T(8,128)(2,1)} %get-tuple-element.46.kron_ref, bf16[8,32,1280]{2,1,0:T(8,128)(2,1)} %get-tuple-element.51.refs_0_, bf16[8,32,1280]{2,1,0:T(8,128)(2,1)} %copy-done.11, bf16[8,32,1280]{2,1,0:T(8,128)(2,1)} %copy-done.9, ...), custom_call_target="tpu_custom_call", output_to_operand_aliasing={{}: (5, {})} | custom-call | flops 335544320 | bytes 3276800 | tf_op jit(solution)/shard_map/backward_chunk/pallas_call | solution.py:121
  202.3 2.8 %backward_chunk.6.refs_4_ = bf16[8,128,1280]{2,1,0:T(8,128)(2,1)} custom-call(bf16[128,512]{1,0:T(8,128)(2,1)} %get-tuple-element.46.kron_ref, bf16[8,32,1280]{2,1,0:T(8,128)(2,1)} %get-tuple-element.49.refs_0_, bf16[8,32,1280]{2,1,0:T(8,128)(2,1)} %collective-permute-done.12.refs_1_, ...), custom_call_target="tpu_custom_call", output_to_operand_aliasing={{}: (5, {})} | custom-call | flops 335544320 | bytes 3276800 | tf_op jit(solution)/shard_map/backward_chunk/pallas_call | solution.py:121
  205.1 2.8 %backward_chunk.7 = bf16[8,128,1280]{2,1,0:T(8,128)(2,1)} custom-call(bf16[128,512]{1,0:T(8,128)(2,1)} %get-tuple-element.46.kron_ref, bf16[8,32,1280]{2,1,0:T(8,128)(2,1)} %get-tuple-element.47.refs_0_, bf16[8,32,1280]{2,1,0:T(8,128)(2,1)} %collective-permute-done.9.refs_1_, ...), custom_call_target="tpu_custom_call", output_to_operand_aliasing={{}: (5, {})} | custom-call | flops 335544320 | bytes 3276800 | tf_op jit(solution)/shard_map/backward_chunk/pallas_call | solution.py:121
  207.9 1.6 fusion.10
  (91 shorter events, 11.9 us)
Async XLA Ops:
  0.6 6.2 %copy-start = (bf16[1280,1280]{1,0:T(8,128)(2,1)S(1)}, bf16[1280,1280]{1,0:T(8,128)(2,1)}, u32[]{:S(2)}) copy-start(bf16[1280,1280]{1,0:T(8,128)(2,1)} %param.9) | copy-start | bytes 9830404
  0.6 6.2 %copy-start.3 = (bf16[1,8,128,1280]{3,2,1,0:T(8,128)(2,1)S(1)}, bf16[1,8,128,1280]{3,2,1,0:T(8,128)(2,1)}, u32[]{:S(2)}) copy-start(bf16[1,8,128,1280]{3,2,1,0:T(8,128)(2,1)} %param.11) | copy-start | bytes 7864324
  0.7 25.5 %collective-permute-start = (bf16[8,128,1280]{2,1,0:T(8,128)(2,1)}, bf16[8,128,1280]{2,1,0:T(8,128)(2,1)}, u32[]{:S(2)}, u32[]{:S(2)}) collective-permute-start(bf16[8,128,1280]{2,1,0:T(8,128)(2,1)} %bitcast.62), channel_id=1, source_target_pairs={{0,1},{1,0},{2,3},{3,2},{4,5},{5,4},{6,7},{7,6},{8,9},{9,8},{10,11... | collective-permute-start | bytes 7864328 | tf_op jit(solution)/shard_map/ppermute | solution.py:15
  4.4 18.1 %collective-permute-start.4 = (bf16[8,32,1280]{2,1,0:T(8,128)(2,1)S(1)}, bf16[8,32,1280]{2,1,0:T(8,128)(2,1)}, u32[]{:S(2)}, u32[]{:S(2)}) collective-permute-start(bf16[8,32,1280]{2,1,0:T(8,128)(2,1)S(1)} %get-tuple-element.62), channel_id=1, source_target_pairs={{0,2},{1,3},{2,0},{3,1},{4,6},{5,7},{6,4},{7,5},{8,10},{9,11},{10,... | collective-permute-start | bytes 1966088 | tf_op jit(solution)/shard_map/ppermute | solution.py:15
  22.5 3.6 %collective-permute-start.5 = (bf16[8,32,1280]{2,1,0:T(8,128)(2,1)}, bf16[8,32,1280]{2,1,0:T(8,128)(2,1)}, u32[]{:S(2)}, u32[]{:S(2)}) collective-permute-start(bf16[8,32,1280]{2,1,0:T(8,128)(2,1)} %collective-permute-done.4.refs_2_), channel_id=1, source_target_pairs={{0,1},{1,0},{2,3},{3,2},{4,5},{5,4},{6,7},{7,6},{8,9},{9,8},{10,11... | collective-permute-start | bytes 1966088 | tf_op jit(solution)/shard_map/ppermute | solution.py:15
  22.6 17.4 %collective-permute-start.3 = (bf16[8,32,1280]{2,1,0:T(8,128)(2,1)}, bf16[8,32,1280]{2,1,0:T(8,128)(2,1)}, u32[]{:S(2)}, u32[]{:S(2)}) collective-permute-start(bf16[8,32,1280]{2,1,0:T(8,128)(2,1)} %get-tuple-element.63), channel_id=1, source_target_pairs={{0,2},{1,3},{2,0},{3,1},{4,6},{5,7},{6,4},{7,5},{8,10},{9,11},{10,... | collective-permute-start | bytes 1966088 | tf_op jit(solution)/shard_map/ppermute | solution.py:15
  40.0 2.4 %collective-permute-start.6 = (bf16[8,32,1280]{2,1,0:T(8,128)(2,1)}, bf16[8,32,1280]{2,1,0:T(8,128)(2,1)}, u32[]{:S(2)}, u32[]{:S(2)}) collective-permute-start(bf16[8,32,1280]{2,1,0:T(8,128)(2,1)} %collective-permute-done.3.refs_2_), channel_id=1, source_target_pairs={{0,1},{1,0},{2,3},{3,2},{4,5},{5,4},{6,7},{7,6},{8,9},{9,8},{10,11... | collective-permute-start | bytes 1966088 | tf_op jit(solution)/shard_map/ppermute | solution.py:15
  40.0 17.5 %collective-permute-start.2 = (bf16[8,32,1280]{2,1,0:T(8,128)(2,1)}, bf16[8,32,1280]{2,1,0:T(8,128)(2,1)}, u32[]{:S(2)}, u32[]{:S(2)}) collective-permute-start(bf16[8,32,1280]{2,1,0:T(8,128)(2,1)} %get-tuple-element.64), channel_id=1, source_target_pairs={{0,2},{1,3},{2,0},{3,1},{4,6},{5,7},{6,4},{7,5},{8,10},{9,11},{10,... | collective-permute-start | bytes 1966088 | tf_op jit(solution)/shard_map/ppermute | solution.py:15
  57.5 2.4 %collective-permute-start.7 = (bf16[8,32,1280]{2,1,0:T(8,128)(2,1)}, bf16[8,32,1280]{2,1,0:T(8,128)(2,1)}, u32[]{:S(2)}, u32[]{:S(2)}) collective-permute-start(bf16[8,32,1280]{2,1,0:T(8,128)(2,1)} %collective-permute-done.2.refs_2_), channel_id=1, source_target_pairs={{0,1},{1,0},{2,3},{3,2},{4,5},{5,4},{6,7},{7,6},{8,9},{9,8},{10,11... | collective-permute-start | bytes 1966088 | tf_op jit(solution)/shard_map/ppermute | solution.py:15
  57.5 17.5 %collective-permute-start.1 = (bf16[8,32,1280]{2,1,0:T(8,128)(2,1)}, bf16[8,32,1280]{2,1,0:T(8,128)(2,1)}, u32[]{:S(2)}, u32[]{:S(2)}) collective-permute-start(bf16[8,32,1280]{2,1,0:T(8,128)(2,1)} %get-tuple-element.65), channel_id=1, source_target_pairs={{0,2},{1,3},{2,0},{3,1},{4,6},{5,7},{6,4},{7,5},{8,10},{9,11},{10,... | collective-permute-start | bytes 1966088 | tf_op jit(solution)/shard_map/ppermute | solution.py:15
  74.9 2.4 %collective-permute-start.8 = (bf16[8,32,1280]{2,1,0:T(8,128)(2,1)}, bf16[8,32,1280]{2,1,0:T(8,128)(2,1)}, u32[]{:S(2)}, u32[]{:S(2)}) collective-permute-start(bf16[8,32,1280]{2,1,0:T(8,128)(2,1)} %collective-permute-done.1.refs_2_), channel_id=1, source_target_pairs={{0,1},{1,0},{2,3},{3,2},{4,5},{5,4},{6,7},{7,6},{8,9},{9,8},{10,11... | collective-permute-start | bytes 1966088 | tf_op jit(solution)/shard_map/ppermute | solution.py:15
  93.9 4.1 %copy-start.2 = (f32[2,2,2,2,2,40,1280]{6,5,4,3,2,1,0:T(8,128)}, f32[2,2,2,2,2,40,1280]{6,5,4,3,2,1,0:T(8,128)S(1)}, u32[]{:S(2)}) copy-start(f32[2,2,2,2,2,40,1280]{6,5,4,3,2,1,0:T(8,128)S(1)} %fusion.16) | copy-start | bytes 19660804
  93.9 4.2 %copy-start.4 = (bf16[1,8,128,1280]{3,2,1,0:T(8,128)(2,1)S(1)}, bf16[1,8,128,1280]{3,2,1,0:T(8,128)(2,1)}, u32[]{:S(2)}) copy-start(bf16[1,8,128,1280]{3,2,1,0:T(8,128)(2,1)} %param.11) | copy-start | bytes 7864324
  98.0 21.5 %collective-permute-start.21 = (f32[2,2,2,2,40,1280]{5,4,3,2,1,0:T(8,128)}, f32[2,2,2,2,40,1280]{5,4,3,2,1,0:T(8,128)}, u32[]{:S(2)}, u32[]{:S(2)}) collective-permute-start(f32[2,2,2,2,40,1280]{5,4,3,2,1,0:T(8,128)} %dynamic-slice_bitcast_fusion), channel_id=1, source_target_pairs={{0,1},{1,0},{2,3},{3,2},{4,5},{5,4},{6,7},{7,6},{8,9},{9,8},{10,11... | collective-permute-start | bytes 9830408 | tf_op jit(solution)/shard_map/ppermute | solution.py:15
  101.6 2.5 %collective-permute-start.29 = (f32[42,128]{1,0:T(8,128)}, f32[42,128]{1,0:T(8,128)S(1)}, u32[]{:S(2)}, u32[]{:S(2)}) collective-permute-start(f32[42,128]{1,0:T(8,128)} %pack_sums.1), channel_id=1, source_target_pairs={{0,1},{1,0},{2,3},{3,2},{4,5},{5,4},{6,7},{7,6},{8,9},{9,8},{10,11... | collective-permute-start | bytes 64520 | tf_op jit(solution)/shard_map/ppermute | solution.py:15
  104.8 3.8 %collective-permute-start.30 = (f32[42,128]{1,0:T(8,128)S(1)}, f32[42,128]{1,0:T(8,128)S(1)}, u32[]{:S(2)}, u32[]{:S(2)}) collective-permute-start(f32[42,128]{1,0:T(8,128)S(1)} %add.115), channel_id=1, source_target_pairs={{0,4},{4,0},{8,12},{12,8},{16,20},{20,16},{24,28},{28,24},{1,5},{5... | collective-permute-start | bytes 64520 | tf_op jit(solution)/shard_map/ppermute | solution.py:15
  108.7 3.8 %collective-permute-start.31 = (f32[42,128]{1,0:T(8,128)S(1)}, f32[42,128]{1,0:T(8,128)S(1)}, u32[]{:S(2)}, u32[]{:S(2)}) collective-permute-start(f32[42,128]{1,0:T(8,128)S(1)} %add.116), channel_id=1, source_target_pairs={{0,8},{4,12},{8,0},{12,4},{16,24},{20,28},{24,16},{28,20},{1,9},{5... | collective-permute-start | bytes 64520 | tf_op jit(solution)/shard_map/ppermute | solution.py:15
  112.5 6.4 %collective-permute-start.32 = (f32[42,128]{1,0:T(8,128)S(1)}, f32[42,128]{1,0:T(8,128)S(1)}, u32[]{:S(2)}, u32[]{:S(2)}) collective-permute-start(f32[42,128]{1,0:T(8,128)S(1)} %add.117), channel_id=1, source_target_pairs={{0,16},{4,20},{8,24},{12,28},{16,0},{20,4},{24,8},{28,12},{1,17},{... | collective-permute-start | bytes 64520 | tf_op jit(solution)/shard_map/ppermute | solution.py:15
  115.3 17.9 %collective-permute-start.19 = (bf16[8,32,1280]{2,1,0:T(8,128)(2,1)}, bf16[8,32,1280]{2,1,0:T(8,128)(2,1)S(1)}, u32[]{:S(2)}, u32[]{:S(2)}) collective-permute-start(bf16[8,32,1280]{2,1,0:T(8,128)(2,1)} %get-tuple-element.53.refs_0_), channel_id=1, source_target_pairs={{0,2},{1,3},{2,0},{3,1},{4,6},{5,7},{6,4},{7,5},{8,10},{9,11},{10,... | collective-permute-start | bytes 1966088 | tf_op jit(solution)/shard_map/ppermute | solution.py:15
  116.8 30.4 %collective-permute-start.16 = (bf16[8,32,1280]{2,1,0:T(8,128)(2,1)}, bf16[8,32,1280]{2,1,0:T(8,128)(2,1)S(1)}, u32[]{:S(2)}, u32[]{:S(2)}) collective-permute-start(bf16[8,32,1280]{2,1,0:T(8,128)(2,1)} %get-tuple-element.51.refs_0_), channel_id=1, source_target_pairs={{0,2},{1,3},{2,0},{3,1},{4,6},{5,7},{6,4},{7,5},{8,10},{9,11},{10,... | collective-permute-start | bytes 1966088 | tf_op jit(solution)/shard_map/ppermute | solution.py:15
  117.4 41.5 %collective-permute-start.13 = (bf16[8,32,1280]{2,1,0:T(8,128)(2,1)}, bf16[8,32,1280]{2,1,0:T(8,128)(2,1)}, u32[]{:S(2)}, u32[]{:S(2)}) collective-permute-start(bf16[8,32,1280]{2,1,0:T(8,128)(2,1)} %get-tuple-element.49.refs_0_), channel_id=1, source_target_pairs={{0,2},{1,3},{2,0},{3,1},{4,6},{5,7},{6,4},{7,5},{8,10},{9,11},{10,... | collective-permute-start | bytes 1966088 | tf_op jit(solution)/shard_map/ppermute | solution.py:15
  118.9 41.5 %collective-permute-start.33 = (f32[42,128]{1,0:T(8,128)S(1)}, f32[42,128]{1,0:T(8,128)S(1)}, u32[]{:S(2)}, u32[]{:S(2)}) collective-permute-start(f32[42,128]{1,0:T(8,128)S(1)} %add.118), channel_id=1, source_target_pairs={{0,2},{1,3},{2,0},{3,1},{4,6},{5,7},{6,4},{7,5},{8,10},{9,11},{10,... | collective-permute-start | bytes 64520 | tf_op jit(solution)/shard_map/ppermute | solution.py:15
  122.8 2.0 copy-start.1
  122.8 2.0 copy-start.14
  123.2 40.1 %collective-permute-start.22 = (bf16[2,2,2,40,640]{4,3,2,0,1:T(8,128)(2,1)S(1)}, bf16[2,2,2,40,640]{4,3,2,0,1:T(8,128)(2,1)S(1)}, u32[]{:S(2)}, u32[]{:S(2)}) collective-permute-start(bf16[2,2,2,40,640]{4,3,2,0,1:T(8,128)(2,1)S(1)} %fusion.2), channel_id=1, source_target_pairs={{0,4},{4,0},{8,12},{12,8},{16,20},{20,16},{24,28},{28,24},{1,5},{5... | collective-permute-start | bytes 1228808 | tf_op jit(solution)/shard_map/ppermute | solution.py:15
  124.8 8.5 %copy-start.6 = (bf16[8,32,1280]{2,1,0:T(8,128)(2,1)S(1)}, bf16[8,32,1280]{2,1,0:T(8,128)(2,1)}, u32[]{:S(2)}) copy-start(bf16[8,32,1280]{2,1,0:T(8,128)(2,1)} %get-tuple-element.53.refs_0_) | copy-start | bytes 1966084
  124.8 22.5 %copy-start.7 = (bf16[8,32,1280]{2,1,0:T(8,128)(2,1)S(1)}, bf16[8,32,1280]{2,1,0:T(8,128)(2,1)}, u32[]{:S(2)}) copy-start(bf16[8,32,1280]{2,1,0:T(8,128)(2,1)} %get-tuple-element.51.refs_0_) | copy-start | bytes 1966084
  133.2 60.3 %copy-start.8 = (bf16[8,32,1280]{2,1,0:T(8,128)(2,1)}, bf16[8,32,1280]{2,1,0:T(8,128)(2,1)S(1)}, u32[]{:S(2)}) copy-start(bf16[8,32,1280]{2,1,0:T(8,128)(2,1)S(1)} %collective-permute-done.19.refs_2_) | copy-start | bytes 1966084
  133.2 57.1 %collective-permute-start.18 = (bf16[8,32,1280]{2,1,0:T(8,128)(2,1)S(1)}, bf16[8,32,1280]{2,1,0:T(8,128)(2,1)S(1)}, u32[]{:S(2)}, u32[]{:S(2)}) collective-permute-start(bf16[8,32,1280]{2,1,0:T(8,128)(2,1)S(1)} %copy-done.6), channel_id=1, source_target_pairs={{0,1},{1,0},{2,3},{3,2},{4,5},{5,4},{6,7},{7,6},{8,9},{9,8},{10,11... | collective-permute-start | bytes 1966088 | tf_op jit(solution)/shard_map/ppermute | solution.py:15
  147.3 25.0 %copy-start.9 = (bf16[8,32,1280]{2,1,0:T(8,128)(2,1)}, bf16[8,32,1280]{2,1,0:T(8,128)(2,1)S(1)}, u32[]{:S(2)}) copy-start(bf16[8,32,1280]{2,1,0:T(8,128)(2,1)S(1)} %collective-permute-done.16.refs_2_) | copy-start | bytes 1966084
  147.3 43.1 %collective-permute-start.15 = (bf16[8,32,1280]{2,1,0:T(8,128)(2,1)S(1)}, bf16[8,32,1280]{2,1,0:T(8,128)(2,1)S(1)}, u32[]{:S(2)}, u32[]{:S(2)}) collective-permute-start(bf16[8,32,1280]{2,1,0:T(8,128)(2,1)S(1)} %copy-done.7), channel_id=1, source_target_pairs={{0,1},{1,0},{2,3},{3,2},{4,5},{5,4},{6,7},{7,6},{8,9},{9,8},{10,11... | collective-permute-start | bytes 1966088 | tf_op jit(solution)/shard_map/ppermute | solution.py:15
  158.9 29.2 %collective-permute-start.10 = (bf16[8,32,1280]{2,1,0:T(8,128)(2,1)}, bf16[8,32,1280]{2,1,0:T(8,128)(2,1)}, u32[]{:S(2)}, u32[]{:S(2)}) collective-permute-start(bf16[8,32,1280]{2,1,0:T(8,128)(2,1)} %get-tuple-element.47.refs_0_), channel_id=1, source_target_pairs={{0,2},{1,3},{2,0},{3,1},{4,6},{5,7},{6,4},{7,5},{8,10},{9,11},{10,... | collective-permute-start | bytes 1966088 | tf_op jit(solution)/shard_map/ppermute | solution.py:15
  160.4 9.8 %collective-permute-start.25 = (bf16[2,2,2,40,640]{4,3,2,1,0:T(8,128)(2,1)S(1)}, bf16[2,2,2,40,640]{4,3,2,1,0:T(8,128)(2,1)S(1)}, u32[]{:S(2)}, u32[]{:S(2)}) collective-permute-start(bf16[2,2,2,40,640]{4,3,2,1,0:T(8,128)(2,1)S(1)} %fusion.1), channel_id=1, source_target_pairs={{0,8},{4,12},{8,0},{12,4},{16,24},{20,28},{24,16},{28,20},{1,9},{5... | collective-permute-start | bytes 1228808 | tf_op jit(solution)/shard_map/ppermute | solution.py:15
  163.3 27.6 %collective-permute-start.17 = (bf16[8,32,1280]{2,1,0:T(8,128)(2,1)S(1)}, bf16[8,32,1280]{2,1,0:T(8,128)(2,1)S(1)}, u32[]{:S(2)}, u32[]{:S(2)}) collective-permute-start(bf16[8,32,1280]{2,1,0:T(8,128)(2,1)S(1)} %collective-permute-done.16.refs_2_), channel_id=1, source_target_pairs={{0,1},{1,0},{2,3},{3,2},{4,5},{5,4},{6,7},{7,6},{8,9},{9,8},{10,11... | collective-permute-start | bytes 1966088 | tf_op jit(solution)/shard_map/ppermute | solution.py:15
  170.3 7.3 %collective-permute-start.23 = (bf16[2,2,40,640]{3,2,1,0:T(8,128)(2,1)S(1)}, bf16[2,2,40,640]{3,2,1,0:T(8,128)(2,1)S(1)}, u32[]{:S(2)}, u32[]{:S(2)}) collective-permute-start(bf16[2,2,40,640]{3,2,1,0:T(8,128)(2,1)S(1)} %fusion.3), channel_id=1, source_target_pairs={{0,8},{4,12},{8,0},{12,4},{16,24},{20,28},{24,16},{28,20},{1,9},{5... | collective-permute-start | bytes 614408 | tf_op jit(solution)/shard_map/ppermute | solution.py:15
  177.5 10.4 %collective-permute-start.26 = (bf16[2,2,40,640]{3,2,1,0:T(8,128)(2,1)S(1)}, bf16[2,2,40,640]{3,2,1,0:T(8,128)(2,1)S(1)}, u32[]{:S(2)}, u32[]{:S(2)}) collective-permute-start(bf16[2,2,40,640]{3,2,1,0:T(8,128)(2,1)S(1)} %fusion.4), channel_id=1, source_target_pairs={{0,16},{4,20},{8,24},{12,28},{16,0},{20,4},{24,8},{28,12},{1,17},{... | collective-permute-start | bytes 614408 | tf_op jit(solution)/shard_map/ppermute | solution.py:15
  188.0 5.6 %collective-permute-start.24 = (bf16[2,40,640]{2,1,0:T(8,128)(2,1)S(1)}, bf16[2,40,640]{2,1,0:T(8,128)(2,1)S(1)}, u32[]{:S(2)}, u32[]{:S(2)}) collective-permute-start(bf16[2,40,640]{2,1,0:T(8,128)(2,1)S(1)} %fusion.11), channel_id=1, source_target_pairs={{0,16},{4,20},{8,24},{12,28},{16,0},{20,4},{24,8},{28,12},{1,17},{... | collective-permute-start | bytes 307208 | tf_op jit(solution)/shard_map/ppermute | solution.py:15
  188.1 5.5 %collective-permute-start.27 = (bf16[2,40,640]{2,1,0:T(8,128)(2,1)S(1)}, bf16[2,40,640]{2,1,0:T(8,128)(2,1)S(1)}, u32[]{:S(2)}, u32[]{:S(2)}) collective-permute-start(bf16[2,40,640]{2,1,0:T(8,128)(2,1)S(1)} %fusion.12), channel_id=1, source_target_pairs={{0,4},{4,0},{8,12},{12,8},{16,20},{20,16},{24,28},{28,24},{1,5},{5... | collective-permute-start | bytes 307208 | tf_op jit(solution)/shard_map/ppermute | solution.py:15
  190.3 5.5 %copy-start.10 = (bf16[8,32,1280]{2,1,0:T(8,128)(2,1)}, bf16[8,32,1280]{2,1,0:T(8,128)(2,1)S(1)}, u32[]{:S(2)}) copy-start(bf16[8,32,1280]{2,1,0:T(8,128)(2,1)S(1)} %collective-permute-done.18.refs_1_) | copy-start | bytes 1966084
  190.3 11.9 %collective-permute-start.12 = (bf16[8,32,1280]{2,1,0:T(8,128)(2,1)}, bf16[8,32,1280]{2,1,0:T(8,128)(2,1)}, u32[]{:S(2)}, u32[]{:S(2)}) collective-permute-start(bf16[8,32,1280]{2,1,0:T(8,128)(2,1)} %get-tuple-element.49.refs_0_), channel_id=1, source_target_pairs={{0,1},{1,0},{2,3},{3,2},{4,5},{5,4},{6,7},{7,6},{8,9},{9,8},{10,11... | collective-permute-start | bytes 1966088 | tf_op jit(solution)/shard_map/ppermute | solution.py:15
  190.3 6.0 %copy-start.11 = (bf16[8,32,1280]{2,1,0:T(8,128)(2,1)}, bf16[8,32,1280]{2,1,0:T(8,128)(2,1)S(1)}, u32[]{:S(2)}) copy-start(bf16[8,32,1280]{2,1,0:T(8,128)(2,1)S(1)} %collective-permute-done.15.refs_1_) | copy-start | bytes 1966084
  190.4 14.8 %collective-permute-start.9 = (bf16[8,32,1280]{2,1,0:T(8,128)(2,1)}, bf16[8,32,1280]{2,1,0:T(8,128)(2,1)}, u32[]{:S(2)}, u32[]{:S(2)}) collective-permute-start(bf16[8,32,1280]{2,1,0:T(8,128)(2,1)} %get-tuple-element.47.refs_0_), channel_id=1, source_target_pairs={{0,1},{1,0},{2,3},{3,2},{4,5},{5,4},{6,7},{7,6},{8,9},{9,8},{10,11... | collective-permute-start | bytes 1966088 | tf_op jit(solution)/shard_map/ppermute | solution.py:15
  190.9 5.5 %copy-start.12 = (bf16[8,32,1280]{2,1,0:T(8,128)(2,1)}, bf16[8,32,1280]{2,1,0:T(8,128)(2,1)S(1)}, u32[]{:S(2)}) copy-start(bf16[8,32,1280]{2,1,0:T(8,128)(2,1)S(1)} %collective-permute-done.17.refs_3_) | copy-start | bytes 1966084
  190.9 11.4 %collective-permute-start.14 = (bf16[8,32,1280]{2,1,0:T(8,128)(2,1)}, bf16[8,32,1280]{2,1,0:T(8,128)(2,1)}, u32[]{:S(2)}, u32[]{:S(2)}) collective-permute-start(bf16[8,32,1280]{2,1,0:T(8,128)(2,1)} %collective-permute-done.13.refs_2_), channel_id=1, source_target_pairs={{0,1},{1,0},{2,3},{3,2},{4,5},{5,4},{6,7},{7,6},{8,9},{9,8},{10,11... | collective-permute-start | bytes 1966088 | tf_op jit(solution)/shard_map/ppermute | solution.py:15
  193.5 2.3 %collective-permute-start.20 = (bf16[8,32,1280]{2,1,0:T(8,128)(2,1)S(1)}, bf16[8,32,1280]{2,1,0:T(8,128)(2,1)S(1)}, u32[]{:S(2)}, u32[]{:S(2)}) collective-permute-start(bf16[8,32,1280]{2,1,0:T(8,128)(2,1)S(1)} %collective-permute-done.19.refs_2_), channel_id=1, source_target_pairs={{0,1},{1,0},{2,3},{3,2},{4,5},{5,4},{6,7},{7,6},{8,9},{9,8},{10,11... | collective-permute-start | bytes 1966088 | tf_op jit(solution)/shard_map/ppermute | solution.py:15
  193.5 11.6 %collective-permute-start.11 = (bf16[8,32,1280]{2,1,0:T(8,128)(2,1)}, bf16[8,32,1280]{2,1,0:T(8,128)(2,1)}, u32[]{:S(2)}, u32[]{:S(2)}) collective-permute-start(bf16[8,32,1280]{2,1,0:T(8,128)(2,1)} %collective-permute-done.10.refs_2_), channel_id=1, source_target_pairs={{0,1},{1,0},{2,3},{3,2},{4,5},{5,4},{6,7},{7,6},{8,9},{9,8},{10,11... | collective-permute-start | bytes 1966088 | tf_op jit(solution)/shard_map/ppermute | solution.py:15
  195.8 0.8 copy-start.13
  195.8 12.1 %collective-permute-start.28 = (bf16[40,1280]{1,0:T(8,128)(2,1)}, bf16[40,1280]{1,0:T(8,128)(2,1)}, u32[]{:S(2)}, u32[]{:S(2)}) collective-permute-start(bf16[40,1280]{1,0:T(8,128)(2,1)} %fusion.13), channel_id=1, source_target_pairs={{0,2},{1,3},{2,0},{3,1},{4,6},{5,7},{6,4},{7,5},{8,10},{9,11},{10,... | collective-permute-start | bytes 307208 | tf_op jit(solution)/shard_map/ppermute | solution.py:15
  (1 other events, 0.7 us)

commit v2 on v0

v2 whole, which is shorter than its diff:
```python
import functools

import jax
import jax.numpy as jnp
from jax import lax
from jax.experimental import pallas as pl
from jax.experimental.pallas import tpu as pltpu
from jax.sharding import PartitionSpec as P

GROUP = 16
SMALL = pl.CostEstimate(flops=1000, bytes_accessed=1000, transcendentals=0)
SMEM = pl.BlockSpec(memory_space=pltpu.SMEM)
VMEM = pl.BlockSpec(memory_space=pltpu.VMEM)


def xor_permute(value, axis, size, mask):
    return lax.ppermute(value, axis, [(i, i ^ mask) for i in range(size)])


def after(value, *earlier):
    return lax.optimization_barrier((value, *earlier))[0]


def iota2(shape, dim):
    return lax.broadcasted_iota(jnp.int32, shape, dim)


def selector(me, parts, steps):
    rows, total = parts * steps * GROUP, parts * steps
    depth, shift = (steps * GROUP).bit_length() - 1, GROUP.bit_length() - 1
    at = iota2((rows, total), 0)
    source = jnp.bitwise_xor(me, lax.shift_right_logical(at, depth))
    step = jnp.bitwise_and(lax.shift_right_logical(at, shift), steps - 1)
    return source * steps + step == iota2((rows, total), 1)


def same_token(rows):
    low = lambda dim: jnp.bitwise_and(iota2((rows, rows), dim), GROUP - 1)
    return low(0) == low(1)


def kron_kernel(parts, steps, me_ref, mixing_ref, thr_ref, fwd_ref, bwd_ref, rows_ref):
    pick = selector(me_ref[0], parts, steps)
    one = jnp.where(pick, 1.0, 0.0).astype(jnp.bfloat16)
    mixing = mixing_ref[...].astype(jnp.bfloat16)
    same = same_token(pick.shape[0])
    dot = functools.partial(lax.dot_general, preferred_element_type=jnp.float32)
    for ref, dim in ((fwd_ref, 0), (bwd_ref, 1)):
        first = dot(one, mixing, (((1,), (dim,)), ((), ()))).astype(jnp.bfloat16)
        wide = dot(first, one, (((1,), (1,)), ((), ())))
        ref[...] = jnp.where(same, wide, 0.0).astype(jnp.bfloat16)
    thr = jnp.broadcast_to(thr_ref[...], pick.shape)
    rows_ref[...] = jnp.sum(jnp.where(pick, thr, 0.0), axis=1, keepdims=True)


def build_krons(info, mixing, threshold, parts, steps):
    rows = parts * steps * GROUP
    vmem = pl.BlockSpec(memory_space=pltpu.VMEM)
    wide = jax.ShapeDtypeStruct((rows, rows), jnp.bfloat16)
    return pl.pallas_call(
        functools.partial(kron_kernel, parts, steps),
        in_specs=[pl.BlockSpec(memory_space=pltpu.SMEM), vmem, vmem],
        out_specs=(vmem, vmem, vmem),
        out_shape=(wide, wide, jax.ShapeDtypeStruct((rows, 1), jnp.float32)),
        name="build_krons",
    )(info, mixing, threshold.reshape(1, -1))


def rows_of(refs, at, tile):
    return jnp.concatenate([r[:, :, at : at + tile].reshape(-1, tile) for r in refs], axis=0)


def forward_kernel(parts, kron_ref, thr_ref, *refs):
    sources, spikes, surrogate_ref = refs[:parts], refs[parts : 2 * parts], refs[-1]
    steps, group, width = sources[0].shape
    rows = steps * group
    kron = kron_ref[...]
    thr = thr_ref[...]
    tile = 256
    for at in range(0, width, tile):
        cur = rows_of(sources, at, tile)
        shifted = jnp.dot(kron, cur, preferred_element_type=jnp.float32) - thr
        fired = jnp.where(shifted > 0, 1.0, 0.0).astype(jnp.bfloat16)
        for k in range(parts):
            spikes[k][:, :, at : at + tile] = fired[k * rows : (k + 1) * rows].reshape(
                steps, group, tile
            )
        small = jnp.exp(-jnp.abs(shifted))
        part = 1.0 / (1.0 + small)
        surrogate_ref[0, :, at : at + tile] = small * part * part


def forward(kron, thr, sources):
    parts = len(sources)
    steps, tokens, width = sources[0].shape
    piece = pl.BlockSpec((steps, GROUP, width), lambda g: (0, g, 0))
    fixed = lambda shape: pl.BlockSpec(shape, lambda g: (0, 0))
    rows = parts * steps * GROUP
    found = pl.pallas_call(
        functools.partial(forward_kernel, parts),
        grid=(tokens // GROUP,),
        in_specs=[fixed(kron.shape), fixed(thr.shape)] + [piece] * parts,
        out_specs=[piece] * parts + [pl.BlockSpec((1, rows, width), lambda g: (g, 0, 0))],
        out_shape=[jax.ShapeDtypeStruct((steps, tokens, width), jnp.bfloat16)] * parts
        + [jax.ShapeDtypeStruct((tokens // GROUP, rows, width), jnp.float32)],
        name="forward",
    )(kron, thr, *sources)
    return found[:parts], found[parts]


def parts_of(mg):
    high = mg.astype(jnp.bfloat16)
    return high, (mg - high.astype(jnp.float32)).astype(jnp.bfloat16)


def backward_kernel(parts, kron_ref, surrogate_ref, *refs):
    grads, outs = refs[:parts], refs[parts:]
    steps, group, width = grads[0].shape
    rows = steps * group
    kron = kron_ref[...]
    tile = 256
    for at in range(0, width, tile):
        mg = rows_of(grads, at, tile).astype(jnp.float32) * surrogate_ref[0, :, at : at + tile]
        grad = jnp.dot(kron, mg.astype(jnp.bfloat16), preferred_element_type=jnp.float32)
        grad = grad.astype(jnp.bfloat16)
        for k in range(parts):
            outs[k][:, :, at : at + tile] = grad[k * rows : (k + 1) * rows].reshape(
                steps, group, tile
            )


def backward(kron, surrogate, grads):
    parts = len(grads)
    steps, tokens, width = grads[0].shape
    rows = parts * steps * GROUP
    piece = pl.BlockSpec((steps, GROUP, width), lambda g: (0, g, 0))
    return pl.pallas_call(
        functools.partial(backward_kernel, parts),
        grid=(tokens // GROUP,),
        in_specs=[
            pl.BlockSpec(kron.shape, lambda g: (0, 0)),
            pl.BlockSpec((1, rows, width), lambda g: (g, 0, 0)),
        ]
        + [piece] * parts,
        out_specs=[piece] * parts,
        out_shape=[jax.ShapeDtypeStruct((steps, tokens, width), jnp.bfloat16)] * parts,
        cost_estimate=pl.CostEstimate(
            flops=8 * rows * rows * width * (tokens // GROUP),
            bytes_accessed=8 * rows * width * (tokens // GROUP),
            transcendentals=0,
        ),
        name="backward",
    )(kron, surrogate, *grads)


def cross_kernel(parts, surrogate_ref, *refs):
    sources, grads, (cross_ref, tsum_ref, both_ref) = (
        refs[:parts],
        refs[parts : 2 * parts],
        refs[2 * parts :],
    )
    steps, group, width = sources[0].shape
    every = parts * steps * group

    @pl.when(pl.program_id(0) == 0)
    def _():
        cross_ref[...] = jnp.zeros_like(cross_ref)
        tsum_ref[...] = jnp.zeros_like(tsum_ref)

    tile = 256
    total = jnp.zeros((every, 128), jnp.float32)
    for at in range(0, width, tile):
        mg = rows_of(grads, at, tile).astype(jnp.float32) * surrogate_ref[0, :, at : at + tile]
        for piece in range(0, tile, 128):
            total = total + mg[:, piece : piece + 128]
        both_ref[:every, at : at + tile], both_ref[every:, at : at + tile] = parts_of(mg)
    tsum_ref[...] += total
    cross = lax.dot_general(
        both_ref[...],
        rows_of(sources, 0, width),
        (((1,), (1,)), ((), ())),
        preferred_element_type=jnp.float32,
    )
    cross_ref[...] += cross[:every] + cross[every:]


def cross_sums(surrogate, sources, grads):
    parts = len(sources)
    steps, tokens, width = sources[0].shape
    rows = parts * steps * GROUP
    piece = pl.BlockSpec((steps, GROUP, width), lambda g: (0, g, 0))
    fixed = lambda shape: pl.BlockSpec(shape, lambda g: (0, 0))
    return pl.pallas_call(
        functools.partial(cross_kernel, parts),
        grid=(tokens // GROUP,),
        in_specs=[pl.BlockSpec((1, rows, width), lambda g: (g, 0, 0))] + [piece] * (2 * parts),
        out_specs=[fixed((rows, rows)), fixed((rows, 128))],
        out_shape=[
            jax.ShapeDtypeStruct((rows, rows), jnp.float32),
            jax.ShapeDtypeStruct((rows, 128), jnp.float32),
        ],
        scratch_shapes=[pltpu.VMEM((2 * rows, width), jnp.bfloat16)],
        cost_estimate=pl.CostEstimate(
            flops=8 * rows * rows * width * (tokens // GROUP),
            bytes_accessed=8 * rows * width * (tokens // GROUP),
            transcendentals=0,
        ),
        name="cross_sums",
    )(surrogate, *sources, *grads)


def sums_kernel(parts, steps, me_ref, bias_ref, cross_ref, tsum_ref, out_ref):
    pick = selector(me_ref[0], parts, steps)
    rows, total = pick.shape
    one = jnp.where(pick, 1.0, 0.0)
    exact = functools.partial(
        lax.dot_general, precision=lax.Precision.HIGHEST, preferred_element_type=jnp.float32
    )
    turned = (((0,), (0,)), ((), ()))
    cross = jnp.where(same_token(rows), cross_ref[...], 0.0)
    narrow = exact(cross, one, (((1,), (0,)), ((), ())))
    row_sum = -jnp.sum(tsum_ref[...], axis=1, keepdims=True)
    out_ref[...] = jnp.zeros_like(out_ref)
    out_ref[:total, :total] = exact(one, narrow, turned)
    out_ref[total : total + 8, :total] = jnp.broadcast_to(
        jnp.sum(one * row_sum, axis=0, keepdims=True), (8, total)
    )
    out_ref[total + 8 : total + 8 + bias_ref.shape[0], :] = bias_ref[...]


def pack_sums(info, bias_rows, cross, tsum, parts, steps):
    rows = parts * steps + 8 + -(-bias_rows.shape[0] // 8) * 8
    return pl.pallas_call(
        functools.partial(sums_kernel, parts, steps),
        in_specs=[SMEM, VMEM, VMEM, VMEM],
        out_specs=VMEM,
        out_shape=jax.ShapeDtypeStruct((rows, 128), jnp.float32),
        cost_estimate=SMALL,
        name="pack_sums",
    )(info, bias_rows, cross, tsum)


def place_kernel(slots, info_ref, *refs):
    pieces, (whole_ref, held_ref, in_sems, out_sems) = refs[: len(slots)], refs[-4:]
    share = held_ref.shape[2]
    loads, stores = [], []
    for n, slot in enumerate(slots):
        at = pl.multiple_of(info_ref[slot] * share, share)
        loads.append(pltpu.make_async_copy(pieces[n], held_ref.at[n], in_sems.at[n]))
        stores.append(
            pltpu.make_async_copy(
                held_ref.at[n], whole_ref.at[:, pl.ds(at, share), :], out_sems.at[n]
            )
        )
    for load in loads:
        load.start()
    for load, store in zip(loads, stores):
        load.wait()
        store.start()
    for store in stores:
        store.wait()


def place(info, pieces, slots, whole, tokens):
    steps, share, width = pieces[0].shape
    args, aliases, count = list(pieces), {}, len(pieces)
    if whole is not None:
        aliases = {1 + count: 0}
        args.append(whole)
    hbm = pl.BlockSpec(memory_space=pl.ANY)
    return pl.pallas_call(
        functools.partial(place_kernel, tuple(slots)),
        in_specs=[SMEM] + [hbm] * len(args),
        out_specs=hbm,
        out_shape=jax.ShapeDtypeStruct((steps, tokens, width), jnp.bfloat16),
        scratch_shapes=[
            pltpu.VMEM((count, steps, share, width), jnp.bfloat16),
            pltpu.SemaphoreType.DMA((count,)),
            pltpu.SemaphoreType.DMA((count,)),
        ],
        input_output_aliases=aliases,
        cost_estimate=SMALL,
        name="place",
    )(info, *args)


def combine_kernel(shapes, counts, extra, joined, info_ref, *refs):
    halves = len(shapes)
    keeps, refs = refs[:halves], refs[halves:]
    gots = []
    for count in counts:
        gots.append(refs[:count])
        refs = refs[count:]
    adds, outs = refs[:extra], refs[extra:]
    for h, (before, behind, slot) in enumerate(shapes):
        keep_ref = keeps[h]
        stay_ref, send_ref = (outs[0], outs[1]) if joined else (outs[2 * h], outs[2 * h + 1])
        beta = info_ref[slot]
        each = keep_ref.shape[0] // counts[h]
        cols = slice(h * keep_ref.shape[2], (h + 1) * keep_ref.shape[2]) if joined else slice(None)

        def value(p, b, q):
            at = (p * 2 + b) * behind + q
            if counts[h] == 1:
                got = gots[h][0][at]
            else:
                part = (p * 2 * behind) // each
                got = gots[h][part][at - part * each]
            return keep_ref[at] + got.astype(jnp.float32)

        for p in range(before):
            for q in range(behind):
                stay_ref[p * behind + q, :, cols] = value(p, beta, q)
                send_ref[p * behind + q, :, cols] = value(p, 1 - beta, q).astype(send_ref.dtype)
    if extra:
        total = adds[0][...]
        for ref in adds[1:]:
            total = total + ref[...]
        outs[-1][...] = total


def combine(info, shapes, halves, adds=(), joined=False):
    out = []
    for (keep, _), (before, behind, _) in zip(halves[:1] if joined else halves, shapes):
        cols = keep.shape[2] * (len(halves) if joined else 1)
        shape = (before * behind, keep.shape[1], cols)
        out += [
            jax.ShapeDtypeStruct(shape, jnp.float32),
            jax.ShapeDtypeStruct(shape, jnp.bfloat16),
        ]
    if adds:
        out.append(jax.ShapeDtypeStruct(adds[0].shape, jnp.float32))
    args = [k for k, _ in halves] + [g for _, got in halves for g in got] + list(adds)
    counts = tuple(len(got) for _, got in halves)
    found = pl.pallas_call(
        functools.partial(combine_kernel, tuple(shapes), counts, len(adds), joined),
        in_specs=[SMEM] + [VMEM] * len(args),
        out_specs=[VMEM] * len(out),
        out_shape=out,
        cost_estimate=SMALL,
        name="combine",
    )(info, *args)
    pairs = [(found[n], found[n + 1]) for n in range(0, len(out) - len(out) % 2, 2)]
    return pairs, found[-1]


def final_kernel(total, biases, keep_ref, got_ref, *refs):
    sums_refs, (out_ref, mix_ref, thr_ref, bias_ref) = refs[:-4], refs[-4:]
    out_ref[...] = (keep_ref[...] + got_ref[...].astype(jnp.float32)).astype(jnp.bfloat16)
    sums = sums_refs[0][...]
    for ref in sums_refs[1:]:
        sums = sums + ref[...]
    mix_ref[...] = sums[:total, :total]
    thr_ref[...] = sums[total : total + 1, :total]
    bias_ref[...] = jnp.concatenate(
        [sums[total + 8 + i : total + 9 + i] for i in range(biases)], axis=1
    )


def final(keep, got, sums, total, width):
    shape = jax.ShapeDtypeStruct
    return pl.pallas_call(
        functools.partial(final_kernel, total, width // 128),
        in_specs=[VMEM] * (2 + len(sums)),
        out_specs=[VMEM] * 4,
        out_shape=[
            shape(keep.shape, jnp.bfloat16),
            shape((total, total), jnp.float32),
            shape((1, total), jnp.float32),
            shape((1, width), jnp.float32),
        ],
        cost_estimate=SMALL,
        name="final",
    )(keep, got, *sums)


def weight_kernel(shard, parts, me_ref, spikes_ref, *refs):
    cots, keep_ref, sends = refs[:parts], refs[parts], refs[parts + 1 :]
    part = jnp.dot(
        spikes_ref[...], rows_of(cots, 0, cots[0].shape[-1]), preferred_element_type=jnp.float32
    )
    core = jnp.bitwise_and(me_ref[0], 1)
    pieces = [part[at : at + shard] for at in range(0, part.shape[0], shard)]
    for mine in range(2):

        @pl.when(core == mine)
        def _():
            for k, piece in enumerate(pieces):
                if k % 2 == mine:
                    keep_ref[k // 2] = piece

    for step, send_ref in enumerate(sends):
        for mine in range(2):

            @pl.when((core == mine) & (pl.program_id(0) == step))
            def _():
                for k, piece in enumerate(pieces):
                    if k % 2 != mine:
                        send_ref[k // 2] = piece.astype(send_ref.dtype)


def weight_half(info, turned, cots, part, shard):
    steps, tokens, width = cots[0].shape
    block, cols = width // 2, width // 2
    count = block // shard // 2
    send = jax.ShapeDtypeStruct((count, shard, cols), jnp.bfloat16)
    found = pl.pallas_call(
        functools.partial(weight_kernel, shard, len(cots)),
        grid=(2,),
        in_specs=[SMEM]
        + [pl.BlockSpec((block, turned.shape[1]), lambda i: (i, 0))]
        + [pl.BlockSpec((steps, tokens, cols), lambda i: (0, 0, part))] * len(cots),
        out_specs=[pl.BlockSpec((count, shard, cols), lambda i: (i, 0, 0))]
        + [pl.BlockSpec((count, shard, cols), lambda i: (0, 0, 0))] * 2,
        out_shape=[jax.ShapeDtypeStruct((2 * count, shard, cols), jnp.float32), send, send],
        cost_estimate=SMALL,
        name="weight_half",
    )(info, turned, *cots)
    return found[0], found[1:]


def body(ndp, ntm, currents, mixing, threshold, weight, bias, cotangent):
    _, steps, tokens, width = currents.shape
    me = lax.axis_index("tm")
    bits = lambda n: n.bit_length() - 1
    share = tokens // ntm
    bdp, btm = bits(ndp), bits(ntm)
    names = [("dp", b) for b in range(bdp - 1, -1, -1)] + [("tm", b) for b in range(btm - 1, -1, -1)]
    sizes = {"dp": ndp, "tm": ntm}
    info = jnp.stack(
        [me]
        + [(lax.axis_index(axis) >> b) & 1 for axis, b in names]
        + [me ^ k for k in range(ntm)]
    )
    slot = lambda bit: 1 + names.index(bit)
    spot = lambda k: 1 + len(names) + k

    def exchange(pieces):
        return [pieces[0]] + [xor_permute(pieces[k], "tm", ntm, k) for k in range(1, ntm)]

    def cut(value):
        found = {}
        for k in list(range(2, ntm)) + [1, 0]:
            found[k] = lax.dynamic_slice_in_dim(value, (me ^ k) * share, share, axis=1)
            value = after(value, found[k])
        return [found[k] for k in range(ntm)]

    def join(ks, pieces, whole=None):
        return place(info, pieces, [spot(k) for k in ks], whole, tokens)

    flat = lambda value: value.reshape(-1, width)
    pieces = cut(currents[0])
    currents_in = exchange(pieces)
    cots = exchange(cut(after(cotangent[0], *pieces[1:])))
    kron_fwd, kron_bwd, thr_rows = build_krons(info, mixing, threshold, ntm, steps)

    def spike_grad(cot):
        grad = jnp.einsum("re,de->rd", flat(cot), weight, preferred_element_type=jnp.float32)
        return grad.astype(jnp.bfloat16).reshape(cot.shape)

    bias_term = jnp.sum(flat(cotangent).astype(jnp.float32), axis=0)
    grads = [spike_grad(cot) for cot in cots[:2]]
    spikes, surrogate = forward(kron_fwd, after(thr_rows, bias_term, *grads), currents_in)
    outs = [
        (jnp.dot(flat(spikes[k]), weight, preferred_element_type=jnp.float32) + bias)
        .astype(jnp.bfloat16)
        .reshape(steps, share, width)
        for k in range(ntm)
    ]
    outs_in = exchange(outs)
    grads.append(None)
    grads += [spike_grad(after(cot, *outs)) for cot in cots[3:]]

    shard = width // (ndp * ntm)
    core, y = ("tm", 0), ("dp", 0)
    zs, xs = [("dp", b) for b in range(1, bdp)], [("tm", b) for b in range(1, btm)]
    half = width // 2
    left = names[:-1]

    if shard % 8 == 0:
        turned = jnp.concatenate([flat(after(a, *outs)) for a in spikes]).T
        late = cots[:2] + [after(cots[2], turned, *grads[3:])] + cots[3:]
        halves = [weight_half(info, turned, late, part, shard) for part in range(2)]
    else:
        whole = sum(
            jnp.einsum("rd,re->de", flat(a), flat(b), preferred_element_type=jnp.float32)
            for a, b in zip(spikes, cots)
        ).reshape(-1, 2, shard, width)
        pick = lambda b: lax.dynamic_index_in_dim(whole, b, 1, keepdims=False)
        keep, send = pick(me & 1), pick(1 - (me & 1)).astype(jnp.bfloat16)
        halves = [(keep[..., c : c + half], [send[..., c : c + half]]) for c in (0, half)]

    sent = halves[-1][1][0]
    routes = ([y] + zs, zs + [y])

    def go(value, *path):
        if all(axis == path[0][0] for axis, _ in path):
            axis = path[0][0]
            return xor_permute(value, axis, sizes[axis], sum(1 << b for _, b in path))
        mask = sum((1 << b) * (ntm if axis == "dp" else 1) for axis, b in path)
        return xor_permute(value, ("dp", "tm"), ndp * ntm, mask)

    def step(state, lefts, bits, adds=(), joined=False):
        shapes = []
        for rest, bit in zip(lefts, bits):
            p = rest.index(bit)
            shapes.append((1 << p, 1 << (len(rest) - p - 1), slot(bit)))
        pairs, total = combine(info, shapes, state, adds, joined)
        return pairs, [[x for x in rest if x != bit] for rest, bit in zip(lefts, bits)], total

    def travel(pairs, bits):
        return [(keep, [go(send, bit)]) for (keep, send), bit in zip(pairs, bits)]

    state = [(keep, [go(after(send, sent), core) for send in sends]) for keep, sends in halves]
    bits = [route[0] for route in routes]
    pairs, lefts, _ = step(state, [left, left], bits)
    state = travel(pairs, bits)
    grads[2] = spike_grad(after(cots[2], outs_in[-1], *[send for _, send in pairs]))
    cgrads = list(backward(kron_bwd, surrogate, grads))
    cgrads_in = exchange(cgrads)

    for at in range(1, bdp):
        gate, adds = [], ()
        if at == 1:
            gate = outs_in[2:-1] + cgrads
        elif at == 2:
            gate = [sums]
        elif at == 3:
            adds = few
        else:
            adds = [total, go(total, ("dp", at - 2))]
        if gate:
            state[0] = (after(state[0][0], *gate), state[0][1])
        bits = [route[at] for route in routes]
        pairs, lefts, total = step(state, lefts, bits, adds)
        state = travel(pairs, bits)
        sends = [send for _, send in pairs]
        if at == 1:
            gated = after(surrogate, *sends)
            cross, tsum = cross_sums(gated, currents_in, grads)
            sums = pack_sums(info, bias_term.reshape(-1, 128), cross, tsum, ntm, steps)
        if at == 2:
            sums = after(sums, *sends)
            sums = sums + go(sums, core)
            few = [sums, go(sums, y), go(sums, ("dp", 1)), go(sums, y, ("dp", 1))]
    adds = few if bdp == 3 else [total, go(total, ("dp", bdp - 2))]
    early = [k for k in range(ntm) if k != 2]
    current_grad = join(early, [after(cgrads_in[0], *sends)] + [cgrads_in[k] for k in early[1:]])
    state[0] = (after(state[0][0], current_grad), state[0][1])
    current_grad = join([2], [cgrads_in[2]], current_grad)

    pairs, lefts, total = step(state, lefts, [xs[0]] * 2, adds, joined=True)
    keep, send = pairs[0]
    output = join(range(ntm), [after(outs_in[0], send)] + outs_in[1:])
    got = go(send, xs[0])
    rest = lefts[0]
    for bit in xs[1:]:
        pairs, (rest,), _ = step([(keep, [got])], [rest], [bit])
        keep, send = pairs[0]
        got = go(send, bit)
    last = [("dp", bdp - 1)] + xs
    sums = [total]
    for n in range(1, 1 << len(last)):
        sums.append(go(total, *[bit for i, bit in enumerate(last) if n >> i & 1]))
    weight_grad, mixing_grad, threshold_grad, bias_grad = final(
        keep.reshape(shard, width), got.reshape(shard, width), sums, ntm * steps, width
    )
    return (
        output[None],
        current_grad[None],
        weight_grad,
        mixing_grad,
        threshold_grad.reshape(-1),
        bias_grad.reshape(-1),
    )


def solution(mesh):
    return jax.shard_map(
        functools.partial(body, mesh.shape["dp"], mesh.shape["tm"]),
        mesh=mesh,
        in_specs=(P("dp", "tm", None, None), P(), P(), P(), P(), P("dp", "tm", None, None)),
        out_specs=(
            P("dp", "tm", None, None),
            P("dp", "tm", None, None),
            P(("dp", "tm"), None),
            P(),
            P(),
            P(),
        ),
        check_vma=False,
    )
```

time: 301 us -> 158 us (0.52)
  blocking collectives: 123 us -> 0 us
  waiting for transfers between devices: 80.6 us -> 21.6 us
  Pallas kernels: 0 us -> 56.6 us
  matrix products: 38.7 us -> 19.6 us
  starting transfers between devices: 13.7 us -> 28.2 us
  between operations: 14.2 us -> 0.87 us
    psum x1 -> x0, blocking collectives: 89.1 us -> none  [body(): lax.psum((mixing_term, threshold_term, bias_term), ('dp', 'tm'))]
    pallas_call x0 -> x15, Pallas kernels: none -> 56.6 us  [the longest x4 11 us: combine(): pl.pallas_call(functools.partial(combine_kernel, tuple(shapes), counts, l...]
    all_to_all x3 -> x0, waiting for transfers between devices: 53.4 us -> none  [the longest x1 27.3 us: body(): lax.all_to_all(spike_grad, 'tm', split_axis=2, concat_axis=1, tiled=True)]
    all_to_all x1 -> x0, blocking collectives: 33.8 us -> none  [body(): lax.all_to_all(tok_spikes, 'tm', split_axis=1, concat_axis=2, tiled=True)]
    ppermute x0 -> x30, starting transfers between devices: none -> 28.2 us  [xor_permute(): return lax.ppermute(value, axis, [(i, i ^ mask) for i in range(size)])]
    reduce_scatter x1 -> x0, waiting for transfers between devices: 27.2 us -> none  [body(): lax.psum_scatter(weight_term, ('dp', 'tm'), scatter_dimension=0, tiled=True)]
    ppermute x0 -> x30, waiting for transfers between devices: none -> 21.6 us  [xor_permute(): return lax.ppermute(value, axis, [(i, i ^ mask) for i in range(size)])]
    dot_general x6 -> x8, matrix products: 38.7 us -> 19.6 us  [the longest x4 10.9 us: spike_grad(): jnp.einsum('re,de->rd', flat(cot), weight, preferred_element_type=jnp.flo...]
  transfers between devices with their start and end apart: 4 -> 30, of which waited for: 3 -> 13; matrix products, arithmetic and copies ran while one was open for 12% -> 28% of each run, Pallas kernels for 0% -> 33%
where the time goes in v2:
time: 158 us; the launch traced here: 157 us
  Pallas kernels  56.6 us (36%)
  starting transfers between devices  28.2 us (18%)
  local copies, waits for them, and re-layouts  23.9 us (15%)
  waiting for transfers between devices  21.6 us (14%)
  matrix products  19.6 us (12%)
  other arithmetic  6.03 us (4%)
    ppermute x30, starting transfers between devices, xor_permute(): return lax.ppermute(value, axis, [(i, i ^ mask) for i in range(size)])  28.2 us
    ppermute x30, waiting for transfers between devices, xor_permute(): return lax.ppermute(value, axis, [(i, i ^ mask) for i in range(size)])  21.6 us
    dynamic_slice x8, local copies, waits for them, and re-layouts, cut(): found[k] = lax.dynamic_slice_in_dim(value, (me ^ k) * share, share, axis=1)  13.1 us
    pallas_call x4, Pallas kernels, combine(): pl.pallas_call(functools.partial(combine_kernel, tuple(shapes), counts, l...  11 us
    pallas_call x2, Pallas kernels, weight_half(): pl.pallas_call(functools.partial(weight_kernel, shard, len(cots)), grid=(...  10.9 us
    dot_general x4, matrix products, spike_grad(): jnp.einsum('re,de->rd', flat(cot), weight, preferred_element_type=jnp.flo...  10.9 us
    pallas_call x3, Pallas kernels, place(): pl.pallas_call(functools.partial(place_kernel, tuple(slots)), in_specs=[S...  8.97 us
    dot_general x4, matrix products, body(): jnp.dot(flat(spikes[k]), weight, preferred_element_type=jnp.float32) + bias  8.7 us
  transfers between devices with their start and end apart: 30, of which 13 were waited for; matrix products, arithmetic and copies ran while one was open for 28% of the time, Pallas kernels for 33%

profile of v2, /device:TPU:0, one launch (start us, length us, event | category | flops | bytes accessed | tf_op | source)
XLA Modules:
  0.0 156.8 jit_solution(18219621204751410413)
XLA Ops:
  0.7 2.1 %dynamic-slice_bitcast_fusion = bf16[8,32,1280]{2,1,0:T(8,128)(2,1)} fusion(bf16[1,8,128,1280]{3,2,1,0:T(8,128)(2,1)} %param.6, s32[]{:T(128)S(6)} %select_n.16), kind=kLoop, calls=%fused_computation.14 | loop fusion | bytes 1310724 | tf_op jit(solution)/shard_map/dynamic_slice | solution.py:444
  2.8 2.9 %collective-permute-start.2 = (bf16[8,32,1280]{2,1,0:T(8,128)(2,1)}, bf16[8,32,1280]{2,1,0:T(8,128)(2,1)}, u32[]{:S(2)}, u32[]{:S(2)}) collective-permute-start(bf16[8,32,1280]{2,1,0:T(8,128)(2,1)} %dynamic-slice_bitcast_fusion), channel_id=1, source_target_pairs={{0,2},{1,3},{2,0},{3,1},{4,6},{5,7},{6,4},{7,5},{8,10},{9,11},{10,... | collective-permute-start | bytes 1966088 | tf_op jit(solution)/shard_map/ppermute | solution.py:17
  5.7 2.0 %constant_dynamic-slice_fusion.6 = bf16[8,32,1280]{2,1,0:T(8,128)(2,1)} fusion(bf16[8,128,1280]{2,1,0:T(8,128)(2,1)} %bitcast.64, s32[]{:T(128)S(6)} %select_n.17), kind=kLoop, calls=%fused_computation.21 | loop fusion | bytes 1310724 | tf_op jit(solution)/shard_map/dynamic_slice | solution.py:444
  7.7 2.1 %constant_dynamic-slice_fusion.5 = bf16[8,32,1280]{2,1,0:T(8,128)(2,1)} fusion(bf16[8,128,1280]{2,1,0:T(8,128)(2,1)} %bitcast.65, s32[]{:T(128)S(6)} %select_n.18), kind=kLoop, calls=%fused_computation.20 | loop fusion | bytes 1310724 | tf_op jit(solution)/shard_map/dynamic_slice | solution.py:444
  9.9 2.0 %constant_dynamic-slice_fusion.4 = bf16[8,32,1280]{2,1,0:T(8,128)(2,1)} fusion(bf16[8,128,1280]{2,1,0:T(8,128)(2,1)} %bitcast.58, s32[]{:T(128)S(6)} %select_n.16), kind=kLoop, calls=%fused_computation.19 | loop fusion | bytes 1310724 | tf_op jit(solution)/shard_map/dynamic_slice | solution.py:444
  12.8 1.6 %collective-permute-start.5 = (bf16[8,32,1280]{2,1,0:T(8,128)(2,1)}, bf16[8,32,1280]{2,1,0:T(8,128)(2,1)}, u32[]{:S(2)}, u32[]{:S(2)}) collective-permute-start(bf16[8,32,1280]{2,1,0:T(8,128)(2,1)} %constant_dynamic-slice_fusion.3), channel_id=1, source_target_pairs={{0,3},{1,2},{2,1},{3,0},{4,7},{5,6},{6,5},{7,4},{8,11},{9,10},{10,... | collective-permute-start | bytes 1966088 | tf_op jit(solution)/shard_map/ppermute | solution.py:17
  17.0 1.9 %convolution_convert_fusion.3 = bf16[256,1280]{1,0:T(8,128)(2,1)} fusion(bf16[256,1280]{1,0:T(8,128)(2,1)S(1)} %bitcast.63, bf16[1280,1280]{1,0:T(8,128)(2,1)S(1)} %copy-done), kind=kOutput, calls=%fused_computation.13 | convolution fusion | flops 839188480 | bytes 4587520 | tf_op jit(solution)/shard_map/re,de->rd/dot_general | solution.py:458
  20.7 2.3 %build_krons.1 = (bf16[512,512]{1,0:T(8,128)(2,1)}, bf16[512,512]{1,0:T(8,128)(2,1)}, f32[512,1]{1,0:T(8,128)}) custom-call(s32[10]{0:T(128)} %stack.40.me_ref.info_ref, f32[32,32]{1,0:T(8,128)} %mixing_ref.1, f32[1,32]{1,0:T(1,128)} %bitcast.80), custom_call_target="tpu_custom_call" | custom-call | tf_op jit(solution)/shard_map/build_krons/pallas_call | solution.py:60
  23.0 2.0 %constant_dynamic-slice_fusion.refs_0_ = bf16[8,32,1280]{2,1,0:T(8,128)(2,1)} fusion(bf16[8,128,1280]{2,1,0:T(8,128)(2,1)} %bitcast.66, s32[]{:T(128)S(6)} %select_n.19), kind=kLoop, calls=%fused_computation.15 | loop fusion | bytes 1310724 | tf_op jit(solution)/shard_map/dynamic_slice | solution.py:444
  25.1 3.0 %convolution_convert_fusion.2 = bf16[256,1280]{1,0:T(8,128)(2,1)} fusion(bf16[256,1280]{1,0:T(8,128)(2,1)} %bitcast.15, bf16[1280,1280]{1,0:T(8,128)(2,1)S(1)} %copy-done), kind=kOutput, calls=%fused_computation.12 | convolution fusion | flops 839188480 | bytes 4587520 | tf_op jit(solution)/shard_map/re,de->rd/dot_general | solution.py:458
  28.0 7.2 %collective-permute-done.3.refs_3_ = bf16[8,32,1280]{2,1,0:T(8,128)(2,1)} collective-permute-done((bf16[8,32,1280]{2,1,0:T(8,128)(2,1)}, bf16[8,32,1280]{2,1,0:T(8,128)(2,1)}, u32[]{:S(2)}, u32[]{:S(2)}) %collective-permute-start.3) | collective-permute-done | bytes 655392 | tf_op jit(solution)/shard_map/ppermute | solution.py:17
  35.2 6.4 %forward.1 = (bf16[8,32,1280]{2,1,0:T(8,128)(2,1)}, bf16[8,32,1280]{2,1,0:T(8,128)(2,1)}, bf16[8,32,1280]{2,1,0:T(8,128)(2,1)}, bf16[8,32,1280]{2,1,0:T(8,128)(2,1)}, f32[2,512,1280]{2,1,0:T(8,128)}) custom-call(bf16[512,512]{1,0:T(8,128)(2,1)} %get-tuple-element.71.kron_ref, f32[512,1]{1,0:T(8,128)} %get-tuple-element.79.thr_ref, ...), custom_call_target="tpu_custom_call" | custom-call | tf_op jit(solution)/shard_map/forward/pallas_call | solution.py:99
  41.6 3.0 %fusion.3 = bf16[256,1280]{1,0:T(8,128)(2,1)} fusion(bf16[256,1280]{1,0:T(8,128)(2,1)} %bitcast.74, bf16[1280,1280]{1,0:T(8,128)(2,1)S(1)} %copy-done, f32[1280]{0:T(1024)S(1)} %copy-done.16), kind=kOutput, calls=%fused_computation.9 | convolution fusion | flops 839516160 | bytes 4592640 | tf_op jit(solution)/shard_map/dot_general | solution.py:465
  44.6 1.9 %fusion.2 = bf16[256,1280]{1,0:T(8,128)(2,1)} fusion(bf16[256,1280]{1,0:T(8,128)(2,1)S(1)} %bitcast.73, bf16[1280,1280]{1,0:T(8,128)(2,1)S(1)} %copy-done, f32[1280]{0:T(1024)S(1)} %copy-done.16), kind=kOutput, calls=%fused_computation.8 | convolution fusion | flops 839516160 | bytes 4592640 | tf_op jit(solution)/shard_map/dot_general | solution.py:465
  46.5 1.9 %fusion.1 = bf16[256,1280]{1,0:T(8,128)(2,1)} fusion(bf16[256,1280]{1,0:T(8,128)(2,1)S(1)} %bitcast.71, bf16[1280,1280]{1,0:T(8,128)(2,1)S(1)} %copy-done, f32[1280]{0:T(1024)S(1)} %copy-done.16), kind=kOutput, calls=%fused_computation.7 | convolution fusion | flops 839516160 | bytes 4592640 | tf_op jit(solution)/shard_map/dot_general | solution.py:465
  48.4 1.9 %fusion = bf16[256,1280]{1,0:T(8,128)(2,1)} fusion(bf16[256,1280]{1,0:T(8,128)(2,1)S(1)} %bitcast.69, bf16[1280,1280]{1,0:T(8,128)(2,1)S(1)} %copy-done, f32[1280]{0:T(1024)S(1)} %copy-done.16), kind=kOutput, calls=%fused_computation.6 | convolution fusion | flops 839516160 | bytes 4592640 | tf_op jit(solution)/shard_map/dot_general | solution.py:465
  50.3 2.2 %collective-permute-start.11 = (bf16[8,32,1280]{2,1,0:T(8,128)(2,1)}, bf16[8,32,1280]{2,1,0:T(8,128)(2,1)}, u32[]{:S(2)}, u32[]{:S(2)}) collective-permute-start(bf16[8,32,1280]{2,1,0:T(8,128)(2,1)} %bitcast.24), channel_id=1, source_target_pairs={{0,3},{1,2},{2,1},{3,0},{4,7},{5,6},{6,5},{7,4},{8,11},{9,10},{10,... | collective-permute-start | bytes 1966088 | tf_op jit(solution)/shard_map/ppermute | solution.py:17
  52.5 2.2 %copy.20 = bf16[256,1280]{0,1:T(8,128)(2,1)} copy(bf16[256,1280]{1,0:T(8,128)(2,1)} %bitcast.75) | data formatting | bytes 1310720 | tf_op jit(solution)/shard_map/reshape | solution.py:451
  54.7 2.2 %copy.19 = bf16[256,1280]{0,1:T(8,128)(2,1)} copy(bf16[256,1280]{1,0:T(8,128)(2,1)} %bitcast.72) | data formatting | bytes 1310720 | tf_op jit(solution)/shard_map/reshape | solution.py:451
  56.9 2.2 %copy.18 = bf16[256,1280]{0,1:T(8,128)(2,1)} copy(bf16[256,1280]{1,0:T(8,128)(2,1)} %bitcast.70) | data formatting | bytes 1310720 | tf_op jit(solution)/shard_map/reshape | solution.py:451
  59.0 2.2 %copy.17 = bf16[256,1280]{0,1:T(8,128)(2,1)} copy(bf16[256,1280]{1,0:T(8,128)(2,1)} %bitcast.68) | data formatting | bytes 1310720 | tf_op jit(solution)/shard_map/reshape | solution.py:451
  61.2 2.9 %maximum_bitcast_fusion.spikes_ref = bf16[1280,1024]{1,0:T(8,128)(2,1)} fusion(bf16[256,1280]{0,1:T(8,128)(2,1)} %copy.20, bf16[256,1280]{0,1:T(8,128)(2,1)} %copy.19, bf16[256,1280]{0,1:T(8,128)(2,1)} %copy.18, bf16[256,1280]{0,1:T(8,128)(2,1)} %copy.17), kind=kLoop, calls=%fused_computation.5 | loop fusion | flops 10485760 | bytes 5242880 | tf_op jit(solution)/shard_map/transpose | solution.py:481
  64.2 3.0 %convolution_convert_fusion.1 = bf16[256,1280]{1,0:T(8,128)(2,1)} fusion(bf16[256,1280]{1,0:T(8,128)(2,1)} %bitcast.30, bf16[1280,1280]{1,0:T(8,128)(2,1)S(1)} %copy-done), kind=kOutput, calls=%fused_computation.11 | convolution fusion | flops 839188480 | bytes 4587520 | tf_op jit(solution)/shard_map/re,de->rd/dot_general | solution.py:458
  67.2 5.4 %weight_half.3 = (f32[16,40,640]{2,1,0:T(8,128)}, bf16[8,40,640]{2,1,0:T(8,128)(2,1)}, bf16[8,40,640]{2,1,0:T(8,128)(2,1)}) custom-call(s32[10]{0:T(128)} %stack.40.me_ref.info_ref, bf16[1280,1024]{1,0:T(8,128)(2,1)} %maximum_bitcast_fusion.spikes_ref, bf16[8,32,1280]{2,1,0:T(8,128)(2,1)} %copy-done.3, bf16[8,32,1280]{2,1,0:T(8,128)(2,1)} %collective-permute-done.refs_1_, ...), custom_call_target="tpu_custom_call" | custom-call | flops 1000 | bytes 1000 | tf_op jit(solution)/shard_map/weight_half/pallas_call | solution.py:407
  72.6 5.5 %weight_half.2 = (f32[16,40,640]{2,1,0:T(8,128)}, bf16[8,40,640]{2,1,0:T(8,128)(2,1)}, bf16[8,40,640]{2,1,0:T(8,128)(2,1)}) custom-call(s32[10]{0:T(128)} %stack.40.me_ref.info_ref, bf16[1280,1024]{1,0:T(8,128)(2,1)} %maximum_bitcast_fusion.spikes_ref, bf16[8,32,1280]{2,1,0:T(8,128)(2,1)} %copy-done.3, bf16[8,32,1280]{2,1,0:T(8,128)(2,1)} %collective-permute-done.refs_1_, ...), custom_call_target="tpu_custom_call" | custom-call | flops 1000 | bytes 1000 | tf_op jit(solution)/shard_map/weight_half/pallas_call | solution.py:407
  81.9 4.1 %combine.4 = (f32[8,40,640]{2,1,0:T(8,128)}, bf16[8,40,640]{2,1,0:T(8,128)(2,1)}, f32[8,40,640]{2,1,0:T(8,128)}, bf16[8,40,640]{2,1,0:T(8,128)(2,1)}) custom-call(s32[10]{0:T(128)} %stack.40.me_ref.info_ref, f32[16,40,640]{2,1,0:T(8,128)} %get-tuple-element.91.refs_0_, f32[16,40,640]{2,1,0:T(8,128)} %get-tuple-element.92.refs_1_, ...), custom_call_target="tpu_custom_call" | custom-call | flops 1000 | bytes 1000 | tf_op jit(solution)/shard_map/combine/pallas_call | solution.py:335
  86.0 1.5 collective-permute-start.12
  87.5 1.6 %collective-permute-start.13 = (bf16[8,40,640]{2,1,0:T(8,128)(2,1)}, bf16[8,40,640]{2,1,0:T(8,128)(2,1)}, u32[]{:S(2)}, u32[]{:S(2)}) collective-permute-start(bf16[8,40,640]{2,1,0:T(8,128)(2,1)} %get-tuple-element.105), channel_id=1, source_target_pairs={{0,8},{4,12},{8,0},{12,4},{16,24},{20,28},{24,16},{28,20},{1,9},{5... | collective-permute-start | bytes 1228808 | tf_op jit(solution)/shard_map/ppermute | solution.py:17
  89.1 3.0 %convolution_convert_fusion = bf16[256,1280]{1,0:T(8,128)(2,1)} fusion(bf16[256,1280]{1,0:T(8,128)(2,1)} %bitcast.32, bf16[1280,1280]{1,0:T(8,128)(2,1)S(1)} %copy-done), kind=kOutput, calls=%fused_computation.10 | convolution fusion | flops 839188480 | bytes 4587520 | tf_op jit(solution)/shard_map/re,de->rd/dot_general | solution.py:458
  92.1 5.3 %backward.1 = (bf16[8,32,1280]{2,1,0:T(8,128)(2,1)}, bf16[8,32,1280]{2,1,0:T(8,128)(2,1)}, bf16[8,32,1280]{2,1,0:T(8,128)(2,1)}, bf16[8,32,1280]{2,1,0:T(8,128)(2,1)}) custom-call(bf16[512,512]{1,0:T(8,128)(2,1)} %get-tuple-element.102.kron_ref, f32[2,512,1280]{2,1,0:T(8,128)} %get-tuple-element.116.surrogate_ref, bf16[8,32,1280]{2,1,0:T(8,128)(2,1)} %bitcast.84, ...), custom_call_target="tpu_custom_call" | custom-call | flops 5368709120 | bytes 10485760 | tf_op jit(solution)/shard_map/backward/pallas_call | solution.py:137
  99.1 2.8 %combine.5 = (f32[4,40,640]{2,1,0:T(8,128)}, bf16[4,40,640]{2,1,0:T(8,128)(2,1)}, f32[4,40,640]{2,1,0:T(8,128)}, bf16[4,40,640]{2,1,0:T(8,128)(2,1)}) custom-call(s32[10]{0:T(128)} %stack.40.me_ref.info_ref, f32[8,40,640]{2,1,0:T(8,128)} %get-tuple-element.111.refs_0_, f32[8,40,640]{2,1,0:T(8,128)} %get-tuple-element.112.refs_1_, ...), custom_call_target="tpu_custom_call" | custom-call | flops 1000 | bytes 1000 | tf_op jit(solution)/shard_map/combine/pallas_call | solution.py:335
  101.9 1.6 %collective-permute-start.14 = (bf16[4,40,640]{2,1,0:T(8,128)(2,1)}, bf16[4,40,640]{2,1,0:T(8,128)(2,1)S(1)}, u32[]{:S(2)}, u32[]{:S(2)}) collective-permute-start(bf16[4,40,640]{2,1,0:T(8,128)(2,1)} %get-tuple-element.114), channel_id=1, source_target_pairs={{0,8},{4,12},{8,0},{12,4},{16,24},{20,28},{24,16},{28,20},{1,9},{5... | collective-permute-start | bytes 614408 | tf_op jit(solution)/shard_map/ppermute | solution.py:17
  105.4 2.7 %collective-permute-done.14.refs_2_ = bf16[4,40,640]{2,1,0:T(8,128)(2,1)S(1)} collective-permute-done((bf16[4,40,640]{2,1,0:T(8,128)(2,1)}, bf16[4,40,640]{2,1,0:T(8,128)(2,1)S(1)}, u32[]{:S(2)}, u32[]{:S(2)}) %collective-permute-start.14) | collective-permute-done | bytes 204832 | tf_op jit(solution)/shard_map/ppermute | solution.py:17
  108.1 2.6 %collective-permute-start.15 = (bf16[4,40,640]{2,1,0:T(8,128)(2,1)}, bf16[4,40,640]{2,1,0:T(8,128)(2,1)}, u32[]{:S(2)}, u32[]{:S(2)}) collective-permute-start(bf16[4,40,640]{2,1,0:T(8,128)(2,1)} %get-tuple-element.115), channel_id=1, source_target_pairs={{0,16},{4,20},{8,24},{12,28},{16,0},{20,4},{24,8},{28,12},{1,17},{... | collective-permute-start | bytes 614408 | tf_op jit(solution)/shard_map/ppermute | solution.py:17
  110.7 6.7 %cross_sums.1 = (f32[512,512]{1,0:T(8,128)}, f32[512,128]{1,0:T(8,128)}) custom-call(f32[2,512,1280]{2,1,0:T(8,128)} %get-tuple-element.116.surrogate_ref, bf16[8,32,1280]{2,1,0:T(8,128)(2,1)} %constant_dynamic-slice_fusion.refs_0_, bf16[8,32,1280]{2,1,0:T(8,128)(2,1)} %collective-permute-done.1.refs_1_, ...), custom_call_target="tpu_custom_call" | custom-call | flops 5368709120 | bytes 10485760 | tf_op jit(solution)/shard_map/cross_sums/pallas_call | solution.py:193
  117.4 3.3 %pack_sums.1 = f32[56,128]{1,0:T(8,128)} custom-call(s32[10]{0:T(128)} %stack.40.me_ref.info_ref, f32[10,128]{1,0:T(8,128)} %bitcast.79, f32[512,512]{1,0:T(8,128)} %get-tuple-element.117.cross_ref, f32[512,128]{1,0:T(8,128)} %get-tuple-element.118.tsum_ref), custom_call_target="tpu_custom_call" | custom-call | flops 1000 | bytes 1000 | tf_op jit(solution)/shard_map/pack_sums/pallas_call | solution.py:233
  120.7 2.1 %combine.6 = (f32[2,40,640]{2,1,0:T(8,128)}, bf16[2,40,640]{2,1,0:T(8,128)(2,1)}, f32[2,40,640]{2,1,0:T(8,128)}, bf16[2,40,640]{2,1,0:T(8,128)(2,1)}) custom-call(s32[10]{0:T(128)} %stack.40.me_ref.info_ref, f32[4,40,640]{2,1,0:T(8,128)} %get-tuple-element.119.refs_0_, f32[4,40,640]{2,1,0:T(8,128)} %get-tuple-element.120.refs_1_, ...), custom_call_target="tpu_custom_call" | custom-call | flops 1000 | bytes 1000 | tf_op jit(solution)/shard_map/combine/pallas_call | solution.py:335
  125.1 1.6 %collective-permute-start.23 = (f32[56,128]{1,0:T(8,128)S(1)}, f32[56,128]{1,0:T(8,128)S(1)}, u32[]{:S(2)}, u32[]{:S(2)}) collective-permute-start(f32[56,128]{1,0:T(8,128)S(1)} %add.54.refs_4_), channel_id=1, source_target_pairs={{0,12},{4,8},{8,4},{12,0},{16,28},{20,24},{24,20},{28,16},{1,13},{... | collective-permute-start | bytes 86024 | tf_op jit(solution)/shard_map/ppermute | solution.py:17
  126.7 3.1 %collective-permute-done.23.refs_7_ = f32[56,128]{1,0:T(8,128)S(1)} collective-permute-done((f32[56,128]{1,0:T(8,128)S(1)}, f32[56,128]{1,0:T(8,128)S(1)}, u32[]{:S(2)}, u32[]{:S(2)}) %collective-permute-start.23) | collective-permute-done | bytes 28704 | tf_op jit(solution)/shard_map/ppermute | solution.py:17
  129.8 1.6 %collective-permute-start.22 = (f32[56,128]{1,0:T(8,128)S(1)}, f32[56,128]{1,0:T(8,128)}, u32[]{:S(2)}, u32[]{:S(2)}) collective-permute-start(f32[56,128]{1,0:T(8,128)S(1)} %add.54.refs_4_), channel_id=1, source_target_pairs={{0,8},{4,12},{8,0},{12,4},{16,24},{20,28},{24,16},{28,20},{1,9},{5... | collective-permute-start | bytes 86024 | tf_op jit(solution)/shard_map/ppermute | solution.py:17
  131.4 2.4 %collective-permute-done.22.refs_6_ = f32[56,128]{1,0:T(8,128)} collective-permute-done((f32[56,128]{1,0:T(8,128)S(1)}, f32[56,128]{1,0:T(8,128)}, u32[]{:S(2)}, u32[]{:S(2)}) %collective-permute-start.22) | collective-permute-done | bytes 28704 | tf_op jit(solution)/shard_map/ppermute | solution.py:17
  134.8 1.4 collective-permute-start.21
  136.2 3.1 %place.3.refs_1_ = bf16[8,128,1280]{2,1,0:T(8,128)(2,1)} custom-call(s32[10]{0:T(128)} %stack.40.me_ref.info_ref, bf16[8,32,1280]{2,1,0:T(8,128)(2,1)} %get-tuple-element.124.refs_0_, bf16[8,32,1280]{2,1,0:T(8,128)(2,1)} %collective-permute-done.16.refs_1_, bf16[8,32,1280]{2,1,0:T(8,128)(2,1)} %collective-permute-done.17.refs_2_), custom_call_target="tpu_custom_call" | custom-call | flops 1000 | bytes 1000 | tf_op jit(solution)/shard_map/place/pallas_call | solution.py:271
  140.3 1.9 %combine.7 = (f32[1,40,1280]{2,1,0:T(8,128)}, bf16[1,40,1280]{2,1,0:T(8,128)(2,1)}, f32[56,128]{1,0:T(8,128)}) custom-call(s32[10]{0:T(128)} %stack.40.me_ref.info_ref, f32[2,40,640]{2,1,0:T(8,128)} %get-tuple-element.125.refs_0_, f32[2,40,640]{2,1,0:T(8,128)} %get-tuple-element.126.refs_1_, bf16[2,40,640]{2,1,0:T(8,128)(2,1)} %copy-done.9, ...), custom_call_target="tpu_custom_call" | custom-call | flops 1000 | bytes 1000 | tf_op jit(solution)/shard_map/combine/pallas_call | solution.py:335
  142.7 3.4 %collective-permute-start.29 = (f32[56,128]{1,0:T(8,128)}, f32[56,128]{1,0:T(8,128)S(1)}, u32[]{:S(2)}, u32[]{:S(2)}) collective-permute-start(f32[56,128]{1,0:T(8,128)} %get-tuple-element.131.refs_0_), channel_id=1, source_target_pairs={{0,18},{1,19},{2,16},{3,17},{4,22},{5,23},{6,20},{7,21},{8,26},{9,... | collective-permute-start | bytes 86024 | tf_op jit(solution)/shard_map/ppermute | solution.py:17
  147.1 2.6 %place.5 = bf16[8,128,1280]{2,1,0:T(8,128)(2,1)} custom-call(s32[10]{0:T(128)} %stack.40.me_ref.info_ref, bf16[8,32,1280]{2,1,0:T(8,128)(2,1)} %collective-permute-done.25.refs_0_, bf16[8,128,1280]{2,1,0:T(8,128)(2,1)} %place.3.refs_1_), custom_call_target="tpu_custom_call", output_to_operand_aliasing={{}: (2, {})} | custom-call | flops 1000 | bytes 1000 | tf_op jit(solution)/shard_map/place/pallas_call | solution.py:271
  149.7 3.3 %place.4 = bf16[8,128,1280]{2,1,0:T(8,128)(2,1)} custom-call(s32[10]{0:T(128)} %stack.40.me_ref.info_ref, bf16[8,32,1280]{2,1,0:T(8,128)(2,1)} %bitcast.76, bf16[8,32,1280]{2,1,0:T(8,128)(2,1)} %collective-permute-done.24.refs_1_, bf16[8,32,1280]{2,1,0:T(8,128)(2,1)} %collective-permute-done.10.refs_2_, bf16[8,32,1280]{2,1,0:T(8,128)(2,1)} %collective-permute-done.11.refs_3_), custom_call_target="tpu_custom_call" | custom-call | flops 1000 | bytes 1000 | tf_op jit(solution)/shard_map/place/pallas_call | solution.py:271
  153.8 1.7 %final.1 = (bf16[40,1280]{1,0:T(8,128)(2,1)}, f32[32,32]{1,0:T(8,128)}, f32[1,32]{1,0:T(1,128)}, f32[1,1280]{1,0:T(1,128)}) custom-call(f32[40,1280]{1,0:T(8,128)} %bitcast.77, bf16[40,1280]{1,0:T(8,128)(2,1)} %bitcast.78, f32[56,128]{1,0:T(8,128)} %get-tuple-element.131.refs_0_, f32[56,128]{1,0:T(8,128)} %copy-done.14, f32[56,128]{1,0:T(8,128)} %copy-done.13, ...), custom_call_target="tpu_custom_call" | custom-call | flops 1000 | bytes 1000 | tf_op jit(solution)/shard_map/final/pallas_call | solution.py:362
  (86 shorter events, 20.4 us)
Async XLA Ops:
  0.6 16.4 %copy-start = (bf16[1280,1280]{1,0:T(8,128)(2,1)S(1)}, bf16[1280,1280]{1,0:T(8,128)(2,1)}, u32[]{:S(2)}) copy-start(bf16[1280,1280]{1,0:T(8,128)(2,1)} %param.9) | copy-start | bytes 9830404
  2.8 32.4 %collective-permute-start.2 = (bf16[8,32,1280]{2,1,0:T(8,128)(2,1)}, bf16[8,32,1280]{2,1,0:T(8,128)(2,1)}, u32[]{:S(2)}, u32[]{:S(2)}) collective-permute-start(bf16[8,32,1280]{2,1,0:T(8,128)(2,1)} %dynamic-slice_bitcast_fusion), channel_id=1, source_target_pairs={{0,2},{1,3},{2,0},{3,1},{4,6},{5,7},{6,4},{7,5},{8,10},{9,11},{10,... | collective-permute-start | bytes 1966088 | tf_op jit(solution)/shard_map/ppermute | solution.py:17
  7.7 27.5 %collective-permute-start.3 = (bf16[8,32,1280]{2,1,0:T(8,128)(2,1)}, bf16[8,32,1280]{2,1,0:T(8,128)(2,1)}, u32[]{:S(2)}, u32[]{:S(2)}) collective-permute-start(bf16[8,32,1280]{2,1,0:T(8,128)(2,1)} %constant_dynamic-slice_fusion.6), channel_id=1, source_target_pairs={{0,3},{1,2},{2,1},{3,0},{4,7},{5,6},{6,5},{7,4},{8,11},{9,10},{10,... | collective-permute-start | bytes 1966088 | tf_op jit(solution)/shard_map/ppermute | solution.py:17
  7.7 4.2 %copy-start.1 = (bf16[1,8,128,1280]{3,2,1,0:T(8,128)(2,1)S(1)}, bf16[1,8,128,1280]{3,2,1,0:T(8,128)(2,1)}, u32[]{:S(2)}) copy-start(bf16[1,8,128,1280]{3,2,1,0:T(8,128)(2,1)} %param.11) | copy-start | bytes 7864324
  9.8 18.2 %collective-permute-start.1 = (bf16[8,32,1280]{2,1,0:T(8,128)(2,1)}, bf16[8,32,1280]{2,1,0:T(8,128)(2,1)}, u32[]{:S(2)}, u32[]{:S(2)}) collective-permute-start(bf16[8,32,1280]{2,1,0:T(8,128)(2,1)} %constant_dynamic-slice_fusion.5), channel_id=1, source_target_pairs={{0,1},{1,0},{2,3},{3,2},{4,5},{5,4},{6,7},{7,6},{8,9},{9,8},{10,11... | collective-permute-start | bytes 1966088 | tf_op jit(solution)/shard_map/ppermute | solution.py:17
  12.8 39.7 %collective-permute-start.5 = (bf16[8,32,1280]{2,1,0:T(8,128)(2,1)}, bf16[8,32,1280]{2,1,0:T(8,128)(2,1)}, u32[]{:S(2)}, u32[]{:S(2)}) collective-permute-start(bf16[8,32,1280]{2,1,0:T(8,128)(2,1)} %constant_dynamic-slice_fusion.3), channel_id=1, source_target_pairs={{0,3},{1,2},{2,1},{3,0},{4,7},{5,6},{6,5},{7,4},{8,11},{9,10},{10,... | collective-permute-start | bytes 1966088 | tf_op jit(solution)/shard_map/ppermute | solution.py:17
  15.4 9.7 %collective-permute-start = (bf16[8,32,1280]{2,1,0:T(8,128)(2,1)}, bf16[8,32,1280]{2,1,0:T(8,128)(2,1)}, u32[]{:S(2)}, u32[]{:S(2)}) collective-permute-start(bf16[8,32,1280]{2,1,0:T(8,128)(2,1)} %constant_dynamic-slice_fusion.2), channel_id=1, source_target_pairs={{0,1},{1,0},{2,3},{3,2},{4,5},{5,4},{6,7},{7,6},{8,9},{9,8},{10,11... | collective-permute-start | bytes 1966088 | tf_op jit(solution)/shard_map/ppermute | solution.py:17
  17.0 1.9 %copy-start.3 = (bf16[8,32,1280]{2,1,0:T(8,128)(2,1)}, bf16[8,32,1280]{2,1,0:T(8,128)(2,1)S(1)}, u32[]{:S(2)}) copy-start(bf16[8,32,1280]{2,1,0:T(8,128)(2,1)S(1)} %constant_dynamic-slice_fusion.1.refs_0_) | copy-start | bytes 1966084
  17.0 2.0 %copy-start.2 = (bf16[1,8,128,1280]{3,2,1,0:T(8,128)(2,1)S(1)}, bf16[1,8,128,1280]{3,2,1,0:T(8,128)(2,1)}, u32[]{:S(2)}) copy-start(bf16[1,8,128,1280]{3,2,1,0:T(8,128)(2,1)} %param.11) | copy-start | bytes 7864324
  25.0 42.1 %collective-permute-start.4 = (bf16[8,32,1280]{2,1,0:T(8,128)(2,1)}, bf16[8,32,1280]{2,1,0:T(8,128)(2,1)}, u32[]{:S(2)}, u32[]{:S(2)}) collective-permute-start(bf16[8,32,1280]{2,1,0:T(8,128)(2,1)} %constant_dynamic-slice_fusion.4), channel_id=1, source_target_pairs={{0,2},{1,3},{2,0},{3,1},{4,6},{5,7},{6,4},{7,5},{8,10},{9,11},{10,... | collective-permute-start | bytes 1966088 | tf_op jit(solution)/shard_map/ppermute | solution.py:17
  28.0 13.5 %copy-start.16 = (f32[1280]{0:T(1024)S(1)}, f32[1280]{0:T(1024)}, u32[]{:S(2)}) copy-start(f32[1280]{0:T(1024)} %param.10) | copy-start | bytes 15364
  41.6 3.0 %copy-start.6 = (bf16[8,32,1280]{2,1,0:T(8,128)(2,1)S(1)}, bf16[8,32,1280]{2,1,0:T(8,128)(2,1)}, u32[]{:S(2)}) copy-start(bf16[8,32,1280]{2,1,0:T(8,128)(2,1)} %get-tuple-element.87) | copy-start | bytes 1966084
  44.6 1.9 %copy-start.5 = (bf16[8,32,1280]{2,1,0:T(8,128)(2,1)S(1)}, bf16[8,32,1280]{2,1,0:T(8,128)(2,1)}, u32[]{:S(2)}) copy-start(bf16[8,32,1280]{2,1,0:T(8,128)(2,1)} %get-tuple-element.86) | copy-start | bytes 1966084
  46.5 1.9 %copy-start.4 = (bf16[8,32,1280]{2,1,0:T(8,128)(2,1)S(1)}, bf16[8,32,1280]{2,1,0:T(8,128)(2,1)}, u32[]{:S(2)}) copy-start(bf16[8,32,1280]{2,1,0:T(8,128)(2,1)} %get-tuple-element.85) | copy-start | bytes 1966084
  50.3 38.8 %collective-permute-start.11 = (bf16[8,32,1280]{2,1,0:T(8,128)(2,1)}, bf16[8,32,1280]{2,1,0:T(8,128)(2,1)}, u32[]{:S(2)}, u32[]{:S(2)}) collective-permute-start(bf16[8,32,1280]{2,1,0:T(8,128)(2,1)} %bitcast.24), channel_id=1, source_target_pairs={{0,3},{1,2},{2,1},{3,0},{4,7},{5,6},{6,5},{7,4},{8,11},{9,10},{10,... | collective-permute-start | bytes 1966088 | tf_op jit(solution)/shard_map/ppermute | solution.py:17
  78.1 2.1 %collective-permute-start.8 = (bf16[8,40,640]{2,1,0:T(8,128)(2,1)}, bf16[8,40,640]{2,1,0:T(8,128)(2,1)}, u32[]{:S(2)}, u32[]{:S(2)}) collective-permute-start(bf16[8,40,640]{2,1,0:T(8,128)(2,1)} %get-tuple-element.98), channel_id=1, source_target_pairs={{0,1},{1,0},{2,3},{3,2},{4,5},{5,4},{6,7},{7,6},{8,9},{9,8},{10,11... | collective-permute-start | bytes 1228808 | tf_op jit(solution)/shard_map/ppermute | solution.py:17
  78.1 2.7 %collective-permute-start.7 = (bf16[8,40,640]{2,1,0:T(8,128)(2,1)}, bf16[8,40,640]{2,1,0:T(8,128)(2,1)}, u32[]{:S(2)}, u32[]{:S(2)}) collective-permute-start(bf16[8,40,640]{2,1,0:T(8,128)(2,1)} %get-tuple-element.97), channel_id=1, source_target_pairs={{0,1},{1,0},{2,3},{3,2},{4,5},{5,4},{6,7},{7,6},{8,9},{9,8},{10,11... | collective-permute-start | bytes 1228808 | tf_op jit(solution)/shard_map/ppermute | solution.py:17
  78.6 2.7 %collective-permute-start.6 = (bf16[8,40,640]{2,1,0:T(8,128)(2,1)}, bf16[8,40,640]{2,1,0:T(8,128)(2,1)}, u32[]{:S(2)}, u32[]{:S(2)}) collective-permute-start(bf16[8,40,640]{2,1,0:T(8,128)(2,1)} %get-tuple-element.95), channel_id=1, source_target_pairs={{0,1},{1,0},{2,3},{3,2},{4,5},{5,4},{6,7},{7,6},{8,9},{9,8},{10,11... | collective-permute-start | bytes 1228808 | tf_op jit(solution)/shard_map/ppermute | solution.py:17
  78.7 3.3 %collective-permute-start.9 = (bf16[8,40,640]{2,1,0:T(8,128)(2,1)}, bf16[8,40,640]{2,1,0:T(8,128)(2,1)}, u32[]{:S(2)}, u32[]{:S(2)}) collective-permute-start(bf16[8,40,640]{2,1,0:T(8,128)(2,1)} %get-tuple-element.100), channel_id=1, source_target_pairs={{0,1},{1,0},{2,3},{3,2},{4,5},{5,4},{6,7},{7,6},{8,9},{9,8},{10,11... | collective-permute-start | bytes 1228808 | tf_op jit(solution)/shard_map/ppermute | solution.py:17
  80.2 17.3 %collective-permute-start.10 = (bf16[8,32,1280]{2,1,0:T(8,128)(2,1)}, bf16[8,32,1280]{2,1,0:T(8,128)(2,1)}, u32[]{:S(2)}, u32[]{:S(2)}) collective-permute-start(bf16[8,32,1280]{2,1,0:T(8,128)(2,1)} %bitcast.82), channel_id=1, source_target_pairs={{0,2},{1,3},{2,0},{3,1},{4,6},{5,7},{6,4},{7,5},{8,10},{9,11},{10,... | collective-permute-start | bytes 1966088 | tf_op jit(solution)/shard_map/ppermute | solution.py:17
  86.0 11.8 %collective-permute-start.12 = (bf16[8,40,640]{2,1,0:T(8,128)(2,1)}, bf16[8,40,640]{2,1,0:T(8,128)(2,1)}, u32[]{:S(2)}, u32[]{:S(2)}) collective-permute-start(bf16[8,40,640]{2,1,0:T(8,128)(2,1)} %get-tuple-element.104), channel_id=1, source_target_pairs={{0,4},{4,0},{8,12},{12,8},{16,20},{20,16},{24,28},{28,24},{1,5},{5... | collective-permute-start | bytes 1228808 | tf_op jit(solution)/shard_map/ppermute | solution.py:17
  87.5 11.5 %collective-permute-start.13 = (bf16[8,40,640]{2,1,0:T(8,128)(2,1)}, bf16[8,40,640]{2,1,0:T(8,128)(2,1)}, u32[]{:S(2)}, u32[]{:S(2)}) collective-permute-start(bf16[8,40,640]{2,1,0:T(8,128)(2,1)} %get-tuple-element.105), channel_id=1, source_target_pairs={{0,8},{4,12},{8,0},{12,4},{16,24},{20,28},{24,16},{28,20},{1,9},{5... | collective-permute-start | bytes 1228808 | tf_op jit(solution)/shard_map/ppermute | solution.py:17
  101.9 6.2 %collective-permute-start.14 = (bf16[4,40,640]{2,1,0:T(8,128)(2,1)}, bf16[4,40,640]{2,1,0:T(8,128)(2,1)S(1)}, u32[]{:S(2)}, u32[]{:S(2)}) collective-permute-start(bf16[4,40,640]{2,1,0:T(8,128)(2,1)} %get-tuple-element.114), channel_id=1, source_target_pairs={{0,8},{4,12},{8,0},{12,4},{16,24},{20,28},{24,16},{28,20},{1,9},{5... | collective-permute-start | bytes 614408 | tf_op jit(solution)/shard_map/ppermute | solution.py:17
  103.5 30.6 %collective-permute-start.16 = (bf16[8,32,1280]{2,1,0:T(8,128)(2,1)}, bf16[8,32,1280]{2,1,0:T(8,128)(2,1)}, u32[]{:S(2)}, u32[]{:S(2)}) collective-permute-start(bf16[8,32,1280]{2,1,0:T(8,128)(2,1)} %get-tuple-element.108), channel_id=1, source_target_pairs={{0,1},{1,0},{2,3},{3,2},{4,5},{5,4},{6,7},{7,6},{8,9},{9,8},{10,11... | collective-permute-start | bytes 1966088 | tf_op jit(solution)/shard_map/ppermute | solution.py:17
  103.5 46.2 %collective-permute-start.24 = (bf16[8,32,1280]{2,1,0:T(8,128)(2,1)}, bf16[8,32,1280]{2,1,0:T(8,128)(2,1)}, u32[]{:S(2)}, u32[]{:S(2)}) collective-permute-start(bf16[8,32,1280]{2,1,0:T(8,128)(2,1)} %bitcast.81), channel_id=1, source_target_pairs={{0,1},{1,0},{2,3},{3,2},{4,5},{5,4},{6,7},{7,6},{8,9},{9,8},{10,11... | collective-permute-start | bytes 1966088 | tf_op jit(solution)/shard_map/ppermute | solution.py:17
  104.0 42.6 %collective-permute-start.25 = (bf16[8,32,1280]{2,1,0:T(8,128)(2,1)}, bf16[8,32,1280]{2,1,0:T(8,128)(2,1)}, u32[]{:S(2)}, u32[]{:S(2)}) collective-permute-start(bf16[8,32,1280]{2,1,0:T(8,128)(2,1)} %get-tuple-element.109), channel_id=1, source_target_pairs={{0,2},{1,3},{2,0},{3,1},{4,6},{5,7},{6,4},{7,5},{8,10},{9,11},{10,... | collective-permute-start | bytes 1966088 | tf_op jit(solution)/shard_map/ppermute | solution.py:17
  104.6 30.2 %collective-permute-start.17 = (bf16[8,32,1280]{2,1,0:T(8,128)(2,1)}, bf16[8,32,1280]{2,1,0:T(8,128)(2,1)}, u32[]{:S(2)}, u32[]{:S(2)}) collective-permute-start(bf16[8,32,1280]{2,1,0:T(8,128)(2,1)} %get-tuple-element.110), channel_id=1, source_target_pairs={{0,3},{1,2},{2,1},{3,0},{4,7},{5,6},{6,5},{7,4},{8,11},{9,10},{10,... | collective-permute-start | bytes 1966088 | tf_op jit(solution)/shard_map/ppermute | solution.py:17
  108.1 9.3 %copy-start.7 = (bf16[4,40,640]{2,1,0:T(8,128)(2,1)}, bf16[4,40,640]{2,1,0:T(8,128)(2,1)S(1)}, u32[]{:S(2)}) copy-start(bf16[4,40,640]{2,1,0:T(8,128)(2,1)S(1)} %collective-permute-done.14.refs_2_) | copy-start | bytes 614404
  108.1 12.6 %collective-permute-start.15 = (bf16[4,40,640]{2,1,0:T(8,128)(2,1)}, bf16[4,40,640]{2,1,0:T(8,128)(2,1)}, u32[]{:S(2)}, u32[]{:S(2)}) collective-permute-start(bf16[4,40,640]{2,1,0:T(8,128)(2,1)} %get-tuple-element.115), channel_id=1, source_target_pairs={{0,16},{4,20},{8,24},{12,28},{16,0},{20,4},{24,8},{28,12},{1,17},{... | collective-permute-start | bytes 614408 | tf_op jit(solution)/shard_map/ppermute | solution.py:17
  122.9 1.4 collective-permute-start.20
  125.1 14.5 %copy-start.8 = (f32[56,128]{1,0:T(8,128)}, f32[56,128]{1,0:T(8,128)S(1)}, u32[]{:S(2)}) copy-start(f32[56,128]{1,0:T(8,128)S(1)} %add.54.refs_4_) | copy-start | bytes 86020
  125.1 4.8 %collective-permute-start.23 = (f32[56,128]{1,0:T(8,128)S(1)}, f32[56,128]{1,0:T(8,128)S(1)}, u32[]{:S(2)}, u32[]{:S(2)}) collective-permute-start(f32[56,128]{1,0:T(8,128)S(1)} %add.54.refs_4_), channel_id=1, source_target_pairs={{0,12},{4,8},{8,4},{12,0},{16,28},{20,24},{24,20},{28,16},{1,13},{... | collective-permute-start | bytes 86024 | tf_op jit(solution)/shard_map/ppermute | solution.py:17
  129.8 9.8 %copy-start.15 = (f32[56,128]{1,0:T(8,128)}, f32[56,128]{1,0:T(8,128)S(1)}, u32[]{:S(2)}) copy-start(f32[56,128]{1,0:T(8,128)S(1)} %collective-permute-done.23.refs_7_) | copy-start | bytes 86020
  129.8 4.0 %collective-permute-start.22 = (f32[56,128]{1,0:T(8,128)S(1)}, f32[56,128]{1,0:T(8,128)}, u32[]{:S(2)}, u32[]{:S(2)}) collective-permute-start(f32[56,128]{1,0:T(8,128)S(1)} %add.54.refs_4_), channel_id=1, source_target_pairs={{0,8},{4,12},{8,0},{12,4},{16,24},{20,28},{24,16},{28,20},{1,9},{5... | collective-permute-start | bytes 86024 | tf_op jit(solution)/shard_map/ppermute | solution.py:17
  133.8 5.8 %collective-permute-start.18 = (bf16[2,40,640]{2,1,0:T(8,128)(2,1)}, bf16[2,40,640]{2,1,0:T(8,128)(2,1)S(1)}, u32[]{:S(2)}, u32[]{:S(2)}) collective-permute-start(bf16[2,40,640]{2,1,0:T(8,128)(2,1)} %get-tuple-element.122), channel_id=1, source_target_pairs={{0,16},{4,20},{8,24},{12,28},{16,0},{20,4},{24,8},{28,12},{1,17},{... | collective-permute-start | bytes 307208 | tf_op jit(solution)/shard_map/ppermute | solution.py:17
  134.1 5.4 %collective-permute-start.19 = (bf16[2,40,640]{2,1,0:T(8,128)(2,1)}, bf16[2,40,640]{2,1,0:T(8,128)(2,1)S(1)}, u32[]{:S(2)}, u32[]{:S(2)}) collective-permute-start(bf16[2,40,640]{2,1,0:T(8,128)(2,1)} %get-tuple-element.123), channel_id=1, source_target_pairs={{0,4},{4,0},{8,12},{12,8},{16,20},{20,16},{24,28},{28,24},{1,5},{5... | collective-permute-start | bytes 307208 | tf_op jit(solution)/shard_map/ppermute | solution.py:17
  134.8 4.7 %collective-permute-start.21 = (f32[56,128]{1,0:T(8,128)S(1)}, f32[56,128]{1,0:T(8,128)}, u32[]{:S(2)}, u32[]{:S(2)}) collective-permute-start(f32[56,128]{1,0:T(8,128)S(1)} %add.54.refs_4_), channel_id=1, source_target_pairs={{0,4},{4,0},{8,12},{12,8},{16,20},{20,16},{24,28},{28,24},{1,5},{5... | collective-permute-start | bytes 86024 | tf_op jit(solution)/shard_map/ppermute | solution.py:17
  139.6 0.6 copy-start.9
  139.6 0.7 copy-start.10
  142.2 10.9 %collective-permute-start.26 = (bf16[1,40,1280]{2,1,0:T(8,128)(2,1)}, bf16[1,40,1280]{2,1,0:T(8,128)(2,1)S(1)}, u32[]{:S(2)}, u32[]{:S(2)}) collective-permute-start(bf16[1,40,1280]{2,1,0:T(8,128)(2,1)} %get-tuple-element.128), channel_id=1, source_target_pairs={{0,2},{1,3},{2,0},{3,1},{4,6},{5,7},{6,4},{7,5},{8,10},{9,11},{10,... | collective-permute-start | bytes 307208 | tf_op jit(solution)/shard_map/ppermute | solution.py:17
  142.7 10.3 %collective-permute-start.29 = (f32[56,128]{1,0:T(8,128)}, f32[56,128]{1,0:T(8,128)S(1)}, u32[]{:S(2)}, u32[]{:S(2)}) collective-permute-start(f32[56,128]{1,0:T(8,128)} %get-tuple-element.131.refs_0_), channel_id=1, source_target_pairs={{0,18},{1,19},{2,16},{3,17},{4,22},{5,23},{6,20},{7,21},{8,26},{9,... | collective-permute-start | bytes 86024 | tf_op jit(solution)/shard_map/ppermute | solution.py:17
  146.1 7.0 %collective-permute-start.28 = (f32[56,128]{1,0:T(8,128)}, f32[56,128]{1,0:T(8,128)S(1)}, u32[]{:S(2)}, u32[]{:S(2)}) collective-permute-start(f32[56,128]{1,0:T(8,128)} %get-tuple-element.131.refs_0_), channel_id=1, source_target_pairs={{0,2},{1,3},{2,0},{3,1},{4,6},{5,7},{6,4},{7,5},{8,10},{9,11},{10,... | collective-permute-start | bytes 86024 | tf_op jit(solution)/shard_map/ppermute | solution.py:17
  146.6 6.5 %collective-permute-start.27 = (f32[56,128]{1,0:T(8,128)}, f32[56,128]{1,0:T(8,128)S(1)}, u32[]{:S(2)}, u32[]{:S(2)}) collective-permute-start(f32[56,128]{1,0:T(8,128)} %get-tuple-element.131.refs_0_), channel_id=1, source_target_pairs={{0,16},{4,20},{8,24},{12,28},{16,0},{20,4},{24,8},{28,12},{1,17},{... | collective-permute-start | bytes 86024 | tf_op jit(solution)/shard_map/ppermute | solution.py:17
  153.1 0.6 copy-start.12
  153.1 0.6 copy-start.13
  153.1 0.6 copy-start.14
  153.1 0.7 copy-start.11

commit v3 on v2

--- a/solution.py
+++ b/solution.py
@@ -145,22 +145,17 @@
         out_specs=[piece] * parts,
         out_shape=[jax.ShapeDtypeStruct((steps, tokens, width), jnp.bfloat16)] * parts,
         cost_estimate=pl.CostEstimate(
-            flops=8 * rows * rows * width * (tokens // GROUP),
-            bytes_accessed=8 * rows * width * (tokens // GROUP),
+            flops=2 * rows * rows * width * (tokens // GROUP),
+            bytes_accessed=2 * rows * width * (tokens // GROUP),
             transcendentals=0,
         ),
         name="backward",
     )(kron, surrogate, *grads)
 
 
-def cross_kernel(parts, surrogate_ref, *refs):
-    sources, grads, (cross_ref, tsum_ref, both_ref) = (
-        refs[:parts],
-        refs[parts : 2 * parts],
-        refs[2 * parts :],
-    )
-    steps, group, width = sources[0].shape
-    every = parts * steps * group
+def cross_of(grads, surrogate, sources, cross_ref, tsum_ref, both_ref):
+    width = sources[0].shape[-1]
+    every = tsum_ref.shape[0]
 
     @pl.when(pl.program_id(0) == 0)
     def _():
@@ -170,7 +165,7 @@
     tile = 256
     total = jnp.zeros((every, 128), jnp.float32)
     for at in range(0, width, tile):
-        mg = rows_of(grads, at, tile).astype(jnp.float32) * surrogate_ref[0, :, at : at + tile]
+        mg = rows_of(grads, at, tile).astype(jnp.float32) * surrogate(at, tile)
         for piece in range(0, tile, 128):
             total = total + mg[:, piece : piece + 128]
         both_ref[:every, at : at + tile], both_ref[every:, at : at + tile] = parts_of(mg)
@@ -184,64 +179,114 @@
     cross_ref[...] += cross[:every] + cross[every:]
 
 
-def cross_sums(surrogate, sources, grads):
+def early_kernel(parts, surrogate_ref, *refs):
+    sources, grads, rest = refs[:parts], refs[parts : 2 * parts - 1], refs[2 * parts - 1 :]
+    rows = sources[0].shape[0] * sources[0].shape[1]
+
+    def surrogate(at, tile):
+        value = surrogate_ref[0, :, at : at + tile]
+        return jnp.concatenate([value[: 2 * rows], value[3 * rows :]], axis=0)
+
+    cross_of(grads, surrogate, sources, *rest)
+
+
+def early_sums(surrogate, sources, grads):
     parts = len(sources)
-    steps, tokens, width = sources[0].shape
-    rows = parts * steps * GROUP
+    steps, share, width = sources[0].shape
+    rows = steps * GROUP
+    every = (parts - 1) * rows
     piece = pl.BlockSpec((steps, GROUP, width), lambda g: (0, g, 0))
     fixed = lambda shape: pl.BlockSpec(shape, lambda g: (0, 0))
     return pl.pallas_call(
-        functools.partial(cross_kernel, parts),
-        grid=(tokens // GROUP,),
-        in_specs=[pl.BlockSpec((1, rows, width), lambda g: (g, 0, 0))] + [piece] * (2 * parts),
-        out_specs=[fixed((rows, rows)), fixed((rows, 128))],
+        functools.partial(early_kernel, parts),
+        grid=(share // GROUP,),
+        in_specs=[pl.BlockSpec((1, parts * rows, width), lambda g: (g, 0, 0))]
+        + [piece] * (2 * parts - 1),
+        out_specs=[fixed((every, parts * rows)), fixed((every, 128))],
         out_shape=[
-            jax.ShapeDtypeStruct((rows, rows), jnp.float32),
-            jax.ShapeDtypeStruct((rows, 128), jnp.float32),
+            jax.ShapeDtypeStruct((every, parts * rows), jnp.float32),
+            jax.ShapeDtypeStruct((every, 128), jnp.float32),
         ],
-        scratch_shapes=[pltpu.VMEM((2 * rows, width), jnp.bfloat16)],
+        scratch_shapes=[pltpu.VMEM((2 * every, width), jnp.bfloat16)],
+        cost_estimate=SMALL,
+        name="early_sums",
+    )(surrogate, *sources, *grads)
+
+
+def sums_kernel(parts, info_ref, surrogate_ref, bias_ref, early_ref, early_tsum_ref, *refs):
+    sources, (grad_ref, out_ref, cross_ref, tsum_ref, both_ref) = refs[:parts], refs[parts:]
+    steps, group, _ = grad_ref.shape
+    cross_of(
+        [grad_ref],
+        lambda at, tile: surrogate_ref[0, :, at : at + tile],
+        sources,
+        cross_ref,
+        tsum_ref,
+        both_ref,
+    )
+
+    @pl.when(pl.program_id(0) == pl.num_programs(0) - 1)
+    def _():
+        before = 2 * steps * group
+        whole = lambda early, late: jnp.concatenate(
+            [early[:before], late[...], early[before:]], axis=0
+        )
+        pick = selector(info_ref[0], parts, steps)
+        rows, total = pick.shape
+        one = jnp.where(pick, 1.0, 0.0)
+        exact = functools.partial(
+            lax.dot_general, precision=lax.Precision.HIGHEST, preferred_element_type=jnp.float32
+        )
+        cross = jnp.where(same_token(rows), whole(early_ref, cross_ref), 0.0)
+        narrow = exact(cross, one, (((1,), (0,)), ((), ())))
+        row_sum = -jnp.sum(whole(early_tsum_ref, tsum_ref), axis=1, keepdims=True)
+        out_ref[...] = jnp.zeros_like(out_ref)
+        out_ref[:total, :total] = exact(one, narrow, (((0,), (0,)), ((), ())))
+        out_ref[total : total + 8, :total] = jnp.broadcast_to(
+            jnp.sum(one * row_sum, axis=0, keepdims=True), (8, total)
+        )
+        out_ref[total + 8 : total + 8 + bias_ref.shape[0], :] = bias_ref[...]
+
+
+def small_sums(info, surrogate, bias_rows, early, sources, grad):
+    parts = len(sources)
+    steps, share, width = sources[0].shape
+    rows = steps * GROUP
+    piece = pl.BlockSpec((steps, GROUP, width), lambda g: (0, g, 0))
+    fixed = lambda shape: pl.BlockSpec(shape, lambda g: (0, 0))
+    out_rows = parts * steps + 8 + -(-bias_rows.shape[0] // 8) * 8
+    return pl.pallas_call(
+        functools.partial(sums_kernel, parts),
+        grid=(share // GROUP,),
+        in_specs=[
+            SMEM,
+            pl.BlockSpec((1, rows, width), lambda g: (g, 2, 0)),
+            fixed(bias_rows.shape),
+            fixed(early[0].shape),
+            fixed(early[1].shape),
+        ]
+        + [piece] * (parts + 1),
+        out_specs=fixed((out_rows, 128)),
+        out_shape=jax.ShapeDtypeStruct((out_rows, 128), jnp.float32),
+        scratch_shapes=[
+            pltpu.VMEM((rows, parts * rows), jnp.float32),
+            pltpu.VMEM((rows, 128), jnp.float32),
+            pltpu.VMEM((2 * rows, width), jnp.bfloat16),
+        ],
         cost_estimate=pl.CostEstimate(
-            flops=8 * rows * rows * width * (tokens // GROUP),
-            bytes_accessed=8 * rows * width * (tokens // GROUP),
+            flops=8 * parts * parts * rows * rows * width * (share // GROUP),
+            bytes_accessed=8 * parts * rows * width * (share // GROUP),
             transcendentals=0,
         ),
-        name="cross_sums",
-    )(surrogate, *sources, *grads)
-
-
-def sums_kernel(parts, steps, me_ref, bias_ref, cross_ref, tsum_ref, out_ref):
-    pick = selector(me_ref[0], parts, steps)
-    rows, total = pick.shape
-    one = jnp.where(pick, 1.0, 0.0)
-    exact = functools.partial(
-        lax.dot_general, precision=lax.Precision.HIGHEST, preferred_element_type=jnp.float32
-    )
-    turned = (((0,), (0,)), ((), ()))
-    cross = jnp.where(same_token(rows), cross_ref[...], 0.0)
-    narrow = exact(cross, one, (((1,), (0,)), ((), ())))
-    row_sum = -jnp.sum(tsum_ref[...], axis=1, keepdims=True)
-    out_ref[...] = jnp.zeros_like(out_ref)
-    out_ref[:total, :total] = exact(one, narrow, turned)
-    out_ref[total : total + 8, :total] = jnp.broadcast_to(
-        jnp.sum(one * row_sum, axis=0, keepdims=True), (8, total)
-    )
-    out_ref[total + 8 : total + 8 + bias_ref.shape[0], :] = bias_ref[...]
-
-
-def pack_sums(info, bias_rows, cross, tsum, parts, steps):
-    rows = parts * steps + 8 + -(-bias_rows.shape[0] // 8) * 8
-    return pl.pallas_call(
-        functools.partial(sums_kernel, parts, steps),
-        in_specs=[SMEM, VMEM, VMEM, VMEM],
-        out_specs=VMEM,
-        out_shape=jax.ShapeDtypeStruct((rows, 128), jnp.float32),
-        cost_estimate=SMALL,
-        name="pack_sums",
-    )(info, bias_rows, cross, tsum)
+        name="small_sums",
+    )(info, surrogate, bias_rows, *early, *sources, grad)
+
+
+HBM = pl.BlockSpec(memory_space=pl.ANY)
 
 
 def place_kernel(slots, info_ref, *refs):
-    pieces, (whole_ref, held_ref, in_sems, out_sems) = refs[: len(slots)], refs[-4:]
+    pieces, (whole_ref, held_ref, in_sems, out_sems) = refs[: len(slots)], refs[len(slots) :]
     share = held_ref.shape[2]
     loads, stores = [], []
     for n, slot in enumerate(slots):
@@ -261,27 +306,22 @@
         store.wait()
 
 
-def place(info, pieces, slots, whole, tokens):
+def place(info, pieces, slots, tokens):
     steps, share, width = pieces[0].shape
-    args, aliases, count = list(pieces), {}, len(pieces)
-    if whole is not None:
-        aliases = {1 + count: 0}
-        args.append(whole)
-    hbm = pl.BlockSpec(memory_space=pl.ANY)
+    count = len(pieces)
     return pl.pallas_call(
         functools.partial(place_kernel, tuple(slots)),
-        in_specs=[SMEM] + [hbm] * len(args),
-        out_specs=hbm,
+        in_specs=[SMEM] + [HBM] * count,
+        out_specs=HBM,
         out_shape=jax.ShapeDtypeStruct((steps, tokens, width), jnp.bfloat16),
         scratch_shapes=[
             pltpu.VMEM((count, steps, share, width), jnp.bfloat16),
             pltpu.SemaphoreType.DMA((count,)),
             pltpu.SemaphoreType.DMA((count,)),
         ],
-        input_output_aliases=aliases,
         cost_estimate=SMALL,
         name="place",
-    )(info, *args)
+    )(info, *pieces)
 
 
 def combine_kernel(shapes, counts, extra, joined, info_ref, *refs):
@@ -352,9 +392,7 @@
         sums = sums + ref[...]
     mix_ref[...] = sums[:total, :total]
     thr_ref[...] = sums[total : total + 1, :total]
-    bias_ref[...] = jnp.concatenate(
-        [sums[total + 8 + i : total + 9 + i] for i in range(biases)], axis=1
-    )
+    bias_ref[...] = sums[total + 8 : total + 8 + biases]
 
 
 def final(keep, got, sums, total, width):
@@ -367,56 +405,65 @@
             shape(keep.shape, jnp.bfloat16),
             shape((total, total), jnp.float32),
             shape((1, total), jnp.float32),
-            shape((1, width), jnp.float32),
+            shape((width // 128, 128), jnp.float32),
         ],
         cost_estimate=SMALL,
         name="final",
     )(keep, got, *sums)
 
 
-def weight_kernel(shard, parts, me_ref, spikes_ref, *refs):
-    cots, keep_ref, sends = refs[:parts], refs[parts], refs[parts + 1 :]
-    part = jnp.dot(
-        spikes_ref[...], rows_of(cots, 0, cots[0].shape[-1]), preferred_element_type=jnp.float32
+def weight_kernel(shard, parts, info_ref, *refs):
+    spikes, cots, outs = refs[:parts], refs[parts : 2 * parts], refs[2 * parts :]
+    part = lax.dot_general(
+        rows_of(spikes, 0, spikes[0].shape[-1]),
+        rows_of(cots, 0, cots[0].shape[-1]),
+        (((0,), (0,)), ((), ())),
+        preferred_element_type=jnp.float32,
     )
-    core = jnp.bitwise_and(me_ref[0], 1)
+    core = jnp.bitwise_and(info_ref[0], 1)
+    step = pl.program_id(0)
     pieces = [part[at : at + shard] for at in range(0, part.shape[0], shard)]
-    for mine in range(2):
-
-        @pl.when(core == mine)
-        def _():
-            for k, piece in enumerate(pieces):
-                if k % 2 == mine:
-                    keep_ref[k // 2] = piece
-
-    for step, send_ref in enumerate(sends):
+    for side in range(2):
         for mine in range(2):
 
-            @pl.when((core == mine) & (pl.program_id(0) == step))
+            @pl.when((core == mine) & (step // 2 == side))
+            def _():
+                for k, piece in enumerate(pieces):
+                    if k % 2 == mine:
+                        outs[side][k // 2] = piece
+
+    for at in range(4):
+        for mine in range(2):
+
+            @pl.when((core == mine) & (step == at))
             def _():
                 for k, piece in enumerate(pieces):
                     if k % 2 != mine:
-                        send_ref[k // 2] = piece.astype(send_ref.dtype)
-
-
-def weight_half(info, turned, cots, part, shard):
-    steps, tokens, width = cots[0].shape
+                        outs[2 + at][k // 2] = piece.astype(jnp.bfloat16)
+
+
+def weight_halves(info, spikes, cots, shard):
+    steps, tokens, width = spikes[0].shape
     block, cols = width // 2, width // 2
     count = block // shard // 2
     send = jax.ShapeDtypeStruct((count, shard, cols), jnp.bfloat16)
+    keep = jax.ShapeDtypeStruct((2 * count, shard, cols), jnp.float32)
     found = pl.pallas_call(
-        functools.partial(weight_kernel, shard, len(cots)),
-        grid=(2,),
+        functools.partial(weight_kernel, shard, len(spikes)),
+        grid=(4,),
         in_specs=[SMEM]
-        + [pl.BlockSpec((block, turned.shape[1]), lambda i: (i, 0))]
-        + [pl.BlockSpec((steps, tokens, cols), lambda i: (0, 0, part))] * len(cots),
-        out_specs=[pl.BlockSpec((count, shard, cols), lambda i: (i, 0, 0))]
-        + [pl.BlockSpec((count, shard, cols), lambda i: (0, 0, 0))] * 2,
-        out_shape=[jax.ShapeDtypeStruct((2 * count, shard, cols), jnp.float32), send, send],
+        + [pl.BlockSpec((steps, tokens, block), lambda i: (0, 0, i % 2))] * len(spikes)
+        + [pl.BlockSpec((steps, tokens, cols), lambda i: (0, 0, i // 2))] * len(spikes),
+        out_specs=[
+            pl.BlockSpec((count, shard, cols), lambda i: (jnp.minimum(i, 1), 0, 0)),
+            pl.BlockSpec((count, shard, cols), lambda i: (jnp.maximum(i - 2, 0), 0, 0)),
+        ]
+        + [pl.BlockSpec((count, shard, cols), lambda i: (0, 0, 0))] * 4,
+        out_shape=[keep, keep] + [send] * 4,
         cost_estimate=SMALL,
-        name="weight_half",
-    )(info, turned, *cots)
-    return found[0], found[1:]
+        name="weight_halves",
+    )(info, *spikes, *cots)
+    return [(found[0], found[2:4]), (found[1], found[4:6])]
 
 
 def body(ndp, ntm, currents, mixing, threshold, weight, bias, cotangent):
@@ -445,9 +492,6 @@
             value = after(value, found[k])
         return [found[k] for k in range(ntm)]
 
-    def join(ks, pieces, whole=None):
-        return place(info, pieces, [spot(k) for k in ks], whole, tokens)
-
     flat = lambda value: value.reshape(-1, width)
     pieces = cut(currents[0])
     currents_in = exchange(pieces)
@@ -471,6 +515,9 @@
     grads.append(None)
     grads += [spike_grad(after(cot, *outs)) for cot in cots[3:]]
 
+    others = [k for k in range(ntm) if k != 2]
+    early = early_sums(after(surrogate, *outs), currents_in, [grads[k] for k in others])
+
     shard = width // (ndp * ntm)
     core, y = ("tm", 0), ("dp", 0)
     zs, xs = [("dp", b) for b in range(1, bdp)], [("tm", b) for b in range(1, btm)]
@@ -478,9 +525,8 @@
     left = names[:-1]
 
     if shard % 8 == 0:
-        turned = jnp.concatenate([flat(after(a, *outs)) for a in spikes]).T
-        late = cots[:2] + [after(cots[2], turned, *grads[3:])] + cots[3:]
-        halves = [weight_half(info, turned, late, part, shard) for part in range(2)]
+        late = cots[:2] + [after(cots[2], *outs, *early)] + cots[3:]
+        halves = weight_halves(info, spikes, late, shard)
     else:
         whole = sum(
             jnp.einsum("rd,re->de", flat(a), flat(b), preferred_element_type=jnp.float32)
@@ -500,68 +546,72 @@
         mask = sum((1 << b) * (ntm if axis == "dp" else 1) for axis, b in path)
         return xor_permute(value, ("dp", "tm"), ndp * ntm, mask)
 
-    def step(state, lefts, bits, adds=(), joined=False):
+    def step(state, lefts, bits, joined=False):
         shapes = []
         for rest, bit in zip(lefts, bits):
             p = rest.index(bit)
             shapes.append((1 << p, 1 << (len(rest) - p - 1), slot(bit)))
-        pairs, total = combine(info, shapes, state, adds, joined)
-        return pairs, [[x for x in rest if x != bit] for rest, bit in zip(lefts, bits)], total
+        pairs, _ = combine(info, shapes, state, (), joined)
+        return pairs, [[x for x in rest if x != bit] for rest, bit in zip(lefts, bits)]
 
     def travel(pairs, bits):
         return [(keep, [go(send, bit)]) for (keep, send), bit in zip(pairs, bits)]
 
     state = [(keep, [go(after(send, sent), core) for send in sends]) for keep, sends in halves]
     bits = [route[0] for route in routes]
-    pairs, lefts, _ = step(state, [left, left], bits)
+    pairs, lefts = step(state, [left, left], bits)
     state = travel(pairs, bits)
     grads[2] = spike_grad(after(cots[2], outs_in[-1], *[send for _, send in pairs]))
     cgrads = list(backward(kron_bwd, surrogate, grads))
     cgrads_in = exchange(cgrads)
 
+    def meet(sums, *bits):
+        for bit in bits:
+            sums = sums + go(sums, bit)
+        return sums
+
     for at in range(1, bdp):
-        gate, adds = [], ()
-        if at == 1:
-            gate = outs_in[2:-1] + cgrads
-        elif at == 2:
-            gate = [sums]
-        elif at == 3:
-            adds = few
-        else:
-            adds = [total, go(total, ("dp", at - 2))]
-        if gate:
-            state[0] = (after(state[0][0], *gate), state[0][1])
+        gate = outs_in[1:3] + cgrads if at == 1 else [sums]
+        if at == 2:
+            gate.append(cgrads_in[1])
+        state[0] = (after(state[0][0], *gate), state[0][1])
         bits = [route[at] for route in routes]
-        pairs, lefts, total = step(state, lefts, bits, adds)
+        pairs, lefts = step(state, lefts, bits)
         state = travel(pairs, bits)
         sends = [send for _, send in pairs]
         if at == 1:
-            gated = after(surrogate, *sends)
-            cross, tsum = cross_sums(gated, currents_in, grads)
-            sums = pack_sums(info, bias_term.reshape(-1, 128), cross, tsum, ntm, steps)
-        if at == 2:
-            sums = after(sums, *sends)
-            sums = sums + go(sums, core)
-            few = [sums, go(sums, y), go(sums, ("dp", 1)), go(sums, y, ("dp", 1))]
-    adds = few if bdp == 3 else [total, go(total, ("dp", bdp - 2))]
-    early = [k for k in range(ntm) if k != 2]
-    current_grad = join(early, [after(cgrads_in[0], *sends)] + [cgrads_in[k] for k in early[1:]])
-    state[0] = (after(state[0][0], current_grad), state[0][1])
-    current_grad = join([2], [cgrads_in[2]], current_grad)
-
-    pairs, lefts, total = step(state, lefts, [xs[0]] * 2, adds, joined=True)
+            sums = small_sums(
+                info,
+                after(surrogate, *sends),
+                bias_term.reshape(-1, 128),
+                early,
+                currents_in,
+                grads[2],
+            )
+            hops = [core, y] + zs
+        else:
+            few = 3 if at == 2 else 1
+            sums = meet(after(sums, *sends), *hops[:few])
+            hops = hops[few:]
+    state[0] = (after(state[0][0], sums), state[0][1])
+
+    pairs, lefts = step(state, lefts, [xs[0]] * 2, joined=True)
     keep, send = pairs[0]
-    output = join(range(ntm), [after(outs_in[0], send)] + outs_in[1:])
     got = go(send, xs[0])
+    spots = list(map(spot, range(ntm)))
+    output = place(info, [after(outs_in[0], send)] + outs_in[1:], spots, tokens)
+    meeting = [after(sums, send)]
+    meeting.append(go(meeting[0], *hops))
+    sums = after(meeting[0], output) + meeting[1]
+    current_grad = place(info, [after(cgrads_in[0], sums)] + cgrads_in[1:], spots, tokens)
     rest = lefts[0]
     for bit in xs[1:]:
-        pairs, (rest,), _ = step([(keep, [got])], [rest], [bit])
+        pairs, (rest,) = step([(keep, [got])], [rest], [bit])
         keep, send = pairs[0]
         got = go(send, bit)
-    last = [("dp", bdp - 1)] + xs
-    sums = [total]
-    for n in range(1, 1 << len(last)):
-        sums.append(go(total, *[bit for i, bit in enumerate(last) if n >> i & 1]))
+    sums = [sums] + [
+        go(sums, *[bit for i, bit in enumerate(xs) if n >> i & 1]) for n in range(1, 1 << len(xs))
+    ]
     weight_grad, mixing_grad, threshold_grad, bias_grad = final(
         keep.reshape(shard, width), got.reshape(shard, width), sums, ntm * steps, width
     )

time: 158 us -> 143 us (0.905)
  local copies, waits for them, and re-layouts: 23.9 us -> 15.8 us
  other arithmetic: 6.03 us -> 1.8 us
  Pallas kernels: 56.6 us -> 54 us
  starting transfers between devices: 28.2 us -> 30 us
    reshape x4 -> x0, local copies, waits for them, and re-layouts: 8.7 us -> none  [body(): flat = lambda value: value.reshape(-1, width)]
    transpose x1 -> x0, other arithmetic: 2.94 us -> none  [body(): turned = jnp.concatenate([flat(after(a, *outs)) for a in spikes]).T]
    pallas_call x3 -> x2, Pallas kernels: 8.97 us -> 6.6 us  [place(): pl.pallas_call(functools.partial(place_kernel, tuple(slots)), in_specs=[S...]
    ppermute x30 -> x28, starting transfers between devices: 28.2 us -> 30 us  [xor_permute(): return lax.ppermute(value, axis, [(i, i ^ mask) for i in range(size)])]
    ppermute x30 -> x28, waiting for transfers between devices: 21.6 us -> 20.4 us  [xor_permute(): return lax.ppermute(value, axis, [(i, i ^ mask) for i in range(size)])]
    pallas_call x4 -> x3, Pallas kernels: 20.9 us -> 20.7 us  [the longest x1 9.6 us: weight_halves(): pl.pallas_call(functools.partial(weight_kernel, shard, len(spikes)), grid...]
  transfers between devices with their start and end apart: 30 -> 28, of which waited for: 13 -> 8; matrix products, arithmetic and copies ran while one was open for 28% -> 23% of each run, Pallas kernels for 33% -> 37%
where the time goes in v3:
time: 143 us; the launch traced here: 142 us
  Pallas kernels  54 us (38%)
  starting transfers between devices  30 us (21%)
  waiting for transfers between devices  20.4 us (14%)
  matrix products  19.5 us (14%)
  local copies, waits for them, and re-layouts  15.8 us (11%)
  other arithmetic  1.8 us (1%)
    ppermute x28, starting transfers between devices, xor_permute(): return lax.ppermute(value, axis, [(i, i ^ mask) for i in range(size)])  30 us
    ppermute x28, waiting for transfers between devices, xor_permute(): return lax.ppermute(value, axis, [(i, i ^ mask) for i in range(size)])  20.4 us
    dynamic_slice x8, local copies, waits for them, and re-layouts, cut(): found[k] = lax.dynamic_slice_in_dim(value, (me ^ k) * share, share, axis=1)  13.1 us
    pallas_call x4, Pallas kernels, combine(): pl.pallas_call(functools.partial(combine_kernel, tuple(shapes), counts, l...  10.9 us
    dot_general x4, matrix products, spike_grad(): jnp.einsum('re,de->rd', flat(cot), weight, preferred_element_type=jnp.flo...  10.9 us
    pallas_call x1, Pallas kernels, weight_halves(): pl.pallas_call(functools.partial(weight_kernel, shard, len(spikes)), grid...  9.6 us
    dot_general x4, matrix products, body(): jnp.dot(flat(spikes[k]), weight, preferred_element_type=jnp.float32) + bias  8.67 us
    pallas_call x2, Pallas kernels, place(): pl.pallas_call(functools.partial(place_kernel, tuple(slots)), in_specs=[S...  6.6 us
  transfers between devices with their start and end apart: 28, of which 8 were waited for; matrix products, arithmetic and copies ran while one was open for 23% of the time, Pallas kernels for 37%

profile of v3, /device:TPU:0, one launch (start us, length us, event | category | flops | bytes accessed | tf_op | source)
XLA Modules:
  0.0 142.3 jit_solution(18402441865738374033)
XLA Ops:
  0.7 2.1 %dynamic-slice_bitcast_fusion = bf16[8,32,1280]{2,1,0:T(8,128)(2,1)} fusion(bf16[1,8,128,1280]{3,2,1,0:T(8,128)(2,1)} %param.6, s32[]{:T(128)S(6)} %select_n.16), kind=kLoop, calls=%fused_computation.13 | loop fusion | bytes 1310724 | tf_op jit(solution)/shard_map/dynamic_slice | solution.py:491
  2.8 2.9 %collective-permute-start.2 = (bf16[8,32,1280]{2,1,0:T(8,128)(2,1)}, bf16[8,32,1280]{2,1,0:T(8,128)(2,1)}, u32[]{:S(2)}, u32[]{:S(2)}) collective-permute-start(bf16[8,32,1280]{2,1,0:T(8,128)(2,1)} %dynamic-slice_bitcast_fusion), channel_id=1, source_target_pairs={{0,2},{1,3},{2,0},{3,1},{4,6},{5,7},{6,4},{7,5},{8,10},{9,11},{10,... | collective-permute-start | bytes 1966088 | tf_op jit(solution)/shard_map/ppermute | solution.py:17
  5.7 2.0 %constant_dynamic-slice_fusion.6 = bf16[8,32,1280]{2,1,0:T(8,128)(2,1)} fusion(bf16[8,128,1280]{2,1,0:T(8,128)(2,1)} %bitcast.63, s32[]{:T(128)S(6)} %select_n.17), kind=kLoop, calls=%fused_computation.20 | loop fusion | bytes 1310724 | tf_op jit(solution)/shard_map/dynamic_slice | solution.py:491
  7.7 2.1 %constant_dynamic-slice_fusion.5 = bf16[8,32,1280]{2,1,0:T(8,128)(2,1)} fusion(bf16[8,128,1280]{2,1,0:T(8,128)(2,1)} %bitcast.64, s32[]{:T(128)S(6)} %select_n.18), kind=kLoop, calls=%fused_computation.19 | loop fusion | bytes 1310724 | tf_op jit(solution)/shard_map/dynamic_slice | solution.py:491
  9.9 2.0 %constant_dynamic-slice_fusion.4 = bf16[8,32,1280]{2,1,0:T(8,128)(2,1)} fusion(bf16[8,128,1280]{2,1,0:T(8,128)(2,1)} %bitcast.53, s32[]{:T(128)S(6)} %select_n.16), kind=kLoop, calls=%fused_computation.18 | loop fusion | bytes 1310724 | tf_op jit(solution)/shard_map/dynamic_slice | solution.py:491
  12.8 1.6 %collective-permute-start.5 = (bf16[8,32,1280]{2,1,0:T(8,128)(2,1)}, bf16[8,32,1280]{2,1,0:T(8,128)(2,1)}, u32[]{:S(2)}, u32[]{:S(2)}) collective-permute-start(bf16[8,32,1280]{2,1,0:T(8,128)(2,1)} %constant_dynamic-slice_fusion.3), channel_id=1, source_target_pairs={{0,3},{1,2},{2,1},{3,0},{4,7},{5,6},{6,5},{7,4},{8,11},{9,10},{10,... | collective-permute-start | bytes 1966088 | tf_op jit(solution)/shard_map/ppermute | solution.py:17
  15.9 1.1 constant_dynamic-slice_fusion.1.refs_4_
  17.0 1.9 %convolution_convert_fusion.3 = bf16[256,1280]{1,0:T(8,128)(2,1)} fusion(bf16[256,1280]{1,0:T(8,128)(2,1)S(1)} %bitcast.68, bf16[1280,1280]{1,0:T(8,128)(2,1)S(1)} %copy-done), kind=kOutput, calls=%fused_computation.12 | convolution fusion | flops 839188480 | bytes 4587520 | tf_op jit(solution)/shard_map/re,de->rd/dot_general | solution.py:502
  20.7 2.3 %build_krons.1 = (bf16[512,512]{1,0:T(8,128)(2,1)}, bf16[512,512]{1,0:T(8,128)(2,1)}, f32[512,1]{1,0:T(8,128)}) custom-call(s32[10]{0:T(128)} %stack.40.me_ref.info_ref, f32[32,32]{1,0:T(8,128)} %mixing_ref.1, f32[1,32]{1,0:T(1,128)} %bitcast.79), custom_call_target="tpu_custom_call" | custom-call | tf_op jit(solution)/shard_map/build_krons/pallas_call | solution.py:60
  23.0 2.0 %constant_dynamic-slice_fusion.refs_0_ = bf16[8,32,1280]{2,1,0:T(8,128)(2,1)} fusion(bf16[8,128,1280]{2,1,0:T(8,128)(2,1)} %bitcast.65, s32[]{:T(128)S(6)} %select_n.19), kind=kLoop, calls=%fused_computation.14 | loop fusion | bytes 1310724 | tf_op jit(solution)/shard_map/dynamic_slice | solution.py:491
  25.0 3.0 %convolution_convert_fusion.2 = bf16[256,1280]{1,0:T(8,128)(2,1)} fusion(bf16[256,1280]{1,0:T(8,128)(2,1)} %bitcast.15, bf16[1280,1280]{1,0:T(8,128)(2,1)S(1)} %copy-done), kind=kOutput, calls=%fused_computation.11 | convolution fusion | flops 839188480 | bytes 4587520 | tf_op jit(solution)/shard_map/re,de->rd/dot_general | solution.py:502
  28.0 7.2 %collective-permute-done.3.refs_3_ = bf16[8,32,1280]{2,1,0:T(8,128)(2,1)} collective-permute-done((bf16[8,32,1280]{2,1,0:T(8,128)(2,1)}, bf16[8,32,1280]{2,1,0:T(8,128)(2,1)}, u32[]{:S(2)}, u32[]{:S(2)}) %collective-permute-start.3) | collective-permute-done | bytes 655392 | tf_op jit(solution)/shard_map/ppermute | solution.py:17
  35.2 6.5 %forward.1 = (bf16[8,32,1280]{2,1,0:T(8,128)(2,1)}, bf16[8,32,1280]{2,1,0:T(8,128)(2,1)}, bf16[8,32,1280]{2,1,0:T(8,128)(2,1)}, bf16[8,32,1280]{2,1,0:T(8,128)(2,1)}, f32[2,512,1280]{2,1,0:T(8,128)}) custom-call(bf16[512,512]{1,0:T(8,128)(2,1)} %get-tuple-element.69.kron_ref, f32[512,1]{1,0:T(8,128)} %get-tuple-element.77.thr_ref, ...), custom_call_target="tpu_custom_call" | custom-call | tf_op jit(solution)/shard_map/forward/pallas_call | solution.py:99
  41.7 3.0 %fusion.3 = bf16[256,1280]{1,0:T(8,128)(2,1)} fusion(bf16[256,1280]{1,0:T(8,128)(2,1)} %bitcast.75, bf16[1280,1280]{1,0:T(8,128)(2,1)S(1)} %copy-done, f32[1280]{0:T(1024)S(1)} %copy-done.13), kind=kOutput, calls=%fused_computation.8 | convolution fusion | flops 839516160 | bytes 4592640 | tf_op jit(solution)/shard_map/dot_general | solution.py:509
  44.7 1.9 %fusion.2 = bf16[256,1280]{1,0:T(8,128)(2,1)} fusion(bf16[256,1280]{1,0:T(8,128)(2,1)S(1)} %bitcast.74, bf16[1280,1280]{1,0:T(8,128)(2,1)S(1)} %copy-done, f32[1280]{0:T(1024)S(1)} %copy-done.13), kind=kOutput, calls=%fused_computation.7 | convolution fusion | flops 839516160 | bytes 4592640 | tf_op jit(solution)/shard_map/dot_general | solution.py:509
  46.6 2.2 %collective-permute-start.12 = (bf16[8,32,1280]{2,1,0:T(8,128)(2,1)}, bf16[8,32,1280]{2,1,0:T(8,128)(2,1)}, u32[]{:S(2)}, u32[]{:S(2)}) collective-permute-start(bf16[8,32,1280]{2,1,0:T(8,128)(2,1)} %bitcast.24), channel_id=1, source_target_pairs={{0,3},{1,2},{2,1},{3,0},{4,7},{5,6},{6,5},{7,4},{8,11},{9,10},{10,... | collective-permute-start | bytes 1966088 | tf_op jit(solution)/shard_map/ppermute | solution.py:17
  48.8 1.9 %fusion.1 = bf16[256,1280]{1,0:T(8,128)(2,1)} fusion(bf16[256,1280]{1,0:T(8,128)(2,1)S(1)} %bitcast.73, bf16[1280,1280]{1,0:T(8,128)(2,1)S(1)} %copy-done, f32[1280]{0:T(1024)S(1)} %copy-done.13), kind=kOutput, calls=%fused_computation.6 | convolution fusion | flops 839516160 | bytes 4592640 | tf_op jit(solution)/shard_map/dot_general | solution.py:509
  50.7 1.9 %fusion = bf16[256,1280]{1,0:T(8,128)(2,1)} fusion(bf16[256,1280]{1,0:T(8,128)(2,1)S(1)} %bitcast.72, bf16[1280,1280]{1,0:T(8,128)(2,1)S(1)} %copy-done, f32[1280]{0:T(1024)S(1)} %copy-done.13), kind=kOutput, calls=%fused_computation.5 | convolution fusion | flops 839516160 | bytes 4592640 | tf_op jit(solution)/shard_map/dot_general | solution.py:509
  52.6 3.0 %convolution_convert_fusion.1 = bf16[256,1280]{1,0:T(8,128)(2,1)} fusion(bf16[256,1280]{1,0:T(8,128)(2,1)} %bitcast.25, bf16[1280,1280]{1,0:T(8,128)(2,1)S(1)} %copy-done), kind=kOutput, calls=%fused_computation.10 | convolution fusion | flops 839188480 | bytes 4587520 | tf_op jit(solution)/shard_map/re,de->rd/dot_general | solution.py:502
  55.6 5.9 %early_sums.1 = (f32[384,512]{1,0:T(8,128)}, f32[384,128]{1,0:T(8,128)}) custom-call(f32[2,512,1280]{2,1,0:T(8,128)} %get-tuple-element.113.surrogate_ref, bf16[8,32,1280]{2,1,0:T(8,128)(2,1)} %constant_dynamic-slice_fusion.refs_0_, bf16[8,32,1280]{2,1,0:T(8,128)(2,1)} %collective-permute-done.1.refs_1_, ...), custom_call_target="tpu_custom_call" | custom-call | flops 1000 | bytes 1000 | tf_op jit(solution)/shard_map/early_sums/pallas_call | solution.py:200
  61.5 2.2 %collective-permute-done.4.refs_6_ = bf16[8,32,1280]{2,1,0:T(8,128)(2,1)} collective-permute-done((bf16[8,32,1280]{2,1,0:T(8,128)(2,1)}, bf16[8,32,1280]{2,1,0:T(8,128)(2,1)}, u32[]{:S(2)}, u32[]{:S(2)}) %collective-permute-start.4) | collective-permute-done | bytes 655392 | tf_op jit(solution)/shard_map/ppermute | solution.py:17
  63.7 9.6 %weight_halves.1 = (f32[16,40,640]{2,1,0:T(8,128)}, f32[16,40,640]{2,1,0:T(8,128)}, bf16[8,40,640]{2,1,0:T(8,128)(2,1)}, bf16[8,40,640]{2,1,0:T(8,128)(2,1)}, bf...) custom-call(s32[10]{0:T(128)} %stack.40.me_ref.info_ref, bf16[8,32,1280]{2,1,0:T(8,128)(2,1)} %get-tuple-element.79.refs_0_, ...), custom_call_target="tpu_custom_call" | custom-call | flops 1000 | bytes 1000 | tf_op jit(solution)/shard_map/weight_halves/pallas_call | solution.py:451
  74.4 1.1 collective-permute-done.8.refs_4_
  76.1 2.1 %collective-permute-start.11 = (bf16[8,32,1280]{2,1,0:T(8,128)(2,1)}, bf16[8,32,1280]{2,1,0:T(8,128)(2,1)}, u32[]{:S(2)}, u32[]{:S(2)}) collective-permute-start(bf16[8,32,1280]{2,1,0:T(8,128)(2,1)} %bitcast.80), channel_id=1, source_target_pairs={{0,2},{1,3},{2,0},{3,1},{4,6},{5,7},{6,4},{7,5},{8,10},{9,11},{10,... | collective-permute-start | bytes 1966088 | tf_op jit(solution)/shard_map/ppermute | solution.py:17
  78.1 4.1 %combine.4 = (f32[8,40,640]{2,1,0:T(8,128)}, bf16[8,40,640]{2,1,0:T(8,128)(2,1)}, f32[8,40,640]{2,1,0:T(8,128)}, bf16[8,40,640]{2,1,0:T(8,128)(2,1)}) custom-call(s32[10]{0:T(128)} %stack.40.me_ref.info_ref, f32[16,40,640]{2,1,0:T(8,128)} %get-tuple-element.89.refs_0_, f32[16,40,640]{2,1,0:T(8,128)} %get-tuple-element.90.refs_1_, ...), custom_call_target="tpu_custom_call" | custom-call | flops 1000 | bytes 1000 | tf_op jit(solution)/shard_map/combine/pallas_call | solution.py:375
  82.2 1.5 %collective-permute-start.13 = (bf16[8,40,640]{2,1,0:T(8,128)(2,1)}, bf16[8,40,640]{2,1,0:T(8,128)(2,1)}, u32[]{:S(2)}, u32[]{:S(2)}) collective-permute-start(bf16[8,40,640]{2,1,0:T(8,128)(2,1)} %get-tuple-element.101), channel_id=1, source_target_pairs={{0,4},{4,0},{8,12},{12,8},{16,20},{20,16},{24,28},{28,24},{1,5},{5... | collective-permute-start | bytes 1228808 | tf_op jit(solution)/shard_map/ppermute | solution.py:17
  83.7 1.6 %collective-permute-start.14 = (bf16[8,40,640]{2,1,0:T(8,128)(2,1)}, bf16[8,40,640]{2,1,0:T(8,128)(2,1)}, u32[]{:S(2)}, u32[]{:S(2)}) collective-permute-start(bf16[8,40,640]{2,1,0:T(8,128)(2,1)} %get-tuple-element.102), channel_id=1, source_target_pairs={{0,8},{4,12},{8,0},{12,4},{16,24},{20,28},{24,16},{28,20},{1,9},{5... | collective-permute-start | bytes 1228808 | tf_op jit(solution)/shard_map/ppermute | solution.py:17
  85.3 3.0 %convolution_convert_fusion = bf16[256,1280]{1,0:T(8,128)(2,1)} fusion(bf16[256,1280]{1,0:T(8,128)(2,1)} %bitcast.27, bf16[1280,1280]{1,0:T(8,128)(2,1)S(1)} %copy-done), kind=kOutput, calls=%fused_computation.9 | convolution fusion | flops 839188480 | bytes 4587520 | tf_op jit(solution)/shard_map/re,de->rd/dot_general | solution.py:502
  88.3 5.3 %backward.1 = (bf16[8,32,1280]{2,1,0:T(8,128)(2,1)}, bf16[8,32,1280]{2,1,0:T(8,128)(2,1)}, bf16[8,32,1280]{2,1,0:T(8,128)(2,1)}, bf16[8,32,1280]{2,1,0:T(8,128)(2,1)}) custom-call(bf16[512,512]{1,0:T(8,128)(2,1)} %get-tuple-element.100.kron_ref, f32[2,512,1280]{2,1,0:T(8,128)} %get-tuple-element.113.surrogate_ref, bf16[8,32,1280]{2,1,0:T(8,128)(2,1)} %bitcast.58, ...), custom_call_target="tpu_custom_call" | custom-call | flops 1342177280 | bytes 2621440 | tf_op jit(solution)/shard_map/backward/pallas_call | solution.py:137
  93.6 1.2 collective-permute-start.24
  95.5 2.8 %combine.5 = (f32[4,40,640]{2,1,0:T(8,128)}, bf16[4,40,640]{2,1,0:T(8,128)(2,1)}, f32[4,40,640]{2,1,0:T(8,128)}, bf16[4,40,640]{2,1,0:T(8,128)(2,1)}) custom-call(s32[10]{0:T(128)} %stack.40.me_ref.info_ref, f32[8,40,640]{2,1,0:T(8,128)} %get-tuple-element.108.refs_0_, f32[8,40,640]{2,1,0:T(8,128)} %get-tuple-element.109.refs_1_, ...), custom_call_target="tpu_custom_call" | custom-call | flops 1000 | bytes 1000 | tf_op jit(solution)/shard_map/combine/pallas_call | solution.py:375
  98.3 1.1 collective-permute-start.16
  99.4 2.6 %collective-permute-start.17 = (bf16[4,40,640]{2,1,0:T(8,128)(2,1)}, bf16[4,40,640]{2,1,0:T(8,128)(2,1)}, u32[]{:S(2)}, u32[]{:S(2)}) collective-permute-start(bf16[4,40,640]{2,1,0:T(8,128)(2,1)} %get-tuple-element.112), channel_id=1, source_target_pairs={{0,16},{4,20},{8,24},{12,28},{16,0},{20,4},{24,8},{28,12},{1,17},{... | collective-permute-start | bytes 614408 | tf_op jit(solution)/shard_map/ppermute | solution.py:17
  102.0 5.2 %small_sums.1 = f32[56,128]{1,0:T(8,128)} custom-call(s32[10]{0:T(128)} %stack.40.me_ref.info_ref, f32[2,512,1280]{2,1,0:T(8,128)} %get-tuple-element.113.surrogate_ref, f32[10,128]{1,0:T(8,128)} %bitcast.78, f32[384,512]{1,0:T(8,128)} %get-tuple-element.86.early_ref, f32[384,128]{1,0:T(8,128)} %get-tuple-element.87.early_tsum_ref, ...), custom_call_target="tpu_custom_call" | custom-call | flops 5368709120 | bytes 10485760 | tf_op jit(solution)/shard_map/small_sums/pallas_call | solution.py:258
  107.2 3.0 %collective-permute-done.16.refs_2_ = bf16[4,40,640]{2,1,0:T(8,128)(2,1)S(1)} collective-permute-done((bf16[4,40,640]{2,1,0:T(8,128)(2,1)}, bf16[4,40,640]{2,1,0:T(8,128)(2,1)S(1)}, u32[]{:S(2)}, u32[]{:S(2)}) %collective-permute-start.16) | collective-permute-done | bytes 204832 | tf_op jit(solution)/shard_map/ppermute | solution.py:17
  110.9 2.1 %combine.6 = (f32[2,40,640]{2,1,0:T(8,128)}, bf16[2,40,640]{2,1,0:T(8,128)(2,1)}, f32[2,40,640]{2,1,0:T(8,128)}, bf16[2,40,640]{2,1,0:T(8,128)(2,1)}) custom-call(s32[10]{0:T(128)} %stack.40.me_ref.info_ref, f32[4,40,640]{2,1,0:T(8,128)} %get-tuple-element.114.refs_0_, f32[4,40,640]{2,1,0:T(8,128)} %get-tuple-element.115.refs_1_, ...), custom_call_target="tpu_custom_call" | custom-call | flops 1000 | bytes 1000 | tf_op jit(solution)/shard_map/combine/pallas_call | solution.py:375
  113.0 1.5 %collective-permute-start.21 = (bf16[2,40,640]{2,1,0:T(8,128)(2,1)}, bf16[2,40,640]{2,1,0:T(8,128)(2,1)S(1)}, u32[]{:S(2)}, u32[]{:S(2)}) collective-permute-start(bf16[2,40,640]{2,1,0:T(8,128)(2,1)} %get-tuple-element.117), channel_id=1, source_target_pairs={{0,16},{4,20},{8,24},{12,28},{16,0},{20,4},{24,8},{28,12},{1,17},{... | collective-permute-start | bytes 307208 | tf_op jit(solution)/shard_map/ppermute | solution.py:17
  114.6 1.2 collective-permute-start.22
  115.8 1.4 collective-permute-done.18
  118.8 3.1 %collective-permute-done.19 = f32[56,128]{1,0:T(8,128)S(1)} collective-permute-done((f32[56,128]{1,0:T(8,128)S(1)}, f32[56,128]{1,0:T(8,128)S(1)}, u32[]{:S(2)}, u32[]{:S(2)}) %collective-permute-start.19) | collective-permute-done | bytes 28704 | tf_op jit(solution)/shard_map/ppermute | solution.py:17
  121.8 3.0 %collective-permute-start.20 = (f32[56,128]{1,0:T(8,128)S(1)}, f32[56,128]{1,0:T(8,128)S(1)}, u32[]{:S(2)}, u32[]{:S(2)}) collective-permute-start(f32[56,128]{1,0:T(8,128)S(1)} %add.64), channel_id=1, source_target_pairs={{0,8},{4,12},{8,0},{12,4},{16,24},{20,28},{24,16},{28,20},{1,9},{5... | collective-permute-start | bytes 86024 | tf_op jit(solution)/shard_map/ppermute | solution.py:17
  124.8 1.8 %collective-permute-done.20 = f32[56,128]{1,0:T(8,128)S(1)} collective-permute-done((f32[56,128]{1,0:T(8,128)S(1)}, f32[56,128]{1,0:T(8,128)S(1)}, u32[]{:S(2)}, u32[]{:S(2)}) %collective-permute-start.20) | collective-permute-done | bytes 28704 | tf_op jit(solution)/shard_map/ppermute | solution.py:17
  127.4 1.9 %combine.7 = (f32[1,40,1280]{2,1,0:T(8,128)}, bf16[1,40,1280]{2,1,0:T(8,128)(2,1)}) custom-call(s32[10]{0:T(128)} %stack.40.me_ref.info_ref, f32[2,40,640]{2,1,0:T(8,128)} %get-tuple-element.120.refs_0_, f32[2,40,640]{2,1,0:T(8,128)} %get-tuple-element.121.refs_1_, bf16[2,40,640]{2,1,0:T(8,128)(2,1)} %copy-done.10, bf16[2,40,640]{2,1,0:T(8,128)(2,1)} %copy-done.11), custom_call_target="tpu_custom_call" | custom-call | flops 1000 | bytes 1000 | tf_op jit(solution)/shard_map/combine/pallas_call | solution.py:375
  129.9 1.8 %collective-permute-start.23 = (f32[56,128]{1,0:T(8,128)S(1)}, f32[56,128]{1,0:T(8,128)S(1)}, u32[]{:S(2)}, u32[]{:S(2)}) collective-permute-start(f32[56,128]{1,0:T(8,128)S(1)} %add.65), channel_id=1, source_target_pairs={{0,16},{4,20},{8,24},{12,28},{16,0},{20,4},{24,8},{28,12},{1,17},{... | collective-permute-start | bytes 86024 | tf_op jit(solution)/shard_map/ppermute | solution.py:17
  131.8 3.3 %place.2 = bf16[8,128,1280]{2,1,0:T(8,128)(2,1)} custom-call(s32[10]{0:T(128)} %stack.40.me_ref.info_ref, bf16[8,32,1280]{2,1,0:T(8,128)(2,1)} %bitcast.71, bf16[8,32,1280]{2,1,0:T(8,128)(2,1)} %collective-permute-done.10.refs_1_, bf16[8,32,1280]{2,1,0:T(8,128)(2,1)} %collective-permute-done.11.refs_2_, bf16[8,32,1280]{2,1,0:T(8,128)(2,1)} %collective-permute-done.12.refs_3_), custom_call_target="tpu_custom_call" | custom-call | flops 1000 | bytes 1000 | tf_op jit(solution)/shard_map/place/pallas_call | solution.py:312
  135.1 1.6 %collective-permute-start.27 = (f32[56,128]{1,0:T(8,128)S(1)}, f32[56,128]{1,0:T(8,128)S(1)}, u32[]{:S(2)}, u32[]{:S(2)}) collective-permute-start(f32[56,128]{1,0:T(8,128)S(1)} %add.66.refs_0_), channel_id=1, source_target_pairs={{0,2},{1,3},{2,0},{3,1},{4,6},{5,7},{6,4},{7,5},{8,10},{9,11},{10,... | collective-permute-start | bytes 86024 | tf_op jit(solution)/shard_map/ppermute | solution.py:17
  136.7 3.3 %place.3 = bf16[8,128,1280]{2,1,0:T(8,128)(2,1)} custom-call(s32[10]{0:T(128)} %stack.40.me_ref.info_ref, bf16[8,32,1280]{2,1,0:T(8,128)(2,1)} %get-tuple-element.126.refs_0_, bf16[8,32,1280]{2,1,0:T(8,128)(2,1)} %collective-permute-done.15.refs_1_, bf16[8,32,1280]{2,1,0:T(8,128)(2,1)} %collective-permute-done.24.refs_2_, ...), custom_call_target="tpu_custom_call" | custom-call | flops 1000 | bytes 1000 | tf_op jit(solution)/shard_map/place/pallas_call | solution.py:312
  140.7 1.7 %final.1 = (bf16[40,1280]{1,0:T(8,128)(2,1)}, f32[32,32]{1,0:T(8,128)}, f32[1,32]{1,0:T(1,128)}, f32[10,128]{1,0:T(8,128)}) custom-call(f32[40,1280]{1,0:T(8,128)} %bitcast.76, bf16[40,1280]{1,0:T(8,128)(2,1)} %bitcast.77, f32[56,128]{1,0:T(8,128)} %copy-done.8, f32[56,128]{1,0:T(8,128)} %copy-done.12), custom_call_target="tpu_custom_call" | custom-call | flops 1000 | bytes 1000 | tf_op jit(solution)/shard_map/final/pallas_call | solution.py:400
  (71 shorter events, 10.7 us)
Async XLA Ops:
  0.6 16.4 %copy-start = (bf16[1280,1280]{1,0:T(8,128)(2,1)S(1)}, bf16[1280,1280]{1,0:T(8,128)(2,1)}, u32[]{:S(2)}) copy-start(bf16[1280,1280]{1,0:T(8,128)(2,1)} %param.9) | copy-start | bytes 9830404
  2.8 32.4 %collective-permute-start.2 = (bf16[8,32,1280]{2,1,0:T(8,128)(2,1)}, bf16[8,32,1280]{2,1,0:T(8,128)(2,1)}, u32[]{:S(2)}, u32[]{:S(2)}) collective-permute-start(bf16[8,32,1280]{2,1,0:T(8,128)(2,1)} %dynamic-slice_bitcast_fusion), channel_id=1, source_target_pairs={{0,2},{1,3},{2,0},{3,1},{4,6},{5,7},{6,4},{7,5},{8,10},{9,11},{10,... | collective-permute-start | bytes 1966088 | tf_op jit(solution)/shard_map/ppermute | solution.py:17
  7.7 27.5 %collective-permute-start.3 = (bf16[8,32,1280]{2,1,0:T(8,128)(2,1)}, bf16[8,32,1280]{2,1,0:T(8,128)(2,1)}, u32[]{:S(2)}, u32[]{:S(2)}) collective-permute-start(bf16[8,32,1280]{2,1,0:T(8,128)(2,1)} %constant_dynamic-slice_fusion.6), channel_id=1, source_target_pairs={{0,3},{1,2},{2,1},{3,0},{4,7},{5,6},{6,5},{7,4},{8,11},{9,10},{10,... | collective-permute-start | bytes 1966088 | tf_op jit(solution)/shard_map/ppermute | solution.py:17
  7.7 4.2 %copy-start.1 = (bf16[1,8,128,1280]{3,2,1,0:T(8,128)(2,1)S(1)}, bf16[1,8,128,1280]{3,2,1,0:T(8,128)(2,1)}, u32[]{:S(2)}) copy-start(bf16[1,8,128,1280]{3,2,1,0:T(8,128)(2,1)} %param.11) | copy-start | bytes 7864324
  9.8 18.2 %collective-permute-start.1 = (bf16[8,32,1280]{2,1,0:T(8,128)(2,1)}, bf16[8,32,1280]{2,1,0:T(8,128)(2,1)}, u32[]{:S(2)}, u32[]{:S(2)}) collective-permute-start(bf16[8,32,1280]{2,1,0:T(8,128)(2,1)} %constant_dynamic-slice_fusion.5), channel_id=1, source_target_pairs={{0,1},{1,0},{2,3},{3,2},{4,5},{5,4},{6,7},{7,6},{8,9},{9,8},{10,11... | collective-permute-start | bytes 1966088 | tf_op jit(solution)/shard_map/ppermute | solution.py:17
  12.8 39.8 %collective-permute-start.5 = (bf16[8,32,1280]{2,1,0:T(8,128)(2,1)}, bf16[8,32,1280]{2,1,0:T(8,128)(2,1)}, u32[]{:S(2)}, u32[]{:S(2)}) collective-permute-start(bf16[8,32,1280]{2,1,0:T(8,128)(2,1)} %constant_dynamic-slice_fusion.3), channel_id=1, source_target_pairs={{0,3},{1,2},{2,1},{3,0},{4,7},{5,6},{6,5},{7,4},{8,11},{9,10},{10,... | collective-permute-start | bytes 1966088 | tf_op jit(solution)/shard_map/ppermute | solution.py:17
  15.4 9.6 %collective-permute-start = (bf16[8,32,1280]{2,1,0:T(8,128)(2,1)}, bf16[8,32,1280]{2,1,0:T(8,128)(2,1)}, u32[]{:S(2)}, u32[]{:S(2)}) collective-permute-start(bf16[8,32,1280]{2,1,0:T(8,128)(2,1)} %constant_dynamic-slice_fusion.2), channel_id=1, source_target_pairs={{0,1},{1,0},{2,3},{3,2},{4,5},{5,4},{6,7},{7,6},{8,9},{9,8},{10,11... | collective-permute-start | bytes 1966088 | tf_op jit(solution)/shard_map/ppermute | solution.py:17
  17.0 2.0 %copy-start.3 = (bf16[8,32,1280]{2,1,0:T(8,128)(2,1)}, bf16[8,32,1280]{2,1,0:T(8,128)(2,1)S(1)}, u32[]{:S(2)}) copy-start(bf16[8,32,1280]{2,1,0:T(8,128)(2,1)S(1)} %constant_dynamic-slice_fusion.1.refs_4_) | copy-start | bytes 1966084
  17.0 2.0 %copy-start.2 = (bf16[1,8,128,1280]{3,2,1,0:T(8,128)(2,1)S(1)}, bf16[1,8,128,1280]{3,2,1,0:T(8,128)(2,1)}, u32[]{:S(2)}) copy-start(bf16[1,8,128,1280]{3,2,1,0:T(8,128)(2,1)} %param.11) | copy-start | bytes 7864324
  24.9 38.8 %collective-permute-start.4 = (bf16[8,32,1280]{2,1,0:T(8,128)(2,1)}, bf16[8,32,1280]{2,1,0:T(8,128)(2,1)}, u32[]{:S(2)}, u32[]{:S(2)}) collective-permute-start(bf16[8,32,1280]{2,1,0:T(8,128)(2,1)} %constant_dynamic-slice_fusion.4), channel_id=1, source_target_pairs={{0,2},{1,3},{2,0},{3,1},{4,6},{5,7},{6,4},{7,5},{8,10},{9,11},{10,... | collective-permute-start | bytes 1966088 | tf_op jit(solution)/shard_map/ppermute | solution.py:17
  28.0 13.7 %copy-start.13 = (f32[1280]{0:T(1024)S(1)}, f32[1280]{0:T(1024)}, u32[]{:S(2)}) copy-start(f32[1280]{0:T(1024)} %param.10) | copy-start | bytes 15364
  41.7 3.0 %copy-start.6 = (bf16[8,32,1280]{2,1,0:T(8,128)(2,1)S(1)}, bf16[8,32,1280]{2,1,0:T(8,128)(2,1)}, u32[]{:S(2)}) copy-start(bf16[8,32,1280]{2,1,0:T(8,128)(2,1)} %get-tuple-element.81.refs_2_) | copy-start | bytes 1966084
  44.7 4.1 %copy-start.5 = (bf16[8,32,1280]{2,1,0:T(8,128)(2,1)S(1)}, bf16[8,32,1280]{2,1,0:T(8,128)(2,1)}, u32[]{:S(2)}) copy-start(bf16[8,32,1280]{2,1,0:T(8,128)(2,1)} %get-tuple-element.80.refs_1_) | copy-start | bytes 1966084
  46.6 38.7 %collective-permute-start.12 = (bf16[8,32,1280]{2,1,0:T(8,128)(2,1)}, bf16[8,32,1280]{2,1,0:T(8,128)(2,1)}, u32[]{:S(2)}, u32[]{:S(2)}) collective-permute-start(bf16[8,32,1280]{2,1,0:T(8,128)(2,1)} %bitcast.24), channel_id=1, source_target_pairs={{0,3},{1,2},{2,1},{3,0},{4,7},{5,6},{6,5},{7,4},{8,11},{9,10},{10,... | collective-permute-start | bytes 1966088 | tf_op jit(solution)/shard_map/ppermute | solution.py:17
  48.8 1.9 %copy-start.4 = (bf16[8,32,1280]{2,1,0:T(8,128)(2,1)S(1)}, bf16[8,32,1280]{2,1,0:T(8,128)(2,1)}, u32[]{:S(2)}) copy-start(bf16[8,32,1280]{2,1,0:T(8,128)(2,1)} %get-tuple-element.79.refs_0_) | copy-start | bytes 1966084
  73.3 2.2 %collective-permute-start.8 = (bf16[8,40,640]{2,1,0:T(8,128)(2,1)}, bf16[8,40,640]{2,1,0:T(8,128)(2,1)}, u32[]{:S(2)}, u32[]{:S(2)}) collective-permute-start(bf16[8,40,640]{2,1,0:T(8,128)(2,1)} %get-tuple-element.96), channel_id=1, source_target_pairs={{0,1},{1,0},{2,3},{3,2},{4,5},{5,4},{6,7},{7,6},{8,9},{9,8},{10,11... | collective-permute-start | bytes 1228808 | tf_op jit(solution)/shard_map/ppermute | solution.py:17
  73.4 2.7 %collective-permute-start.9 = (bf16[8,40,640]{2,1,0:T(8,128)(2,1)}, bf16[8,40,640]{2,1,0:T(8,128)(2,1)}, u32[]{:S(2)}, u32[]{:S(2)}) collective-permute-start(bf16[8,40,640]{2,1,0:T(8,128)(2,1)} %get-tuple-element.98), channel_id=1, source_target_pairs={{0,1},{1,0},{2,3},{3,2},{4,5},{5,4},{6,7},{7,6},{8,9},{9,8},{10,11... | collective-permute-start | bytes 1228808 | tf_op jit(solution)/shard_map/ppermute | solution.py:17
  73.9 4.2 %collective-permute-start.7 = (bf16[8,40,640]{2,1,0:T(8,128)(2,1)}, bf16[8,40,640]{2,1,0:T(8,128)(2,1)}, u32[]{:S(2)}, u32[]{:S(2)}) collective-permute-start(bf16[8,40,640]{2,1,0:T(8,128)(2,1)} %get-tuple-element.95), channel_id=1, source_target_pairs={{0,1},{1,0},{2,3},{3,2},{4,5},{5,4},{6,7},{7,6},{8,9},{9,8},{10,11... | collective-permute-start | bytes 1228808 | tf_op jit(solution)/shard_map/ppermute | solution.py:17
  74.0 4.2 %collective-permute-start.6 = (bf16[8,40,640]{2,1,0:T(8,128)(2,1)}, bf16[8,40,640]{2,1,0:T(8,128)(2,1)}, u32[]{:S(2)}, u32[]{:S(2)}) collective-permute-start(bf16[8,40,640]{2,1,0:T(8,128)(2,1)} %get-tuple-element.93), channel_id=1, source_target_pairs={{0,1},{1,0},{2,3},{3,2},{4,5},{5,4},{6,7},{7,6},{8,9},{9,8},{10,11... | collective-permute-start | bytes 1228808 | tf_op jit(solution)/shard_map/ppermute | solution.py:17
  75.5 18.1 %collective-permute-start.10 = (bf16[8,32,1280]{2,1,0:T(8,128)(2,1)}, bf16[8,32,1280]{2,1,0:T(8,128)(2,1)}, u32[]{:S(2)}, u32[]{:S(2)}) collective-permute-start(bf16[8,32,1280]{2,1,0:T(8,128)(2,1)} %bitcast.81), channel_id=1, source_target_pairs={{0,1},{1,0},{2,3},{3,2},{4,5},{5,4},{6,7},{7,6},{8,9},{9,8},{10,11... | collective-permute-start | bytes 1966088 | tf_op jit(solution)/shard_map/ppermute | solution.py:17
  76.1 18.8 %collective-permute-start.11 = (bf16[8,32,1280]{2,1,0:T(8,128)(2,1)}, bf16[8,32,1280]{2,1,0:T(8,128)(2,1)}, u32[]{:S(2)}, u32[]{:S(2)}) collective-permute-start(bf16[8,32,1280]{2,1,0:T(8,128)(2,1)} %bitcast.80), channel_id=1, source_target_pairs={{0,2},{1,3},{2,0},{3,1},{4,6},{5,7},{6,4},{7,5},{8,10},{9,11},{10,... | collective-permute-start | bytes 1966088 | tf_op jit(solution)/shard_map/ppermute | solution.py:17
  82.2 13.3 %collective-permute-start.13 = (bf16[8,40,640]{2,1,0:T(8,128)(2,1)}, bf16[8,40,640]{2,1,0:T(8,128)(2,1)}, u32[]{:S(2)}, u32[]{:S(2)}) collective-permute-start(bf16[8,40,640]{2,1,0:T(8,128)(2,1)} %get-tuple-element.101), channel_id=1, source_target_pairs={{0,4},{4,0},{8,12},{12,8},{16,20},{20,16},{24,28},{28,24},{1,5},{5... | collective-permute-start | bytes 1228808 | tf_op jit(solution)/shard_map/ppermute | solution.py:17
  83.7 11.7 %collective-permute-start.14 = (bf16[8,40,640]{2,1,0:T(8,128)(2,1)}, bf16[8,40,640]{2,1,0:T(8,128)(2,1)}, u32[]{:S(2)}, u32[]{:S(2)}) collective-permute-start(bf16[8,40,640]{2,1,0:T(8,128)(2,1)} %get-tuple-element.102), channel_id=1, source_target_pairs={{0,8},{4,12},{8,0},{12,4},{16,24},{20,28},{24,16},{28,20},{1,9},{5... | collective-permute-start | bytes 1228808 | tf_op jit(solution)/shard_map/ppermute | solution.py:17
  93.6 13.6 %collective-permute-start.15 = (bf16[8,32,1280]{2,1,0:T(8,128)(2,1)}, bf16[8,32,1280]{2,1,0:T(8,128)(2,1)}, u32[]{:S(2)}, u32[]{:S(2)}) collective-permute-start(bf16[8,32,1280]{2,1,0:T(8,128)(2,1)} %get-tuple-element.105), channel_id=1, source_target_pairs={{0,1},{1,0},{2,3},{3,2},{4,5},{5,4},{6,7},{7,6},{8,9},{9,8},{10,11... | collective-permute-start | bytes 1966088 | tf_op jit(solution)/shard_map/ppermute | solution.py:17
  93.6 43.1 %collective-permute-start.24 = (bf16[8,32,1280]{2,1,0:T(8,128)(2,1)}, bf16[8,32,1280]{2,1,0:T(8,128)(2,1)}, u32[]{:S(2)}, u32[]{:S(2)}) collective-permute-start(bf16[8,32,1280]{2,1,0:T(8,128)(2,1)} %get-tuple-element.106), channel_id=1, source_target_pairs={{0,2},{1,3},{2,0},{3,1},{4,6},{5,7},{6,4},{7,5},{8,10},{9,11},{10,... | collective-permute-start | bytes 1966088 | tf_op jit(solution)/shard_map/ppermute | solution.py:17
  94.8 41.8 %collective-permute-start.25 = (bf16[8,32,1280]{2,1,0:T(8,128)(2,1)}, bf16[8,32,1280]{2,1,0:T(8,128)(2,1)}, u32[]{:S(2)}, u32[]{:S(2)}) collective-permute-start(bf16[8,32,1280]{2,1,0:T(8,128)(2,1)} %get-tuple-element.107), channel_id=1, source_target_pairs={{0,3},{1,2},{2,1},{3,0},{4,7},{5,6},{6,5},{7,4},{8,11},{9,10},{10,... | collective-permute-start | bytes 1966088 | tf_op jit(solution)/shard_map/ppermute | solution.py:17
  98.3 11.9 %collective-permute-start.16 = (bf16[4,40,640]{2,1,0:T(8,128)(2,1)}, bf16[4,40,640]{2,1,0:T(8,128)(2,1)S(1)}, u32[]{:S(2)}, u32[]{:S(2)}) collective-permute-start(bf16[4,40,640]{2,1,0:T(8,128)(2,1)} %get-tuple-element.111), channel_id=1, source_target_pairs={{0,8},{4,12},{8,0},{12,4},{16,24},{20,28},{24,16},{28,20},{1,9},{5... | collective-permute-start | bytes 614408 | tf_op jit(solution)/shard_map/ppermute | solution.py:17
  99.4 10.8 %collective-permute-start.17 = (bf16[4,40,640]{2,1,0:T(8,128)(2,1)}, bf16[4,40,640]{2,1,0:T(8,128)(2,1)}, u32[]{:S(2)}, u32[]{:S(2)}) collective-permute-start(bf16[4,40,640]{2,1,0:T(8,128)(2,1)} %get-tuple-element.112), channel_id=1, source_target_pairs={{0,16},{4,20},{8,24},{12,28},{16,0},{20,4},{24,8},{28,12},{1,17},{... | collective-permute-start | bytes 614408 | tf_op jit(solution)/shard_map/ppermute | solution.py:17
  110.2 0.7 copy-start.7
  113.0 13.7 %collective-permute-start.21 = (bf16[2,40,640]{2,1,0:T(8,128)(2,1)}, bf16[2,40,640]{2,1,0:T(8,128)(2,1)S(1)}, u32[]{:S(2)}, u32[]{:S(2)}) collective-permute-start(bf16[2,40,640]{2,1,0:T(8,128)(2,1)} %get-tuple-element.117), channel_id=1, source_target_pairs={{0,16},{4,20},{8,24},{12,28},{16,0},{20,4},{24,8},{28,12},{1,17},{... | collective-permute-start | bytes 307208 | tf_op jit(solution)/shard_map/ppermute | solution.py:17
  114.6 12.1 %collective-permute-start.22 = (bf16[2,40,640]{2,1,0:T(8,128)(2,1)}, bf16[2,40,640]{2,1,0:T(8,128)(2,1)S(1)}, u32[]{:S(2)}, u32[]{:S(2)}) collective-permute-start(bf16[2,40,640]{2,1,0:T(8,128)(2,1)} %get-tuple-element.118), channel_id=1, source_target_pairs={{0,4},{4,0},{8,12},{12,8},{16,20},{20,16},{24,28},{28,24},{1,5},{5... | collective-permute-start | bytes 307208 | tf_op jit(solution)/shard_map/ppermute | solution.py:17
  115.8 1.4 collective-permute-start.18
  118.0 3.9 %collective-permute-start.19 = (f32[56,128]{1,0:T(8,128)S(1)}, f32[56,128]{1,0:T(8,128)S(1)}, u32[]{:S(2)}, u32[]{:S(2)}) collective-permute-start(f32[56,128]{1,0:T(8,128)S(1)} %add.63), channel_id=1, source_target_pairs={{0,4},{4,0},{8,12},{12,8},{16,20},{20,16},{24,28},{28,24},{1,5},{5... | collective-permute-start | bytes 86024 | tf_op jit(solution)/shard_map/ppermute | solution.py:17
  121.8 4.8 %collective-permute-start.20 = (f32[56,128]{1,0:T(8,128)S(1)}, f32[56,128]{1,0:T(8,128)S(1)}, u32[]{:S(2)}, u32[]{:S(2)}) collective-permute-start(f32[56,128]{1,0:T(8,128)S(1)} %add.64), channel_id=1, source_target_pairs={{0,8},{4,12},{8,0},{12,4},{16,24},{20,28},{24,16},{28,20},{1,9},{5... | collective-permute-start | bytes 86024 | tf_op jit(solution)/shard_map/ppermute | solution.py:17
  126.7 0.6 copy-start.10
  126.7 0.7 copy-start.11
  129.3 10.7 %collective-permute-start.26 = (bf16[1,40,1280]{2,1,0:T(8,128)(2,1)}, bf16[1,40,1280]{2,1,0:T(8,128)(2,1)S(1)}, u32[]{:S(2)}, u32[]{:S(2)}) collective-permute-start(bf16[1,40,1280]{2,1,0:T(8,128)(2,1)} %get-tuple-element.122), channel_id=1, source_target_pairs={{0,2},{1,3},{2,0},{3,1},{4,6},{5,7},{6,4},{7,5},{8,10},{9,11},{10,... | collective-permute-start | bytes 307208 | tf_op jit(solution)/shard_map/ppermute | solution.py:17
  129.9 5.1 %collective-permute-start.23 = (f32[56,128]{1,0:T(8,128)S(1)}, f32[56,128]{1,0:T(8,128)S(1)}, u32[]{:S(2)}, u32[]{:S(2)}) collective-permute-start(f32[56,128]{1,0:T(8,128)S(1)} %add.65), channel_id=1, source_target_pairs={{0,16},{4,20},{8,24},{12,28},{16,0},{20,4},{24,8},{28,12},{1,17},{... | collective-permute-start | bytes 86024 | tf_op jit(solution)/shard_map/ppermute | solution.py:17
  135.1 4.9 %copy-start.8 = (f32[56,128]{1,0:T(8,128)}, f32[56,128]{1,0:T(8,128)S(1)}, u32[]{:S(2)}) copy-start(f32[56,128]{1,0:T(8,128)S(1)} %add.66.refs_0_) | copy-start | bytes 86020
  135.1 4.9 %collective-permute-start.27 = (f32[56,128]{1,0:T(8,128)S(1)}, f32[56,128]{1,0:T(8,128)S(1)}, u32[]{:S(2)}, u32[]{:S(2)}) collective-permute-start(f32[56,128]{1,0:T(8,128)S(1)} %add.66.refs_0_), channel_id=1, source_target_pairs={{0,2},{1,3},{2,0},{3,1},{4,6},{5,7},{6,4},{7,5},{8,10},{9,11},{10,... | collective-permute-start | bytes 86024 | tf_op jit(solution)/shard_map/ppermute | solution.py:17
  140.0 0.6 copy-start.12
  140.0 0.6 copy-start.9

commit v4 on v3

--- a/solution.py
+++ b/solution.py
@@ -179,43 +179,50 @@
     cross_ref[...] += cross[:every] + cross[every:]
 
 
-def early_kernel(parts, surrogate_ref, *refs):
+def packed(pick, ours, cross, tsum, out_rows):
+    total = pick.shape[1]
+    one = jnp.where(pick, 1.0, 0.0)
+    left = ours(one)
+    exact = functools.partial(
+        lax.dot_general, precision=lax.Precision.HIGHEST, preferred_element_type=jnp.float32
+    )
+    low = lambda dim: jnp.bitwise_and(iota2(cross.shape, dim), GROUP - 1)
+    narrow = exact(jnp.where(low(0) == low(1), cross, 0.0), one, (((1,), (0,)), ((), ())))
+    weights = exact(left, narrow, (((0,), (0,)), ((), ())))
+    row_sum = -jnp.sum(tsum, axis=1, keepdims=True)
+    thresholds = jnp.broadcast_to(jnp.sum(left * row_sum, axis=0, keepdims=True), (8, total))
+    found = jnp.concatenate([weights, thresholds], axis=0)
+    found = jnp.concatenate([found, jnp.zeros((total + 8, 128 - total), jnp.float32)], axis=1)
+    return jnp.concatenate([found, jnp.zeros((out_rows - total - 8, 128), jnp.float32)], axis=0)
+
+
+def early_kernel(parts, info_ref, surrogate_ref, bias_ref, *refs):
     sources, grads, rest = refs[:parts], refs[parts : 2 * parts - 1], refs[2 * parts - 1 :]
-    rows = sources[0].shape[0] * sources[0].shape[1]
-
-    def surrogate(at, tile):
-        value = surrogate_ref[0, :, at : at + tile]
-        return jnp.concatenate([value[: 2 * rows], value[3 * rows :]], axis=0)
-
-    cross_of(grads, surrogate, sources, *rest)
-
-
-def early_sums(surrogate, sources, grads):
-    parts = len(sources)
-    steps, share, width = sources[0].shape
+    out_ref, cross_ref, tsum_ref, both_ref = rest
+    steps = sources[0].shape[0]
     rows = steps * GROUP
-    every = (parts - 1) * rows
-    piece = pl.BlockSpec((steps, GROUP, width), lambda g: (0, g, 0))
-    fixed = lambda shape: pl.BlockSpec(shape, lambda g: (0, 0))
-    return pl.pallas_call(
-        functools.partial(early_kernel, parts),
-        grid=(share // GROUP,),
-        in_specs=[pl.BlockSpec((1, parts * rows, width), lambda g: (g, 0, 0))]
-        + [piece] * (2 * parts - 1),
-        out_specs=[fixed((every, parts * rows)), fixed((every, 128))],
-        out_shape=[
-            jax.ShapeDtypeStruct((every, parts * rows), jnp.float32),
-            jax.ShapeDtypeStruct((every, 128), jnp.float32),
-        ],
-        scratch_shapes=[pltpu.VMEM((2 * every, width), jnp.bfloat16)],
-        cost_estimate=SMALL,
-        name="early_sums",
-    )(surrogate, *sources, *grads)
-
-
-def sums_kernel(parts, info_ref, surrogate_ref, bias_ref, early_ref, early_tsum_ref, *refs):
+    others = lambda value: jnp.concatenate([value[: 2 * rows], value[3 * rows :]], axis=0)
+    cross_of(
+        grads,
+        lambda at, tile: others(surrogate_ref[0, :, at : at + tile]),
+        sources,
+        cross_ref,
+        tsum_ref,
+        both_ref,
+    )
+
+    @pl.when(pl.program_id(0) == pl.num_programs(0) - 1)
+    def _():
+        pick = selector(info_ref[0], parts, steps)
+        out_ref[...] = packed(pick, others, cross_ref[...], tsum_ref[...], out_ref.shape[0])
+        first = pick.shape[1] + 8
+        out_ref[first : first + bias_ref.shape[0], :] = bias_ref[...]
+
+
+def late_kernel(parts, info_ref, surrogate_ref, early_ref, *refs):
     sources, (grad_ref, out_ref, cross_ref, tsum_ref, both_ref) = refs[:parts], refs[parts:]
-    steps, group, _ = grad_ref.shape
+    steps = grad_ref.shape[0]
+    rows = steps * GROUP
     cross_of(
         [grad_ref],
         lambda at, tile: surrogate_ref[0, :, at : at + tile],
@@ -227,59 +234,49 @@
 
     @pl.when(pl.program_id(0) == pl.num_programs(0) - 1)
     def _():
-        before = 2 * steps * group
-        whole = lambda early, late: jnp.concatenate(
-            [early[:before], late[...], early[before:]], axis=0
+        pick = selector(info_ref[0], parts, steps)
+        out_ref[...] = early_ref[...] + packed(
+            pick,
+            lambda value: value[2 * rows : 3 * rows],
+            cross_ref[...],
+            tsum_ref[...],
+            out_ref.shape[0],
         )
-        pick = selector(info_ref[0], parts, steps)
-        rows, total = pick.shape
-        one = jnp.where(pick, 1.0, 0.0)
-        exact = functools.partial(
-            lax.dot_general, precision=lax.Precision.HIGHEST, preferred_element_type=jnp.float32
-        )
-        cross = jnp.where(same_token(rows), whole(early_ref, cross_ref), 0.0)
-        narrow = exact(cross, one, (((1,), (0,)), ((), ())))
-        row_sum = -jnp.sum(whole(early_tsum_ref, tsum_ref), axis=1, keepdims=True)
-        out_ref[...] = jnp.zeros_like(out_ref)
-        out_ref[:total, :total] = exact(one, narrow, (((0,), (0,)), ((), ())))
-        out_ref[total : total + 8, :total] = jnp.broadcast_to(
-            jnp.sum(one * row_sum, axis=0, keepdims=True), (8, total)
-        )
-        out_ref[total + 8 : total + 8 + bias_ref.shape[0], :] = bias_ref[...]
-
-
-def small_sums(info, surrogate, bias_rows, early, sources, grad):
+
+
+def small_sums(info, surrogate, extra, sources, grads):
     parts = len(sources)
     steps, share, width = sources[0].shape
     rows = steps * GROUP
+    late = len(grads) == 1
+    every = len(grads) * rows
     piece = pl.BlockSpec((steps, GROUP, width), lambda g: (0, g, 0))
     fixed = lambda shape: pl.BlockSpec(shape, lambda g: (0, 0))
-    out_rows = parts * steps + 8 + -(-bias_rows.shape[0] // 8) * 8
+    out_rows = extra.shape[0] if late else parts * steps + 8 + -(-extra.shape[0] // 8) * 8
+    if late:
+        some = pl.BlockSpec((1, rows, width), lambda g: (g, 2, 0))
+        cost = pl.CostEstimate(
+            flops=8 * parts * parts * rows * rows * width * (share // GROUP),
+            bytes_accessed=8 * parts * rows * width * (share // GROUP),
+            transcendentals=0,
+        )
+    else:
+        some = pl.BlockSpec((1, parts * rows, width), lambda g: (g, 0, 0))
+        cost = SMALL
     return pl.pallas_call(
-        functools.partial(sums_kernel, parts),
+        functools.partial(late_kernel if late else early_kernel, parts),
         grid=(share // GROUP,),
-        in_specs=[
-            SMEM,
-            pl.BlockSpec((1, rows, width), lambda g: (g, 2, 0)),
-            fixed(bias_rows.shape),
-            fixed(early[0].shape),
-            fixed(early[1].shape),
-        ]
-        + [piece] * (parts + 1),
+        in_specs=[SMEM, some, fixed(extra.shape)] + [piece] * (parts + len(grads)),
         out_specs=fixed((out_rows, 128)),
         out_shape=jax.ShapeDtypeStruct((out_rows, 128), jnp.float32),
         scratch_shapes=[
-            pltpu.VMEM((rows, parts * rows), jnp.float32),
-            pltpu.VMEM((rows, 128), jnp.float32),
-            pltpu.VMEM((2 * rows, width), jnp.bfloat16),
+            pltpu.VMEM((every, parts * rows), jnp.float32),
+            pltpu.VMEM((every, 128), jnp.float32),
+            pltpu.VMEM((2 * every, width), jnp.bfloat16),
         ],
-        cost_estimate=pl.CostEstimate(
-            flops=8 * parts * parts * rows * rows * width * (share // GROUP),
-            bytes_accessed=8 * parts * rows * width * (share // GROUP),
-            transcendentals=0,
-        ),
-        name="small_sums",
-    )(info, surrogate, bias_rows, *early, *sources, grad)
+        cost_estimate=cost,
+        name="late_sums" if late else "early_sums",
+    )(info, surrogate, extra, *sources, *grads)
 
 
 HBM = pl.BlockSpec(memory_space=pl.ANY)
@@ -413,33 +410,27 @@
 
 
 def weight_kernel(shard, parts, info_ref, *refs):
-    spikes, cots, outs = refs[:parts], refs[parts : 2 * parts], refs[2 * parts :]
-    part = lax.dot_general(
-        rows_of(spikes, 0, spikes[0].shape[-1]),
-        rows_of(cots, 0, cots[0].shape[-1]),
-        (((0,), (0,)), ((), ())),
-        preferred_element_type=jnp.float32,
-    )
+    spikes, cots, outs = refs[:parts], refs[parts : 2 * parts], refs[2 * parts : -1]
+    part_ref = refs[-1]
+    half = part_ref.shape[2]
     core = jnp.bitwise_and(info_ref[0], 1)
+    turned = rows_of(spikes, 0, spikes[0].shape[-1]).T
+    for side in range(2):
+        part_ref[side] = jnp.dot(
+            turned, rows_of(cots, side * half, half), preferred_element_type=jnp.float32
+        )
+    count = part_ref.shape[1] // shard // 2
     step = pl.program_id(0)
-    pieces = [part[at : at + shard] for at in range(0, part.shape[0], shard)]
     for side in range(2):
-        for mine in range(2):
-
-            @pl.when((core == mine) & (step // 2 == side))
-            def _():
-                for k, piece in enumerate(pieces):
-                    if k % 2 == mine:
-                        outs[side][k // 2] = piece
-
-    for at in range(4):
-        for mine in range(2):
-
-            @pl.when((core == mine) & (step == at))
-            def _():
-                for k, piece in enumerate(pieces):
-                    if k % 2 != mine:
-                        outs[2 + at][k // 2] = piece.astype(jnp.bfloat16)
+        for n in range(count):
+            at = lambda odd: pl.ds(pl.multiple_of((2 * n + odd) * shard, 8), shard)
+            outs[side][n] = part_ref[side, at(core), :]
+            send = part_ref[side, at(1 - core), :].astype(jnp.bfloat16)
+            for now in range(2):
+
+                @pl.when(step == now)
+                def _():
+                    outs[2 + 2 * side + now][n] = send
 
 
 def weight_halves(info, spikes, cots, shard):
@@ -450,16 +441,14 @@
     keep = jax.ShapeDtypeStruct((2 * count, shard, cols), jnp.float32)
     found = pl.pallas_call(
         functools.partial(weight_kernel, shard, len(spikes)),
-        grid=(4,),
+        grid=(2,),
         in_specs=[SMEM]
-        + [pl.BlockSpec((steps, tokens, block), lambda i: (0, 0, i % 2))] * len(spikes)
-        + [pl.BlockSpec((steps, tokens, cols), lambda i: (0, 0, i // 2))] * len(spikes),
-        out_specs=[
-            pl.BlockSpec((count, shard, cols), lambda i: (jnp.minimum(i, 1), 0, 0)),
-            pl.BlockSpec((count, shard, cols), lambda i: (jnp.maximum(i - 2, 0), 0, 0)),
-        ]
+        + [pl.BlockSpec((steps, tokens, block), lambda i: (0, 0, i))] * len(spikes)
+        + [pl.BlockSpec((steps, tokens, width), lambda i: (0, 0, 0))] * len(spikes),
+        out_specs=[pl.BlockSpec((count, shard, cols), lambda i: (i, 0, 0))] * 2
         + [pl.BlockSpec((count, shard, cols), lambda i: (0, 0, 0))] * 4,
         out_shape=[keep, keep] + [send] * 4,
+        scratch_shapes=[pltpu.VMEM((2, block, cols), jnp.float32)],
         cost_estimate=SMALL,
         name="weight_halves",
     )(info, *spikes, *cots)
@@ -516,7 +505,13 @@
     grads += [spike_grad(after(cot, *outs)) for cot in cots[3:]]
 
     others = [k for k in range(ntm) if k != 2]
-    early = early_sums(after(surrogate, *outs), currents_in, [grads[k] for k in others])
+    early = small_sums(
+        info,
+        after(surrogate, *outs),
+        bias_term.reshape(-1, 128),
+        currents_in,
+        [grads[k] for k in others],
+    )
 
     shard = width // (ndp * ntm)
     core, y = ("tm", 0), ("dp", 0)
@@ -525,7 +520,7 @@
     left = names[:-1]
 
     if shard % 8 == 0:
-        late = cots[:2] + [after(cots[2], *outs, *early)] + cots[3:]
+        late = cots[:2] + [after(cots[2], *outs, early)] + cots[3:]
         halves = weight_halves(info, spikes, late, shard)
     else:
         whole = sum(
@@ -537,7 +532,7 @@
         halves = [(keep[..., c : c + half], [send[..., c : c + half]]) for c in (0, half)]
 
     sent = halves[-1][1][0]
-    routes = ([y] + zs, zs + [y])
+    routes = ([y] + zs[:1], zs[:1] + [y])
 
     def go(value, *path):
         if all(axis == path[0][0] for axis, _ in path):
@@ -570,47 +565,45 @@
             sums = sums + go(sums, bit)
         return sums
 
-    for at in range(1, bdp):
-        gate = outs_in[1:3] + cgrads if at == 1 else [sums]
-        if at == 2:
-            gate.append(cgrads_in[1])
-        state[0] = (after(state[0][0], *gate), state[0][1])
-        bits = [route[at] for route in routes]
-        pairs, lefts = step(state, lefts, bits)
-        state = travel(pairs, bits)
-        sends = [send for _, send in pairs]
-        if at == 1:
-            sums = small_sums(
-                info,
-                after(surrogate, *sends),
-                bias_term.reshape(-1, 128),
-                early,
-                currents_in,
-                grads[2],
-            )
-            hops = [core, y] + zs
+    spots = list(map(spot, range(ntm)))
+
+    def gated(state, *gate):
+        return [(after(state[0][0], *gate), state[0][1])] + state[1:]
+
+    bits = [route[1] for route in routes]
+    pairs, lefts = step(gated(state, *outs_in[1:3], *cgrads), lefts, bits)
+    state = travel(pairs, bits)
+    sends = [send for _, send in pairs]
+    sums = small_sums(info, after(surrogate, *sends), early, currents_in, grads[2:3])
+    hops, gate = [core, y] + zs, [sums, cgrads_in[1]]
+    for bit in zs[1:]:
+        pairs, lefts = step(gated(state, *gate), lefts, [bit] * len(state), joined=len(state) > 1)
+        lefts = lefts[:1]
+        state = travel(pairs, [bit])
+        sums = after(sums, pairs[0][1])
+        if bit == zs[1]:
+            sums = meet(sums, core)
+            output = place(info, [after(outs_in[0], sums)] + outs_in[1:], spots, tokens)
+            sums = meet(after(sums, output) + go(sums, y), hops[2])
+            hops = hops[3:]
         else:
-            few = 3 if at == 2 else 1
-            sums = meet(after(sums, *sends), *hops[:few])
-            hops = hops[few:]
-    state[0] = (after(state[0][0], sums), state[0][1])
-
-    pairs, lefts = step(state, lefts, [xs[0]] * 2, joined=True)
+            sums, hops = meet(sums, hops[0]), hops[1:]
+        gate = [sums]
+
+    pairs, lefts = step(gated(state, *gate), lefts, xs[:1])
     keep, send = pairs[0]
     got = go(send, xs[0])
-    spots = list(map(spot, range(ntm)))
-    output = place(info, [after(outs_in[0], send)] + outs_in[1:], spots, tokens)
-    meeting = [after(sums, send)]
-    meeting.append(go(meeting[0], *hops))
-    sums = after(meeting[0], output) + meeting[1]
-    current_grad = place(info, [after(cgrads_in[0], sums)] + cgrads_in[1:], spots, tokens)
+    current_grad = place(info, [after(cgrads_in[0], send)] + cgrads_in[1:], spots, tokens)
     rest = lefts[0]
     for bit in xs[1:]:
         pairs, (rest,) = step([(keep, [got])], [rest], [bit])
         keep, send = pairs[0]
         got = go(send, bit)
+    hops += xs
+    sums = after(sums, send)
     sums = [sums] + [
-        go(sums, *[bit for i, bit in enumerate(xs) if n >> i & 1]) for n in range(1, 1 << len(xs))
+        go(sums, *[bit for i, bit in enumerate(hops) if n >> i & 1])
+        for n in range(1, 1 << len(hops))
     ]
     weight_grad, mixing_grad, threshold_grad, bias_grad = final(
         keep.reshape(shard, width), got.reshape(shard, width), sums, ntm * steps, width

time: 143 us -> 136 us (0.951)
  starting transfers between devices: 30 us -> 27 us
  waiting for transfers between devices: 20.4 us -> 17.5 us
    ppermute x28, starting transfers between devices: 30 us -> 27 us  [xor_permute(): return lax.ppermute(value, axis, [(i, i ^ mask) for i in range(size)])]
    ppermute x28, waiting for transfers between devices: 20.4 us -> 17.5 us  [xor_permute(): return lax.ppermute(value, axis, [(i, i ^ mask) for i in range(size)])]
  transfers between devices with their start and end apart: 28 -> 28, of which waited for: 8 -> 8; matrix products, arithmetic and copies ran while one was open for 23% -> 24% of each run, Pallas kernels for 37% -> 38%
where the time goes in v4:
time: 136 us; the launch traced here: 135 us
  Pallas kernels  53.3 us (39%)
  starting transfers between devices  27 us (20%)
  matrix products  19.5 us (14%)
  waiting for transfers between devices  17.5 us (13%)
  local copies, waits for them, and re-layouts  15.1 us (11%)
  other arithmetic  1.79 us (1%)
    ppermute x28, starting transfers between devices, xor_permute(): return lax.ppermute(value, axis, [(i, i ^ mask) for i in range(size)])  27 us
    ppermute x28, waiting for transfers between devices, xor_permute(): return lax.ppermute(value, axis, [(i, i ^ mask) for i in range(size)])  17.5 us
    dynamic_slice x8, local copies, waits for them, and re-layouts, cut(): found[k] = lax.dynamic_slice_in_dim(value, (me ^ k) * share, share, axis=1)  13.1 us
    pallas_call x2, Pallas kernels, small_sums(): pl.pallas_call(functools.partial(late_kernel if late else early_kernel, p...  10.9 us
    pallas_call x4, Pallas kernels, combine(): pl.pallas_call(functools.partial(combine_kernel, tuple(shapes), counts, l...  10.9 us
    dot_general x4, matrix products, spike_grad(): jnp.einsum('re,de->rd', flat(cot), weight, preferred_element_type=jnp.flo...  10.9 us
    pallas_call x1, Pallas kernels, weight_halves(): pl.pallas_call(functools.partial(weight_kernel, shard, len(spikes)), grid...  9.1 us
    dot_general x4, matrix products, body(): jnp.dot(flat(spikes[k]), weight, preferred_element_type=jnp.float32) + bias  8.66 us
  transfers between devices with their start and end apart: 28, of which 8 were waited for; matrix products, arithmetic and copies ran while one was open for 24% of the time, Pallas kernels for 38%

profile of v4, /device:TPU:0, one launch (start us, length us, event | category | flops | bytes accessed | tf_op | source)
XLA Modules:
  0.0 135.2 jit_solution(16526075066262602207)
XLA Ops:
  0.7 2.1 %dynamic-slice_bitcast_fusion = bf16[8,32,1280]{2,1,0:T(8,128)(2,1)} fusion(bf16[1,8,128,1280]{3,2,1,0:T(8,128)(2,1)} %param.6, s32[]{:T(128)S(6)} %select_n.16), kind=kLoop, calls=%fused_computation.13 | loop fusion | bytes 1310724 | tf_op jit(solution)/shard_map/dynamic_slice | solution.py:480
  2.8 2.9 %collective-permute-start.2 = (bf16[8,32,1280]{2,1,0:T(8,128)(2,1)}, bf16[8,32,1280]{2,1,0:T(8,128)(2,1)}, u32[]{:S(2)}, u32[]{:S(2)}) collective-permute-start(bf16[8,32,1280]{2,1,0:T(8,128)(2,1)} %dynamic-slice_bitcast_fusion), channel_id=1, source_target_pairs={{0,2},{1,3},{2,0},{3,1},{4,6},{5,7},{6,4},{7,5},{8,10},{9,11},{10,... | collective-permute-start | bytes 1966088 | tf_op jit(solution)/shard_map/ppermute | solution.py:17
  5.7 2.0 %constant_dynamic-slice_fusion.6 = bf16[8,32,1280]{2,1,0:T(8,128)(2,1)} fusion(bf16[8,128,1280]{2,1,0:T(8,128)(2,1)} %bitcast.63, s32[]{:T(128)S(6)} %select_n.17), kind=kLoop, calls=%fused_computation.20 | loop fusion | bytes 1310724 | tf_op jit(solution)/shard_map/dynamic_slice | solution.py:480
  7.7 2.1 %constant_dynamic-slice_fusion.5 = bf16[8,32,1280]{2,1,0:T(8,128)(2,1)} fusion(bf16[8,128,1280]{2,1,0:T(8,128)(2,1)} %bitcast.64, s32[]{:T(128)S(6)} %select_n.18), kind=kLoop, calls=%fused_computation.19 | loop fusion | bytes 1310724 | tf_op jit(solution)/shard_map/dynamic_slice | solution.py:480
  9.9 2.0 %constant_dynamic-slice_fusion.4 = bf16[8,32,1280]{2,1,0:T(8,128)(2,1)} fusion(bf16[8,128,1280]{2,1,0:T(8,128)(2,1)} %bitcast.53, s32[]{:T(128)S(6)} %select_n.16), kind=kLoop, calls=%fused_computation.18 | loop fusion | bytes 1310724 | tf_op jit(solution)/shard_map/dynamic_slice | solution.py:480
  12.8 1.6 %collective-permute-start.5 = (bf16[8,32,1280]{2,1,0:T(8,128)(2,1)}, bf16[8,32,1280]{2,1,0:T(8,128)(2,1)}, u32[]{:S(2)}, u32[]{:S(2)}) collective-permute-start(bf16[8,32,1280]{2,1,0:T(8,128)(2,1)} %constant_dynamic-slice_fusion.3), channel_id=1, source_target_pairs={{0,3},{1,2},{2,1},{3,0},{4,7},{5,6},{6,5},{7,4},{8,11},{9,10},{10,... | collective-permute-start | bytes 1966088 | tf_op jit(solution)/shard_map/ppermute | solution.py:17
  14.4 1.0 constant_dynamic-slice_fusion.2
  15.9 1.1 constant_dynamic-slice_fusion.1.refs_4_
  17.1 1.9 %convolution_convert_fusion.3 = bf16[256,1280]{1,0:T(8,128)(2,1)} fusion(bf16[256,1280]{1,0:T(8,128)(2,1)S(1)} %bitcast.68, bf16[1280,1280]{1,0:T(8,128)(2,1)S(1)} %copy-done), kind=kOutput, calls=%fused_computation.12 | convolution fusion | flops 839188480 | bytes 4587520 | tf_op jit(solution)/shard_map/re,de->rd/dot_general | solution.py:491
  19.0 1.0 convert_reduce_fusion
  20.6 2.3 %build_krons.1 = (bf16[512,512]{1,0:T(8,128)(2,1)}, bf16[512,512]{1,0:T(8,128)(2,1)}, f32[512,1]{1,0:T(8,128)}) custom-call(s32[10]{0:T(128)} %stack.40.me_ref.info_ref, f32[32,32]{1,0:T(8,128)} %mixing_ref.1, f32[1,32]{1,0:T(1,128)} %bitcast.79), custom_call_target="tpu_custom_call" | custom-call | tf_op jit(solution)/shard_map/build_krons/pallas_call | solution.py:60
  22.9 2.0 %constant_dynamic-slice_fusion.refs_0_ = bf16[8,32,1280]{2,1,0:T(8,128)(2,1)} fusion(bf16[8,128,1280]{2,1,0:T(8,128)(2,1)} %bitcast.65, s32[]{:T(128)S(6)} %select_n.19), kind=kLoop, calls=%fused_computation.14 | loop fusion | bytes 1310724 | tf_op jit(solution)/shard_map/dynamic_slice | solution.py:480
  25.0 3.0 %convolution_convert_fusion.2 = bf16[256,1280]{1,0:T(8,128)(2,1)} fusion(bf16[256,1280]{1,0:T(8,128)(2,1)} %bitcast.15, bf16[1280,1280]{1,0:T(8,128)(2,1)S(1)} %copy-done), kind=kOutput, calls=%fused_computation.11 | convolution fusion | flops 839188480 | bytes 4587520 | tf_op jit(solution)/shard_map/re,de->rd/dot_general | solution.py:491
  28.0 7.2 %collective-permute-done.3.refs_3_ = bf16[8,32,1280]{2,1,0:T(8,128)(2,1)} collective-permute-done((bf16[8,32,1280]{2,1,0:T(8,128)(2,1)}, bf16[8,32,1280]{2,1,0:T(8,128)(2,1)}, u32[]{:S(2)}, u32[]{:S(2)}) %collective-permute-start.3) | collective-permute-done | bytes 655392 | tf_op jit(solution)/shard_map/ppermute | solution.py:17
  35.2 6.5 %forward.1 = (bf16[8,32,1280]{2,1,0:T(8,128)(2,1)}, bf16[8,32,1280]{2,1,0:T(8,128)(2,1)}, bf16[8,32,1280]{2,1,0:T(8,128)(2,1)}, bf16[8,32,1280]{2,1,0:T(8,128)(2,1)}, f32[2,512,1280]{2,1,0:T(8,128)}) custom-call(bf16[512,512]{1,0:T(8,128)(2,1)} %get-tuple-element.65.kron_ref, f32[512,1]{1,0:T(8,128)} %get-tuple-element.73.thr_ref, ...), custom_call_target="tpu_custom_call" | custom-call | tf_op jit(solution)/shard_map/forward/pallas_call | solution.py:99
  41.7 3.0 %fusion.3 = bf16[256,1280]{1,0:T(8,128)(2,1)} fusion(bf16[256,1280]{1,0:T(8,128)(2,1)} %bitcast.75, bf16[1280,1280]{1,0:T(8,128)(2,1)S(1)} %copy-done, f32[1280]{0:T(1024)S(1)} %copy-done.14), kind=kOutput, calls=%fused_computation.8 | convolution fusion | flops 839516160 | bytes 4592640 | tf_op jit(solution)/shard_map/dot_general | solution.py:498
  44.8 1.9 %fusion.2 = bf16[256,1280]{1,0:T(8,128)(2,1)} fusion(bf16[256,1280]{1,0:T(8,128)(2,1)S(1)} %bitcast.74, bf16[1280,1280]{1,0:T(8,128)(2,1)S(1)} %copy-done, f32[1280]{0:T(1024)S(1)} %copy-done.14), kind=kOutput, calls=%fused_computation.7 | convolution fusion | flops 839516160 | bytes 4592640 | tf_op jit(solution)/shard_map/dot_general | solution.py:498
  46.6 2.2 %collective-permute-start.12 = (bf16[8,32,1280]{2,1,0:T(8,128)(2,1)}, bf16[8,32,1280]{2,1,0:T(8,128)(2,1)}, u32[]{:S(2)}, u32[]{:S(2)}) collective-permute-start(bf16[8,32,1280]{2,1,0:T(8,128)(2,1)} %bitcast.24), channel_id=1, source_target_pairs={{0,3},{1,2},{2,1},{3,0},{4,7},{5,6},{6,5},{7,4},{8,11},{9,10},{10,... | collective-permute-start | bytes 1966088 | tf_op jit(solution)/shard_map/ppermute | solution.py:17
  48.9 1.9 %fusion.1 = bf16[256,1280]{1,0:T(8,128)(2,1)} fusion(bf16[256,1280]{1,0:T(8,128)(2,1)S(1)} %bitcast.73, bf16[1280,1280]{1,0:T(8,128)(2,1)S(1)} %copy-done, f32[1280]{0:T(1024)S(1)} %copy-done.14), kind=kOutput, calls=%fused_computation.6 | convolution fusion | flops 839516160 | bytes 4592640 | tf_op jit(solution)/shard_map/dot_general | solution.py:498
  50.7 1.9 %fusion = bf16[256,1280]{1,0:T(8,128)(2,1)} fusion(bf16[256,1280]{1,0:T(8,128)(2,1)S(1)} %bitcast.72, bf16[1280,1280]{1,0:T(8,128)(2,1)S(1)} %copy-done, f32[1280]{0:T(1024)S(1)} %copy-done.14), kind=kOutput, calls=%fused_computation.5 | convolution fusion | flops 839516160 | bytes 4592640 | tf_op jit(solution)/shard_map/dot_general | solution.py:498
  52.6 3.0 %convolution_convert_fusion.1 = bf16[256,1280]{1,0:T(8,128)(2,1)} fusion(bf16[256,1280]{1,0:T(8,128)(2,1)} %bitcast.26, bf16[1280,1280]{1,0:T(8,128)(2,1)S(1)} %copy-done), kind=kOutput, calls=%fused_computation.10 | convolution fusion | flops 839188480 | bytes 4587520 | tf_op jit(solution)/shard_map/re,de->rd/dot_general | solution.py:491
  55.6 6.9 %early_sums.1.early_ref = f32[56,128]{1,0:T(8,128)} custom-call(s32[10]{0:T(128)} %stack.40.me_ref.info_ref, f32[2,512,1280]{2,1,0:T(8,128)} %get-tuple-element.106.surrogate_ref, f32[10,128]{1,0:T(8,128)} %bitcast.78, bf16[8,32,1280]{2,1,0:T(8,128)(2,1)} %constant_dynamic-slice_fusion.refs_0_, bf16[8,32,1280]{2,1,0:T(8,128)(2,1)} %collective-permute-done.1.refs_1_, ...), custom_call_target="tpu_custom_call" | custom-call | flops 1000 | bytes 1000 | tf_op jit(solution)/shard_map/early_sums/pallas_call | solution.py:266
  62.5 1.3 collective-permute-done.4.refs_6_
  63.7 9.1 %weight_halves.1 = (f32[16,40,640]{2,1,0:T(8,128)}, f32[16,40,640]{2,1,0:T(8,128)}, bf16[8,40,640]{2,1,0:T(8,128)(2,1)}, bf16[8,40,640]{2,1,0:T(8,128)(2,1)}, bf...) custom-call(s32[10]{0:T(128)} %stack.40.me_ref.info_ref, bf16[8,32,1280]{2,1,0:T(8,128)(2,1)} %get-tuple-element.75.refs_0_, ...), custom_call_target="tpu_custom_call" | custom-call | flops 1000 | bytes 1000 | tf_op jit(solution)/shard_map/weight_halves/pallas_call | solution.py:442
  73.9 1.1 collective-permute-done.8.refs_4_
  75.6 2.1 %collective-permute-start.11 = (bf16[8,32,1280]{2,1,0:T(8,128)(2,1)}, bf16[8,32,1280]{2,1,0:T(8,128)(2,1)}, u32[]{:S(2)}, u32[]{:S(2)}) collective-permute-start(bf16[8,32,1280]{2,1,0:T(8,128)(2,1)} %bitcast.80), channel_id=1, source_target_pairs={{0,2},{1,3},{2,0},{3,1},{4,6},{5,7},{6,4},{7,5},{8,10},{9,11},{10,... | collective-permute-start | bytes 1966088 | tf_op jit(solution)/shard_map/ppermute | solution.py:17
  77.6 4.1 %combine.4 = (f32[8,40,640]{2,1,0:T(8,128)}, bf16[8,40,640]{2,1,0:T(8,128)(2,1)}, f32[8,40,640]{2,1,0:T(8,128)}, bf16[8,40,640]{2,1,0:T(8,128)(2,1)}) custom-call(s32[10]{0:T(128)} %stack.40.me_ref.info_ref, f32[16,40,640]{2,1,0:T(8,128)} %get-tuple-element.83.refs_0_, f32[16,40,640]{2,1,0:T(8,128)} %get-tuple-element.84.refs_1_, ...), custom_call_target="tpu_custom_call" | custom-call | flops 1000 | bytes 1000 | tf_op jit(solution)/shard_map/combine/pallas_call | solution.py:372
  81.7 1.5 %collective-permute-start.13 = (bf16[8,40,640]{2,1,0:T(8,128)(2,1)}, bf16[8,40,640]{2,1,0:T(8,128)(2,1)}, u32[]{:S(2)}, u32[]{:S(2)}) collective-permute-start(bf16[8,40,640]{2,1,0:T(8,128)(2,1)} %get-tuple-element.95), channel_id=1, source_target_pairs={{0,4},{4,0},{8,12},{12,8},{16,20},{20,16},{24,28},{28,24},{1,5},{5... | collective-permute-start | bytes 1228808 | tf_op jit(solution)/shard_map/ppermute | solution.py:17
  83.3 1.6 %collective-permute-start.14 = (bf16[8,40,640]{2,1,0:T(8,128)(2,1)}, bf16[8,40,640]{2,1,0:T(8,128)(2,1)}, u32[]{:S(2)}, u32[]{:S(2)}) collective-permute-start(bf16[8,40,640]{2,1,0:T(8,128)(2,1)} %get-tuple-element.96), channel_id=1, source_target_pairs={{0,8},{4,12},{8,0},{12,4},{16,24},{20,28},{24,16},{28,20},{1,9},{5... | collective-permute-start | bytes 1228808 | tf_op jit(solution)/shard_map/ppermute | solution.py:17
  84.8 3.0 %convolution_convert_fusion = bf16[256,1280]{1,0:T(8,128)(2,1)} fusion(bf16[256,1280]{1,0:T(8,128)(2,1)} %bitcast.28, bf16[1280,1280]{1,0:T(8,128)(2,1)S(1)} %copy-done), kind=kOutput, calls=%fused_computation.9 | convolution fusion | flops 839188480 | bytes 4587520 | tf_op jit(solution)/shard_map/re,de->rd/dot_general | solution.py:491
  87.8 5.3 %backward.1 = (bf16[8,32,1280]{2,1,0:T(8,128)(2,1)}, bf16[8,32,1280]{2,1,0:T(8,128)(2,1)}, bf16[8,32,1280]{2,1,0:T(8,128)(2,1)}, bf16[8,32,1280]{2,1,0:T(8,128)(2,1)}) custom-call(bf16[512,512]{1,0:T(8,128)(2,1)} %get-tuple-element.94.kron_ref, f32[2,512,1280]{2,1,0:T(8,128)} %get-tuple-element.106.surrogate_ref, bf16[8,32,1280]{2,1,0:T(8,128)(2,1)} %bitcast.58, ...), custom_call_target="tpu_custom_call" | custom-call | flops 1342177280 | bytes 2621440 | tf_op jit(solution)/shard_map/backward/pallas_call | solution.py:137
  93.1 1.3 collective-permute-start.22
  95.0 2.8 %combine.5 = (f32[4,40,640]{2,1,0:T(8,128)}, bf16[4,40,640]{2,1,0:T(8,128)(2,1)}, f32[4,40,640]{2,1,0:T(8,128)}, bf16[4,40,640]{2,1,0:T(8,128)(2,1)}) custom-call(s32[10]{0:T(128)} %stack.40.me_ref.info_ref, f32[8,40,640]{2,1,0:T(8,128)} %get-tuple-element.102.refs_0_, f32[8,40,640]{2,1,0:T(8,128)} %get-tuple-element.103.refs_1_, ...), custom_call_target="tpu_custom_call" | custom-call | flops 1000 | bytes 1000 | tf_op jit(solution)/shard_map/combine/pallas_call | solution.py:372
  97.8 1.1 collective-permute-start.16
  99.6 4.1 %late_sums.1 = f32[56,128]{1,0:T(8,128)} custom-call(s32[10]{0:T(128)} %stack.40.me_ref.info_ref, f32[2,512,1280]{2,1,0:T(8,128)} %get-tuple-element.106.surrogate_ref, f32[56,128]{1,0:T(8,128)} %early_sums.1.early_ref, bf16[8,32,1280]{2,1,0:T(8,128)(2,1)} %constant_dynamic-slice_fusion.refs_0_, bf16[8,32,1280]{2,1,0:T(8,128)(2,1)} %collective-permute-done.1.refs_1_, ...), custom_call_target="tpu_custom_call" | custom-call | flops 5368709120 | bytes 10485760 | tf_op jit(solution)/shard_map/late_sums/pallas_call | solution.py:266
  103.7 1.7 %collective-permute-done.16.refs_2_ = bf16[4,40,640]{2,1,0:T(8,128)(2,1)S(1)} collective-permute-done((bf16[4,40,640]{2,1,0:T(8,128)(2,1)}, bf16[4,40,640]{2,1,0:T(8,128)(2,1)S(1)}, u32[]{:S(2)}, u32[]{:S(2)}) %collective-permute-start.16) | collective-permute-done | bytes 204832 | tf_op jit(solution)/shard_map/ppermute | solution.py:17
  105.4 0.9 collective-permute-done.17.refs_3_
  106.3 2.2 %combine.6 = (f32[2,40,1280]{2,1,0:T(8,128)}, bf16[2,40,1280]{2,1,0:T(8,128)(2,1)}) custom-call(s32[10]{0:T(128)} %stack.40.me_ref.info_ref, f32[4,40,640]{2,1,0:T(8,128)} %get-tuple-element.108.refs_0_, f32[4,40,640]{2,1,0:T(8,128)} %get-tuple-element.109.refs_1_, bf16[4,40,640]{2,1,0:T(8,128)(2,1)} %copy-done.8, ...), custom_call_target="tpu_custom_call" | custom-call | flops 1000 | bytes 1000 | tf_op jit(solution)/shard_map/combine/pallas_call | solution.py:372
  108.5 2.6 %collective-permute-start.21 = (bf16[2,40,1280]{2,1,0:T(8,128)(2,1)}, bf16[2,40,1280]{2,1,0:T(8,128)(2,1)S(1)}, u32[]{:S(2)}, u32[]{:S(2)}) collective-permute-start(bf16[2,40,1280]{2,1,0:T(8,128)(2,1)} %get-tuple-element.110), channel_id=1, source_target_pairs={{0,16},{4,20},{8,24},{12,28},{16,0},{20,4},{24,8},{28,12},{1,17},{... | collective-permute-start | bytes 614408 | tf_op jit(solution)/shard_map/ppermute | solution.py:17
  111.1 1.4 %collective-permute-done.18 = f32[56,128]{1,0:T(8,128)S(1)} collective-permute-done((f32[56,128]{1,0:T(8,128)}, f32[56,128]{1,0:T(8,128)S(1)}, u32[]{:S(2)}, u32[]{:S(2)}) %collective-permute-start.18) | collective-permute-done | bytes 28704 | tf_op jit(solution)/shard_map/ppermute | solution.py:17
  113.2 1.5 %collective-permute-start.19 = (f32[56,128]{1,0:T(8,128)S(1)}, f32[56,128]{1,0:T(8,128)S(1)}, u32[]{:S(2)}, u32[]{:S(2)}) collective-permute-start(f32[56,128]{1,0:T(8,128)S(1)} %add.60), channel_id=1, source_target_pairs={{0,4},{4,0},{8,12},{12,8},{16,20},{20,16},{24,28},{28,24},{1,5},{5... | collective-permute-start | bytes 86024 | tf_op jit(solution)/shard_map/ppermute | solution.py:17
  114.7 3.3 %place.2 = bf16[8,128,1280]{2,1,0:T(8,128)(2,1)} custom-call(s32[10]{0:T(128)} %stack.40.me_ref.info_ref, bf16[8,32,1280]{2,1,0:T(8,128)(2,1)} %bitcast.71, bf16[8,32,1280]{2,1,0:T(8,128)(2,1)} %collective-permute-done.10.refs_1_, bf16[8,32,1280]{2,1,0:T(8,128)(2,1)} %collective-permute-done.11.refs_2_, bf16[8,32,1280]{2,1,0:T(8,128)(2,1)} %collective-permute-done.12.refs_3_), custom_call_target="tpu_custom_call" | custom-call | flops 1000 | bytes 1000 | tf_op jit(solution)/shard_map/place/pallas_call | solution.py:309
  118.6 3.4 %collective-permute-done.20 = f32[56,128]{1,0:T(8,128)S(1)} collective-permute-done((f32[56,128]{1,0:T(8,128)S(1)}, f32[56,128]{1,0:T(8,128)S(1)}, u32[]{:S(2)}, u32[]{:S(2)}) %collective-permute-start.20) | collective-permute-done | bytes 28704 | tf_op jit(solution)/shard_map/ppermute | solution.py:17
  122.7 1.8 %combine.7 = (f32[1,40,1280]{2,1,0:T(8,128)}, bf16[1,40,1280]{2,1,0:T(8,128)(2,1)}) custom-call(s32[10]{0:T(128)} %stack.40.me_ref.info_ref, f32[2,40,1280]{2,1,0:T(8,128)} %get-tuple-element.115.refs_0_, bf16[2,40,1280]{2,1,0:T(8,128)(2,1)} %copy-done.7), custom_call_target="tpu_custom_call" | custom-call | flops 1000 | bytes 1000 | tf_op jit(solution)/shard_map/combine/pallas_call | solution.py:372
  125.1 1.2 collective-permute-start.27
  127.0 2.4 %collective-permute-start.25 = (f32[56,128]{1,0:T(8,128)S(1)}, f32[56,128]{1,0:T(8,128)S(1)}, u32[]{:S(2)}, u32[]{:S(2)}) collective-permute-start(f32[56,128]{1,0:T(8,128)S(1)} %add.62.refs_0_), channel_id=1, source_target_pairs={{0,16},{4,20},{8,24},{12,28},{16,0},{20,4},{24,8},{28,12},{1,17},{... | collective-permute-start | bytes 86024 | tf_op jit(solution)/shard_map/ppermute | solution.py:17
  129.5 3.3 %place.3 = bf16[8,128,1280]{2,1,0:T(8,128)(2,1)} custom-call(s32[10]{0:T(128)} %stack.40.me_ref.info_ref, bf16[8,32,1280]{2,1,0:T(8,128)(2,1)} %get-tuple-element.117.refs_0_, bf16[8,32,1280]{2,1,0:T(8,128)(2,1)} %collective-permute-done.15.refs_1_, bf16[8,32,1280]{2,1,0:T(8,128)(2,1)} %collective-permute-done.22.refs_2_, ...), custom_call_target="tpu_custom_call" | custom-call | flops 1000 | bytes 1000 | tf_op jit(solution)/shard_map/place/pallas_call | solution.py:309
  133.5 1.7 %final.1 = (bf16[40,1280]{1,0:T(8,128)(2,1)}, f32[32,32]{1,0:T(8,128)}, f32[1,32]{1,0:T(1,128)}, f32[10,128]{1,0:T(8,128)}) custom-call(f32[40,1280]{1,0:T(8,128)} %bitcast.76, bf16[40,1280]{1,0:T(8,128)(2,1)} %bitcast.77, f32[56,128]{1,0:T(8,128)} %copy-done.9, f32[56,128]{1,0:T(8,128)} %copy-done.13, f32[56,128]{1,0:T(8,128)} %copy-done.12, ...), custom_call_target="tpu_custom_call" | custom-call | flops 1000 | bytes 1000 | tf_op jit(solution)/shard_map/final/pallas_call | solution.py:397
  (72 shorter events, 9.1 us)
Async XLA Ops:
  0.6 16.4 %copy-start = (bf16[1280,1280]{1,0:T(8,128)(2,1)S(1)}, bf16[1280,1280]{1,0:T(8,128)(2,1)}, u32[]{:S(2)}) copy-start(bf16[1280,1280]{1,0:T(8,128)(2,1)} %param.9) | copy-start | bytes 9830404
  2.8 32.4 %collective-permute-start.2 = (bf16[8,32,1280]{2,1,0:T(8,128)(2,1)}, bf16[8,32,1280]{2,1,0:T(8,128)(2,1)}, u32[]{:S(2)}, u32[]{:S(2)}) collective-permute-start(bf16[8,32,1280]{2,1,0:T(8,128)(2,1)} %dynamic-slice_bitcast_fusion), channel_id=1, source_target_pairs={{0,2},{1,3},{2,0},{3,1},{4,6},{5,7},{6,4},{7,5},{8,10},{9,11},{10,... | collective-permute-start | bytes 1966088 | tf_op jit(solution)/shard_map/ppermute | solution.py:17
  7.7 27.5 %collective-permute-start.3 = (bf16[8,32,1280]{2,1,0:T(8,128)(2,1)}, bf16[8,32,1280]{2,1,0:T(8,128)(2,1)}, u32[]{:S(2)}, u32[]{:S(2)}) collective-permute-start(bf16[8,32,1280]{2,1,0:T(8,128)(2,1)} %constant_dynamic-slice_fusion.6), channel_id=1, source_target_pairs={{0,3},{1,2},{2,1},{3,0},{4,7},{5,6},{6,5},{7,4},{8,11},{9,10},{10,... | collective-permute-start | bytes 1966088 | tf_op jit(solution)/shard_map/ppermute | solution.py:17
  7.7 4.2 %copy-start.1 = (bf16[1,8,128,1280]{3,2,1,0:T(8,128)(2,1)S(1)}, bf16[1,8,128,1280]{3,2,1,0:T(8,128)(2,1)}, u32[]{:S(2)}) copy-start(bf16[1,8,128,1280]{3,2,1,0:T(8,128)(2,1)} %param.11) | copy-start | bytes 7864324
  9.8 18.2 %collective-permute-start.1 = (bf16[8,32,1280]{2,1,0:T(8,128)(2,1)}, bf16[8,32,1280]{2,1,0:T(8,128)(2,1)}, u32[]{:S(2)}, u32[]{:S(2)}) collective-permute-start(bf16[8,32,1280]{2,1,0:T(8,128)(2,1)} %constant_dynamic-slice_fusion.5), channel_id=1, source_target_pairs={{0,1},{1,0},{2,3},{3,2},{4,5},{5,4},{6,7},{7,6},{8,9},{9,8},{10,11... | collective-permute-start | bytes 1966088 | tf_op jit(solution)/shard_map/ppermute | solution.py:17
  12.8 39.8 %collective-permute-start.5 = (bf16[8,32,1280]{2,1,0:T(8,128)(2,1)}, bf16[8,32,1280]{2,1,0:T(8,128)(2,1)}, u32[]{:S(2)}, u32[]{:S(2)}) collective-permute-start(bf16[8,32,1280]{2,1,0:T(8,128)(2,1)} %constant_dynamic-slice_fusion.3), channel_id=1, source_target_pairs={{0,3},{1,2},{2,1},{3,0},{4,7},{5,6},{6,5},{7,4},{8,11},{9,10},{10,... | collective-permute-start | bytes 1966088 | tf_op jit(solution)/shard_map/ppermute | solution.py:17
  15.4 9.5 %collective-permute-start = (bf16[8,32,1280]{2,1,0:T(8,128)(2,1)}, bf16[8,32,1280]{2,1,0:T(8,128)(2,1)}, u32[]{:S(2)}, u32[]{:S(2)}) collective-permute-start(bf16[8,32,1280]{2,1,0:T(8,128)(2,1)} %constant_dynamic-slice_fusion.2), channel_id=1, source_target_pairs={{0,1},{1,0},{2,3},{3,2},{4,5},{5,4},{6,7},{7,6},{8,9},{9,8},{10,11... | collective-permute-start | bytes 1966088 | tf_op jit(solution)/shard_map/ppermute | solution.py:17
  17.0 1.9 %copy-start.3 = (bf16[8,32,1280]{2,1,0:T(8,128)(2,1)}, bf16[8,32,1280]{2,1,0:T(8,128)(2,1)S(1)}, u32[]{:S(2)}) copy-start(bf16[8,32,1280]{2,1,0:T(8,128)(2,1)S(1)} %constant_dynamic-slice_fusion.1.refs_4_) | copy-start | bytes 1966084
  17.1 2.0 %copy-start.2 = (bf16[1,8,128,1280]{3,2,1,0:T(8,128)(2,1)S(1)}, bf16[1,8,128,1280]{3,2,1,0:T(8,128)(2,1)}, u32[]{:S(2)}) copy-start(bf16[1,8,128,1280]{3,2,1,0:T(8,128)(2,1)} %param.11) | copy-start | bytes 7864324
  24.9 38.8 %collective-permute-start.4 = (bf16[8,32,1280]{2,1,0:T(8,128)(2,1)}, bf16[8,32,1280]{2,1,0:T(8,128)(2,1)}, u32[]{:S(2)}, u32[]{:S(2)}) collective-permute-start(bf16[8,32,1280]{2,1,0:T(8,128)(2,1)} %constant_dynamic-slice_fusion.4), channel_id=1, source_target_pairs={{0,2},{1,3},{2,0},{3,1},{4,6},{5,7},{6,4},{7,5},{8,10},{9,11},{10,... | collective-permute-start | bytes 1966088 | tf_op jit(solution)/shard_map/ppermute | solution.py:17
  28.0 13.7 %copy-start.14 = (f32[1280]{0:T(1024)S(1)}, f32[1280]{0:T(1024)}, u32[]{:S(2)}) copy-start(f32[1280]{0:T(1024)} %param.10) | copy-start | bytes 15364
  41.7 3.0 %copy-start.6 = (bf16[8,32,1280]{2,1,0:T(8,128)(2,1)S(1)}, bf16[8,32,1280]{2,1,0:T(8,128)(2,1)}, u32[]{:S(2)}) copy-start(bf16[8,32,1280]{2,1,0:T(8,128)(2,1)} %get-tuple-element.78.refs_2_) | copy-start | bytes 1966084
  44.8 4.1 %copy-start.5 = (bf16[8,32,1280]{2,1,0:T(8,128)(2,1)S(1)}, bf16[8,32,1280]{2,1,0:T(8,128)(2,1)}, u32[]{:S(2)}) copy-start(bf16[8,32,1280]{2,1,0:T(8,128)(2,1)} %get-tuple-element.77.refs_1_) | copy-start | bytes 1966084
  46.6 38.2 %collective-permute-start.12 = (bf16[8,32,1280]{2,1,0:T(8,128)(2,1)}, bf16[8,32,1280]{2,1,0:T(8,128)(2,1)}, u32[]{:S(2)}, u32[]{:S(2)}) collective-permute-start(bf16[8,32,1280]{2,1,0:T(8,128)(2,1)} %bitcast.24), channel_id=1, source_target_pairs={{0,3},{1,2},{2,1},{3,0},{4,7},{5,6},{6,5},{7,4},{8,11},{9,10},{10,... | collective-permute-start | bytes 1966088 | tf_op jit(solution)/shard_map/ppermute | solution.py:17
  48.9 1.9 %copy-start.4 = (bf16[8,32,1280]{2,1,0:T(8,128)(2,1)S(1)}, bf16[8,32,1280]{2,1,0:T(8,128)(2,1)}, u32[]{:S(2)}) copy-start(bf16[8,32,1280]{2,1,0:T(8,128)(2,1)} %get-tuple-element.75.refs_0_) | copy-start | bytes 1966084
  72.8 2.2 %collective-permute-start.8 = (bf16[8,40,640]{2,1,0:T(8,128)(2,1)}, bf16[8,40,640]{2,1,0:T(8,128)(2,1)}, u32[]{:S(2)}, u32[]{:S(2)}) collective-permute-start(bf16[8,40,640]{2,1,0:T(8,128)(2,1)} %get-tuple-element.90), channel_id=1, source_target_pairs={{0,1},{1,0},{2,3},{3,2},{4,5},{5,4},{6,7},{7,6},{8,9},{9,8},{10,11... | collective-permute-start | bytes 1228808 | tf_op jit(solution)/shard_map/ppermute | solution.py:17
  72.9 2.7 %collective-permute-start.9 = (bf16[8,40,640]{2,1,0:T(8,128)(2,1)}, bf16[8,40,640]{2,1,0:T(8,128)(2,1)}, u32[]{:S(2)}, u32[]{:S(2)}) collective-permute-start(bf16[8,40,640]{2,1,0:T(8,128)(2,1)} %get-tuple-element.92), channel_id=1, source_target_pairs={{0,1},{1,0},{2,3},{3,2},{4,5},{5,4},{6,7},{7,6},{8,9},{9,8},{10,11... | collective-permute-start | bytes 1228808 | tf_op jit(solution)/shard_map/ppermute | solution.py:17
  73.4 4.2 %collective-permute-start.7 = (bf16[8,40,640]{2,1,0:T(8,128)(2,1)}, bf16[8,40,640]{2,1,0:T(8,128)(2,1)}, u32[]{:S(2)}, u32[]{:S(2)}) collective-permute-start(bf16[8,40,640]{2,1,0:T(8,128)(2,1)} %get-tuple-element.89), channel_id=1, source_target_pairs={{0,1},{1,0},{2,3},{3,2},{4,5},{5,4},{6,7},{7,6},{8,9},{9,8},{10,11... | collective-permute-start | bytes 1228808 | tf_op jit(solution)/shard_map/ppermute | solution.py:17
  73.5 4.2 %collective-permute-start.6 = (bf16[8,40,640]{2,1,0:T(8,128)(2,1)}, bf16[8,40,640]{2,1,0:T(8,128)(2,1)}, u32[]{:S(2)}, u32[]{:S(2)}) collective-permute-start(bf16[8,40,640]{2,1,0:T(8,128)(2,1)} %get-tuple-element.87), channel_id=1, source_target_pairs={{0,1},{1,0},{2,3},{3,2},{4,5},{5,4},{6,7},{7,6},{8,9},{9,8},{10,11... | collective-permute-start | bytes 1228808 | tf_op jit(solution)/shard_map/ppermute | solution.py:17
  75.0 18.1 %collective-permute-start.10 = (bf16[8,32,1280]{2,1,0:T(8,128)(2,1)}, bf16[8,32,1280]{2,1,0:T(8,128)(2,1)}, u32[]{:S(2)}, u32[]{:S(2)}) collective-permute-start(bf16[8,32,1280]{2,1,0:T(8,128)(2,1)} %bitcast.81), channel_id=1, source_target_pairs={{0,1},{1,0},{2,3},{3,2},{4,5},{5,4},{6,7},{7,6},{8,9},{9,8},{10,11... | collective-permute-start | bytes 1966088 | tf_op jit(solution)/shard_map/ppermute | solution.py:17
  75.6 18.8 %collective-permute-start.11 = (bf16[8,32,1280]{2,1,0:T(8,128)(2,1)}, bf16[8,32,1280]{2,1,0:T(8,128)(2,1)}, u32[]{:S(2)}, u32[]{:S(2)}) collective-permute-start(bf16[8,32,1280]{2,1,0:T(8,128)(2,1)} %bitcast.80), channel_id=1, source_target_pairs={{0,2},{1,3},{2,0},{3,1},{4,6},{5,7},{6,4},{7,5},{8,10},{9,11},{10,... | collective-permute-start | bytes 1966088 | tf_op jit(solution)/shard_map/ppermute | solution.py:17
  81.7 13.3 %collective-permute-start.13 = (bf16[8,40,640]{2,1,0:T(8,128)(2,1)}, bf16[8,40,640]{2,1,0:T(8,128)(2,1)}, u32[]{:S(2)}, u32[]{:S(2)}) collective-permute-start(bf16[8,40,640]{2,1,0:T(8,128)(2,1)} %get-tuple-element.95), channel_id=1, source_target_pairs={{0,4},{4,0},{8,12},{12,8},{16,20},{20,16},{24,28},{28,24},{1,5},{5... | collective-permute-start | bytes 1228808 | tf_op jit(solution)/shard_map/ppermute | solution.py:17
  83.3 11.7 %collective-permute-start.14 = (bf16[8,40,640]{2,1,0:T(8,128)(2,1)}, bf16[8,40,640]{2,1,0:T(8,128)(2,1)}, u32[]{:S(2)}, u32[]{:S(2)}) collective-permute-start(bf16[8,40,640]{2,1,0:T(8,128)(2,1)} %get-tuple-element.96), channel_id=1, source_target_pairs={{0,8},{4,12},{8,0},{12,4},{16,24},{20,28},{24,16},{28,20},{1,9},{5... | collective-permute-start | bytes 1228808 | tf_op jit(solution)/shard_map/ppermute | solution.py:17
  93.1 10.6 %collective-permute-start.15 = (bf16[8,32,1280]{2,1,0:T(8,128)(2,1)}, bf16[8,32,1280]{2,1,0:T(8,128)(2,1)}, u32[]{:S(2)}, u32[]{:S(2)}) collective-permute-start(bf16[8,32,1280]{2,1,0:T(8,128)(2,1)} %get-tuple-element.99), channel_id=1, source_target_pairs={{0,1},{1,0},{2,3},{3,2},{4,5},{5,4},{6,7},{7,6},{8,9},{9,8},{10,11... | collective-permute-start | bytes 1966088 | tf_op jit(solution)/shard_map/ppermute | solution.py:17
  93.1 33.9 %collective-permute-start.22 = (bf16[8,32,1280]{2,1,0:T(8,128)(2,1)}, bf16[8,32,1280]{2,1,0:T(8,128)(2,1)}, u32[]{:S(2)}, u32[]{:S(2)}) collective-permute-start(bf16[8,32,1280]{2,1,0:T(8,128)(2,1)} %get-tuple-element.100), channel_id=1, source_target_pairs={{0,2},{1,3},{2,0},{3,1},{4,6},{5,7},{6,4},{7,5},{8,10},{9,11},{10,... | collective-permute-start | bytes 1966088 | tf_op jit(solution)/shard_map/ppermute | solution.py:17
  94.4 35.1 %collective-permute-start.23 = (bf16[8,32,1280]{2,1,0:T(8,128)(2,1)}, bf16[8,32,1280]{2,1,0:T(8,128)(2,1)}, u32[]{:S(2)}, u32[]{:S(2)}) collective-permute-start(bf16[8,32,1280]{2,1,0:T(8,128)(2,1)} %get-tuple-element.101), channel_id=1, source_target_pairs={{0,3},{1,2},{2,1},{3,0},{4,7},{5,6},{6,5},{7,4},{8,11},{9,10},{10,... | collective-permute-start | bytes 1966088 | tf_op jit(solution)/shard_map/ppermute | solution.py:17
  97.8 7.5 %collective-permute-start.16 = (bf16[4,40,640]{2,1,0:T(8,128)(2,1)}, bf16[4,40,640]{2,1,0:T(8,128)(2,1)S(1)}, u32[]{:S(2)}, u32[]{:S(2)}) collective-permute-start(bf16[4,40,640]{2,1,0:T(8,128)(2,1)} %get-tuple-element.104), channel_id=1, source_target_pairs={{0,8},{4,12},{8,0},{12,4},{16,24},{20,28},{24,16},{28,20},{1,9},{5... | collective-permute-start | bytes 614408 | tf_op jit(solution)/shard_map/ppermute | solution.py:17
  98.9 7.3 %collective-permute-start.17 = (bf16[4,40,640]{2,1,0:T(8,128)(2,1)}, bf16[4,40,640]{2,1,0:T(8,128)(2,1)}, u32[]{:S(2)}, u32[]{:S(2)}) collective-permute-start(bf16[4,40,640]{2,1,0:T(8,128)(2,1)} %get-tuple-element.105), channel_id=1, source_target_pairs={{0,4},{4,0},{8,12},{12,8},{16,20},{20,16},{24,28},{28,24},{1,5},{5... | collective-permute-start | bytes 614408 | tf_op jit(solution)/shard_map/ppermute | solution.py:17
  105.4 0.9 copy-start.8
  108.5 13.6 %collective-permute-start.21 = (bf16[2,40,1280]{2,1,0:T(8,128)(2,1)}, bf16[2,40,1280]{2,1,0:T(8,128)(2,1)S(1)}, u32[]{:S(2)}, u32[]{:S(2)}) collective-permute-start(bf16[2,40,1280]{2,1,0:T(8,128)(2,1)} %get-tuple-element.110), channel_id=1, source_target_pairs={{0,16},{4,20},{8,24},{12,28},{16,0},{20,4},{24,8},{28,12},{1,17},{... | collective-permute-start | bytes 614408 | tf_op jit(solution)/shard_map/ppermute | solution.py:17
  111.0 1.4 %collective-permute-start.18 = (f32[56,128]{1,0:T(8,128)}, f32[56,128]{1,0:T(8,128)S(1)}, u32[]{:S(2)}, u32[]{:S(2)}) collective-permute-start(f32[56,128]{1,0:T(8,128)} %late_sums.1), channel_id=1, source_target_pairs={{0,1},{1,0},{2,3},{3,2},{4,5},{5,4},{6,7},{7,6},{8,9},{9,8},{10,11... | collective-permute-start | bytes 86024 | tf_op jit(solution)/shard_map/ppermute | solution.py:17
  113.2 4.8 %collective-permute-start.19 = (f32[56,128]{1,0:T(8,128)S(1)}, f32[56,128]{1,0:T(8,128)S(1)}, u32[]{:S(2)}, u32[]{:S(2)}) collective-permute-start(f32[56,128]{1,0:T(8,128)S(1)} %add.60), channel_id=1, source_target_pairs={{0,4},{4,0},{8,12},{12,8},{16,20},{20,16},{24,28},{28,24},{1,5},{5... | collective-permute-start | bytes 86024 | tf_op jit(solution)/shard_map/ppermute | solution.py:17
  118.1 3.9 %collective-permute-start.20 = (f32[56,128]{1,0:T(8,128)S(1)}, f32[56,128]{1,0:T(8,128)S(1)}, u32[]{:S(2)}, u32[]{:S(2)}) collective-permute-start(f32[56,128]{1,0:T(8,128)S(1)} %add.61), channel_id=1, source_target_pairs={{0,8},{4,12},{8,0},{12,4},{16,24},{20,28},{24,16},{28,20},{1,9},{5... | collective-permute-start | bytes 86024 | tf_op jit(solution)/shard_map/ppermute | solution.py:17
  122.0 10.9 %copy-start.9 = (f32[56,128]{1,0:T(8,128)}, f32[56,128]{1,0:T(8,128)S(1)}, u32[]{:S(2)}) copy-start(f32[56,128]{1,0:T(8,128)S(1)} %add.62.refs_0_) | copy-start | bytes 86020
  122.0 0.7 copy-start.7
  124.5 8.3 %collective-permute-start.24 = (bf16[1,40,1280]{2,1,0:T(8,128)(2,1)}, bf16[1,40,1280]{2,1,0:T(8,128)(2,1)S(1)}, u32[]{:S(2)}, u32[]{:S(2)}) collective-permute-start(bf16[1,40,1280]{2,1,0:T(8,128)(2,1)} %get-tuple-element.116), channel_id=1, source_target_pairs={{0,2},{1,3},{2,0},{3,1},{4,6},{5,7},{6,4},{7,5},{8,10},{9,11},{10,... | collective-permute-start | bytes 307208 | tf_op jit(solution)/shard_map/ppermute | solution.py:17
  125.1 7.7 %collective-permute-start.27 = (f32[56,128]{1,0:T(8,128)S(1)}, f32[56,128]{1,0:T(8,128)S(1)}, u32[]{:S(2)}, u32[]{:S(2)}) collective-permute-start(f32[56,128]{1,0:T(8,128)S(1)} %add.62.refs_0_), channel_id=1, source_target_pairs={{0,18},{1,19},{2,16},{3,17},{4,22},{5,23},{6,20},{7,21},{8,26},{9,... | collective-permute-start | bytes 86024 | tf_op jit(solution)/shard_map/ppermute | solution.py:17
  126.3 6.5 %collective-permute-start.26 = (f32[56,128]{1,0:T(8,128)S(1)}, f32[56,128]{1,0:T(8,128)S(1)}, u32[]{:S(2)}, u32[]{:S(2)}) collective-permute-start(f32[56,128]{1,0:T(8,128)S(1)} %add.62.refs_0_), channel_id=1, source_target_pairs={{0,2},{1,3},{2,0},{3,1},{4,6},{5,7},{6,4},{7,5},{8,10},{9,11},{10,... | collective-permute-start | bytes 86024 | tf_op jit(solution)/shard_map/ppermute | solution.py:17
  127.0 5.8 %collective-permute-start.25 = (f32[56,128]{1,0:T(8,128)S(1)}, f32[56,128]{1,0:T(8,128)S(1)}, u32[]{:S(2)}, u32[]{:S(2)}) collective-permute-start(f32[56,128]{1,0:T(8,128)S(1)} %add.62.refs_0_), channel_id=1, source_target_pairs={{0,16},{4,20},{8,24},{12,28},{16,0},{20,4},{24,8},{28,12},{1,17},{... | collective-permute-start | bytes 86024 | tf_op jit(solution)/shard_map/ppermute | solution.py:17
  132.8 0.6 copy-start.11
  132.8 0.6 copy-start.12
  132.8 0.6 copy-start.13
  132.9 0.7 copy-start.10

commit v5 on v4

--- a/solution.py
+++ b/solution.py
@@ -412,20 +412,22 @@
 def weight_kernel(shard, parts, info_ref, *refs):
     spikes, cots, outs = refs[:parts], refs[parts : 2 * parts], refs[2 * parts : -1]
     part_ref = refs[-1]
-    half = part_ref.shape[2]
+    half = part_ref.shape[1] // 2
     core = jnp.bitwise_and(info_ref[0], 1)
-    turned = rows_of(spikes, 0, spikes[0].shape[-1]).T
-    for side in range(2):
-        part_ref[side] = jnp.dot(
-            turned, rows_of(cots, side * half, half), preferred_element_type=jnp.float32
-        )
-    count = part_ref.shape[1] // shard // 2
+    part_ref[...] = lax.dot_general(
+        rows_of(spikes, 0, spikes[0].shape[-1]),
+        rows_of(cots, 0, cots[0].shape[-1]),
+        (((0,), (0,)), ((), ())),
+        preferred_element_type=jnp.float32,
+    )
+    count = part_ref.shape[0] // shard // 2
     step = pl.program_id(0)
     for side in range(2):
         for n in range(count):
             at = lambda odd: pl.ds(pl.multiple_of((2 * n + odd) * shard, 8), shard)
-            outs[side][n] = part_ref[side, at(core), :]
-            send = part_ref[side, at(1 - core), :].astype(jnp.bfloat16)
+            cols = slice(side * half, (side + 1) * half)
+            outs[side][n] = part_ref[at(core), cols]
+            send = part_ref[at(1 - core), cols].astype(jnp.bfloat16)
             for now in range(2):
 
                 @pl.when(step == now)
@@ -448,7 +450,7 @@
         out_specs=[pl.BlockSpec((count, shard, cols), lambda i: (i, 0, 0))] * 2
         + [pl.BlockSpec((count, shard, cols), lambda i: (0, 0, 0))] * 4,
         out_shape=[keep, keep] + [send] * 4,
-        scratch_shapes=[pltpu.VMEM((2, block, cols), jnp.float32)],
+        scratch_shapes=[pltpu.VMEM((block, width), jnp.float32)],
         cost_estimate=SMALL,
         name="weight_halves",
     )(info, *spikes, *cots)

time: 136 us -> 135 us (level)
  no operation moved by 1% of the time
where the time goes in v5:
time: 135 us
  Pallas kernels  52.7 us (39%)
  starting transfers between devices  27 us (20%)
  matrix products  19.5 us (14%)
  waiting for transfers between devices  17.5 us (13%)
  local copies, waits for them, and re-layouts  15.1 us (11%)
  other arithmetic  1.79 us (1%)
    ppermute x28, starting transfers between devices, xor_permute(): return lax.ppermute(value, axis, [(i, i ^ mask) for i in range(size)])  27 us
    ppermute x28, waiting for transfers between devices, xor_permute(): return lax.ppermute(value, axis, [(i, i ^ mask) for i in range(size)])  17.5 us
    dynamic_slice x8, local copies, waits for them, and re-layouts, cut(): found[k] = lax.dynamic_slice_in_dim(value, (me ^ k) * share, share, axis=1)  13.1 us
    pallas_call x2, Pallas kernels, small_sums(): pl.pallas_call(functools.partial(late_kernel if late else early_kernel, p...  11 us
    pallas_call x4, Pallas kernels, combine(): pl.pallas_call(functools.partial(combine_kernel, tuple(shapes), counts, l...  10.9 us
    dot_general x4, matrix products, spike_grad(): jnp.einsum('re,de->rd', flat(cot), weight, preferred_element_type=jnp.flo...  10.9 us
    dot_general x4, matrix products, body(): jnp.dot(flat(spikes[k]), weight, preferred_element_type=jnp.float32) + bias  8.66 us
    pallas_call x1, Pallas kernels, weight_halves(): pl.pallas_call(functools.partial(weight_kernel, shard, len(spikes)), grid...  8.51 us
  transfers between devices with their start and end apart: 28, of which 8 were waited for; matrix products, arithmetic and copies ran while one was open for 24% of the time, Pallas kernels for 38%

profile of v5, /device:TPU:0, one launch (start us, length us, event | category | flops | bytes accessed | tf_op | source)
XLA Modules:
  0.0 134.6 jit_solution(2940796578514744609)
XLA Ops:
  0.7 2.1 %dynamic-slice_bitcast_fusion = bf16[8,32,1280]{2,1,0:T(8,128)(2,1)} fusion(bf16[1,8,128,1280]{3,2,1,0:T(8,128)(2,1)} %param.6, s32[]{:T(128)S(6)} %select_n.16), kind=kLoop, calls=%fused_computation.13 | loop fusion | bytes 1310724 | tf_op jit(solution)/shard_map/dynamic_slice | solution.py:482
  2.8 2.9 %collective-permute-start.2 = (bf16[8,32,1280]{2,1,0:T(8,128)(2,1)}, bf16[8,32,1280]{2,1,0:T(8,128)(2,1)}, u32[]{:S(2)}, u32[]{:S(2)}) collective-permute-start(bf16[8,32,1280]{2,1,0:T(8,128)(2,1)} %dynamic-slice_bitcast_fusion), channel_id=1, source_target_pairs={{0,2},{1,3},{2,0},{3,1},{4,6},{5,7},{6,4},{7,5},{8,10},{9,11},{10,... | collective-permute-start | bytes 1966088 | tf_op jit(solution)/shard_map/ppermute | solution.py:17
  5.7 2.0 %constant_dynamic-slice_fusion.6 = bf16[8,32,1280]{2,1,0:T(8,128)(2,1)} fusion(bf16[8,128,1280]{2,1,0:T(8,128)(2,1)} %bitcast.63, s32[]{:T(128)S(6)} %select_n.17), kind=kLoop, calls=%fused_computation.20 | loop fusion | bytes 1310724 | tf_op jit(solution)/shard_map/dynamic_slice | solution.py:482
  7.7 2.1 %constant_dynamic-slice_fusion.5 = bf16[8,32,1280]{2,1,0:T(8,128)(2,1)} fusion(bf16[8,128,1280]{2,1,0:T(8,128)(2,1)} %bitcast.64, s32[]{:T(128)S(6)} %select_n.18), kind=kLoop, calls=%fused_computation.19 | loop fusion | bytes 1310724 | tf_op jit(solution)/shard_map/dynamic_slice | solution.py:482
  9.9 2.0 %constant_dynamic-slice_fusion.4 = bf16[8,32,1280]{2,1,0:T(8,128)(2,1)} fusion(bf16[8,128,1280]{2,1,0:T(8,128)(2,1)} %bitcast.53, s32[]{:T(128)S(6)} %select_n.16), kind=kLoop, calls=%fused_computation.18 | loop fusion | bytes 1310724 | tf_op jit(solution)/shard_map/dynamic_slice | solution.py:482
  11.9 0.9 constant_dynamic-slice_fusion.3
  12.8 1.6 %collective-permute-start.5 = (bf16[8,32,1280]{2,1,0:T(8,128)(2,1)}, bf16[8,32,1280]{2,1,0:T(8,128)(2,1)}, u32[]{:S(2)}, u32[]{:S(2)}) collective-permute-start(bf16[8,32,1280]{2,1,0:T(8,128)(2,1)} %constant_dynamic-slice_fusion.3), channel_id=1, source_target_pairs={{0,3},{1,2},{2,1},{3,0},{4,7},{5,6},{6,5},{7,4},{8,11},{9,10},{10,... | collective-permute-start | bytes 1966088 | tf_op jit(solution)/shard_map/ppermute | solution.py:17
  14.4 1.0 constant_dynamic-slice_fusion.2
  15.9 1.1 constant_dynamic-slice_fusion.1.refs_4_
  17.1 1.9 %convolution_convert_fusion.3 = bf16[256,1280]{1,0:T(8,128)(2,1)} fusion(bf16[256,1280]{1,0:T(8,128)(2,1)S(1)} %bitcast.68, bf16[1280,1280]{1,0:T(8,128)(2,1)S(1)} %copy-done), kind=kOutput, calls=%fused_computation.12 | convolution fusion | flops 839188480 | bytes 4587520 | tf_op jit(solution)/shard_map/re,de->rd/dot_general | solution.py:493
  19.0 1.0 convert_reduce_fusion
  20.6 2.3 %build_krons.1 = (bf16[512,512]{1,0:T(8,128)(2,1)}, bf16[512,512]{1,0:T(8,128)(2,1)}, f32[512,1]{1,0:T(8,128)}) custom-call(s32[10]{0:T(128)} %stack.40.me_ref.info_ref, f32[32,32]{1,0:T(8,128)} %mixing_ref.1, f32[1,32]{1,0:T(1,128)} %bitcast.79), custom_call_target="tpu_custom_call" | custom-call | tf_op jit(solution)/shard_map/build_krons/pallas_call | solution.py:60
  22.9 2.0 %constant_dynamic-slice_fusion.refs_0_ = bf16[8,32,1280]{2,1,0:T(8,128)(2,1)} fusion(bf16[8,128,1280]{2,1,0:T(8,128)(2,1)} %bitcast.65, s32[]{:T(128)S(6)} %select_n.19), kind=kLoop, calls=%fused_computation.14 | loop fusion | bytes 1310724 | tf_op jit(solution)/shard_map/dynamic_slice | solution.py:482
  25.0 3.0 %convolution_convert_fusion.2 = bf16[256,1280]{1,0:T(8,128)(2,1)} fusion(bf16[256,1280]{1,0:T(8,128)(2,1)} %bitcast.15, bf16[1280,1280]{1,0:T(8,128)(2,1)S(1)} %copy-done), kind=kOutput, calls=%fused_computation.11 | convolution fusion | flops 839188480 | bytes 4587520 | tf_op jit(solution)/shard_map/re,de->rd/dot_general | solution.py:493
  28.0 7.2 %collective-permute-done.3.refs_3_ = bf16[8,32,1280]{2,1,0:T(8,128)(2,1)} collective-permute-done((bf16[8,32,1280]{2,1,0:T(8,128)(2,1)}, bf16[8,32,1280]{2,1,0:T(8,128)(2,1)}, u32[]{:S(2)}, u32[]{:S(2)}) %collective-permute-start.3) | collective-permute-done | bytes 655392 | tf_op jit(solution)/shard_map/ppermute | solution.py:17
  35.2 6.5 %forward.1 = (bf16[8,32,1280]{2,1,0:T(8,128)(2,1)}, bf16[8,32,1280]{2,1,0:T(8,128)(2,1)}, bf16[8,32,1280]{2,1,0:T(8,128)(2,1)}, bf16[8,32,1280]{2,1,0:T(8,128)(2,1)}, f32[2,512,1280]{2,1,0:T(8,128)}) custom-call(bf16[512,512]{1,0:T(8,128)(2,1)} %get-tuple-element.65.kron_ref, f32[512,1]{1,0:T(8,128)} %get-tuple-element.73.thr_ref, ...), custom_call_target="tpu_custom_call" | custom-call | tf_op jit(solution)/shard_map/forward/pallas_call | solution.py:99
  41.7 3.0 %fusion.3 = bf16[256,1280]{1,0:T(8,128)(2,1)} fusion(bf16[256,1280]{1,0:T(8,128)(2,1)} %bitcast.75, bf16[1280,1280]{1,0:T(8,128)(2,1)S(1)} %copy-done, f32[1280]{0:T(1024)S(1)} %copy-done.14), kind=kOutput, calls=%fused_computation.8 | convolution fusion | flops 839516160 | bytes 4592640 | tf_op jit(solution)/shard_map/dot_general | solution.py:500
  44.8 1.9 %fusion.2 = bf16[256,1280]{1,0:T(8,128)(2,1)} fusion(bf16[256,1280]{1,0:T(8,128)(2,1)S(1)} %bitcast.74, bf16[1280,1280]{1,0:T(8,128)(2,1)S(1)} %copy-done, f32[1280]{0:T(1024)S(1)} %copy-done.14), kind=kOutput, calls=%fused_computation.7 | convolution fusion | flops 839516160 | bytes 4592640 | tf_op jit(solution)/shard_map/dot_general | solution.py:500
  46.6 2.2 %collective-permute-start.12 = (bf16[8,32,1280]{2,1,0:T(8,128)(2,1)}, bf16[8,32,1280]{2,1,0:T(8,128)(2,1)}, u32[]{:S(2)}, u32[]{:S(2)}) collective-permute-start(bf16[8,32,1280]{2,1,0:T(8,128)(2,1)} %bitcast.24), channel_id=1, source_target_pairs={{0,3},{1,2},{2,1},{3,0},{4,7},{5,6},{6,5},{7,4},{8,11},{9,10},{10,... | collective-permute-start | bytes 1966088 | tf_op jit(solution)/shard_map/ppermute | solution.py:17
  48.9 1.9 %fusion.1 = bf16[256,1280]{1,0:T(8,128)(2,1)} fusion(bf16[256,1280]{1,0:T(8,128)(2,1)S(1)} %bitcast.73, bf16[1280,1280]{1,0:T(8,128)(2,1)S(1)} %copy-done, f32[1280]{0:T(1024)S(1)} %copy-done.14), kind=kOutput, calls=%fused_computation.6 | convolution fusion | flops 839516160 | bytes 4592640 | tf_op jit(solution)/shard_map/dot_general | solution.py:500
  50.7 1.9 %fusion = bf16[256,1280]{1,0:T(8,128)(2,1)} fusion(bf16[256,1280]{1,0:T(8,128)(2,1)S(1)} %bitcast.72, bf16[1280,1280]{1,0:T(8,128)(2,1)S(1)} %copy-done, f32[1280]{0:T(1024)S(1)} %copy-done.14), kind=kOutput, calls=%fused_computation.5 | convolution fusion | flops 839516160 | bytes 4592640 | tf_op jit(solution)/shard_map/dot_general | solution.py:500
  52.6 3.0 %convolution_convert_fusion.1 = bf16[256,1280]{1,0:T(8,128)(2,1)} fusion(bf16[256,1280]{1,0:T(8,128)(2,1)} %bitcast.26, bf16[1280,1280]{1,0:T(8,128)(2,1)S(1)} %copy-done), kind=kOutput, calls=%fused_computation.10 | convolution fusion | flops 839188480 | bytes 4587520 | tf_op jit(solution)/shard_map/re,de->rd/dot_general | solution.py:493
  55.6 6.9 %early_sums.1.early_ref = f32[56,128]{1,0:T(8,128)} custom-call(s32[10]{0:T(128)} %stack.40.me_ref.info_ref, f32[2,512,1280]{2,1,0:T(8,128)} %get-tuple-element.106.surrogate_ref, f32[10,128]{1,0:T(8,128)} %bitcast.78, bf16[8,32,1280]{2,1,0:T(8,128)(2,1)} %constant_dynamic-slice_fusion.refs_0_, bf16[8,32,1280]{2,1,0:T(8,128)(2,1)} %collective-permute-done.1.refs_1_, ...), custom_call_target="tpu_custom_call" | custom-call | flops 1000 | bytes 1000 | tf_op jit(solution)/shard_map/early_sums/pallas_call | solution.py:266
  62.5 1.3 collective-permute-done.4.refs_6_
  63.7 8.5 %weight_halves.1 = (f32[16,40,640]{2,1,0:T(8,128)}, f32[16,40,640]{2,1,0:T(8,128)}, bf16[8,40,640]{2,1,0:T(8,128)(2,1)}, bf16[8,40,640]{2,1,0:T(8,128)(2,1)}, bf...) custom-call(s32[10]{0:T(128)} %stack.40.me_ref.info_ref, bf16[8,32,1280]{2,1,0:T(8,128)(2,1)} %get-tuple-element.75.refs_0_, ...), custom_call_target="tpu_custom_call" | custom-call | flops 1000 | bytes 1000 | tf_op jit(solution)/shard_map/weight_halves/pallas_call | solution.py:444
  73.3 1.1 collective-permute-done.8.refs_4_
  75.0 2.1 %collective-permute-start.11 = (bf16[8,32,1280]{2,1,0:T(8,128)(2,1)}, bf16[8,32,1280]{2,1,0:T(8,128)(2,1)}, u32[]{:S(2)}, u32[]{:S(2)}) collective-permute-start(bf16[8,32,1280]{2,1,0:T(8,128)(2,1)} %bitcast.80), channel_id=1, source_target_pairs={{0,2},{1,3},{2,0},{3,1},{4,6},{5,7},{6,4},{7,5},{8,10},{9,11},{10,... | collective-permute-start | bytes 1966088 | tf_op jit(solution)/shard_map/ppermute | solution.py:17
  77.1 4.1 %combine.4 = (f32[8,40,640]{2,1,0:T(8,128)}, bf16[8,40,640]{2,1,0:T(8,128)(2,1)}, f32[8,40,640]{2,1,0:T(8,128)}, bf16[8,40,640]{2,1,0:T(8,128)(2,1)}) custom-call(s32[10]{0:T(128)} %stack.40.me_ref.info_ref, f32[16,40,640]{2,1,0:T(8,128)} %get-tuple-element.83.refs_0_, f32[16,40,640]{2,1,0:T(8,128)} %get-tuple-element.84.refs_1_, ...), custom_call_target="tpu_custom_call" | custom-call | flops 1000 | bytes 1000 | tf_op jit(solution)/shard_map/combine/pallas_call | solution.py:372
  81.1 1.5 %collective-permute-start.13 = (bf16[8,40,640]{2,1,0:T(8,128)(2,1)}, bf16[8,40,640]{2,1,0:T(8,128)(2,1)}, u32[]{:S(2)}, u32[]{:S(2)}) collective-permute-start(bf16[8,40,640]{2,1,0:T(8,128)(2,1)} %get-tuple-element.95), channel_id=1, source_target_pairs={{0,4},{4,0},{8,12},{12,8},{16,20},{20,16},{24,28},{28,24},{1,5},{5... | collective-permute-start | bytes 1228808 | tf_op jit(solution)/shard_map/ppermute | solution.py:17
  82.7 1.6 %collective-permute-start.14 = (bf16[8,40,640]{2,1,0:T(8,128)(2,1)}, bf16[8,40,640]{2,1,0:T(8,128)(2,1)}, u32[]{:S(2)}, u32[]{:S(2)}) collective-permute-start(bf16[8,40,640]{2,1,0:T(8,128)(2,1)} %get-tuple-element.96), channel_id=1, source_target_pairs={{0,8},{4,12},{8,0},{12,4},{16,24},{20,28},{24,16},{28,20},{1,9},{5... | collective-permute-start | bytes 1228808 | tf_op jit(solution)/shard_map/ppermute | solution.py:17
  84.3 3.0 %convolution_convert_fusion = bf16[256,1280]{1,0:T(8,128)(2,1)} fusion(bf16[256,1280]{1,0:T(8,128)(2,1)} %bitcast.28, bf16[1280,1280]{1,0:T(8,128)(2,1)S(1)} %copy-done), kind=kOutput, calls=%fused_computation.9 | convolution fusion | flops 839188480 | bytes 4587520 | tf_op jit(solution)/shard_map/re,de->rd/dot_general | solution.py:493
  87.2 5.3 %backward.1 = (bf16[8,32,1280]{2,1,0:T(8,128)(2,1)}, bf16[8,32,1280]{2,1,0:T(8,128)(2,1)}, bf16[8,32,1280]{2,1,0:T(8,128)(2,1)}, bf16[8,32,1280]{2,1,0:T(8,128)(2,1)}) custom-call(bf16[512,512]{1,0:T(8,128)(2,1)} %get-tuple-element.94.kron_ref, f32[2,512,1280]{2,1,0:T(8,128)} %get-tuple-element.106.surrogate_ref, bf16[8,32,1280]{2,1,0:T(8,128)(2,1)} %bitcast.58, ...), custom_call_target="tpu_custom_call" | custom-call | flops 1342177280 | bytes 2621440 | tf_op jit(solution)/shard_map/backward/pallas_call | solution.py:137
  92.5 1.2 collective-permute-start.22
  94.4 2.8 %combine.5 = (f32[4,40,640]{2,1,0:T(8,128)}, bf16[4,40,640]{2,1,0:T(8,128)(2,1)}, f32[4,40,640]{2,1,0:T(8,128)}, bf16[4,40,640]{2,1,0:T(8,128)(2,1)}) custom-call(s32[10]{0:T(128)} %stack.40.me_ref.info_ref, f32[8,40,640]{2,1,0:T(8,128)} %get-tuple-element.102.refs_0_, f32[8,40,640]{2,1,0:T(8,128)} %get-tuple-element.103.refs_1_, ...), custom_call_target="tpu_custom_call" | custom-call | flops 1000 | bytes 1000 | tf_op jit(solution)/shard_map/combine/pallas_call | solution.py:372
  97.2 1.1 collective-permute-start.16
  99.0 4.1 %late_sums.1 = f32[56,128]{1,0:T(8,128)} custom-call(s32[10]{0:T(128)} %stack.40.me_ref.info_ref, f32[2,512,1280]{2,1,0:T(8,128)} %get-tuple-element.106.surrogate_ref, f32[56,128]{1,0:T(8,128)} %early_sums.1.early_ref, bf16[8,32,1280]{2,1,0:T(8,128)(2,1)} %constant_dynamic-slice_fusion.refs_0_, bf16[8,32,1280]{2,1,0:T(8,128)(2,1)} %collective-permute-done.1.refs_1_, ...), custom_call_target="tpu_custom_call" | custom-call | flops 5368709120 | bytes 10485760 | tf_op jit(solution)/shard_map/late_sums/pallas_call | solution.py:266
  103.1 1.7 %collective-permute-done.16.refs_2_ = bf16[4,40,640]{2,1,0:T(8,128)(2,1)S(1)} collective-permute-done((bf16[4,40,640]{2,1,0:T(8,128)(2,1)}, bf16[4,40,640]{2,1,0:T(8,128)(2,1)S(1)}, u32[]{:S(2)}, u32[]{:S(2)}) %collective-permute-start.16) | collective-permute-done | bytes 204832 | tf_op jit(solution)/shard_map/ppermute | solution.py:17
  105.7 2.2 %combine.6 = (f32[2,40,1280]{2,1,0:T(8,128)}, bf16[2,40,1280]{2,1,0:T(8,128)(2,1)}) custom-call(s32[10]{0:T(128)} %stack.40.me_ref.info_ref, f32[4,40,640]{2,1,0:T(8,128)} %get-tuple-element.108.refs_0_, f32[4,40,640]{2,1,0:T(8,128)} %get-tuple-element.109.refs_1_, bf16[4,40,640]{2,1,0:T(8,128)(2,1)} %copy-done.8, ...), custom_call_target="tpu_custom_call" | custom-call | flops 1000 | bytes 1000 | tf_op jit(solution)/shard_map/combine/pallas_call | solution.py:372
  107.9 2.6 %collective-permute-start.21 = (bf16[2,40,1280]{2,1,0:T(8,128)(2,1)}, bf16[2,40,1280]{2,1,0:T(8,128)(2,1)S(1)}, u32[]{:S(2)}, u32[]{:S(2)}) collective-permute-start(bf16[2,40,1280]{2,1,0:T(8,128)(2,1)} %get-tuple-element.110), channel_id=1, source_target_pairs={{0,16},{4,20},{8,24},{12,28},{16,0},{20,4},{24,8},{28,12},{1,17},{... | collective-permute-start | bytes 614408 | tf_op jit(solution)/shard_map/ppermute | solution.py:17
  110.4 1.4 %collective-permute-done.18 = f32[56,128]{1,0:T(8,128)S(1)} collective-permute-done((f32[56,128]{1,0:T(8,128)}, f32[56,128]{1,0:T(8,128)S(1)}, u32[]{:S(2)}, u32[]{:S(2)}) %collective-permute-start.18) | collective-permute-done | bytes 28704 | tf_op jit(solution)/shard_map/ppermute | solution.py:17
  112.6 1.5 %collective-permute-start.19 = (f32[56,128]{1,0:T(8,128)S(1)}, f32[56,128]{1,0:T(8,128)S(1)}, u32[]{:S(2)}, u32[]{:S(2)}) collective-permute-start(f32[56,128]{1,0:T(8,128)S(1)} %add.60), channel_id=1, source_target_pairs={{0,4},{4,0},{8,12},{12,8},{16,20},{20,16},{24,28},{28,24},{1,5},{5... | collective-permute-start | bytes 86024 | tf_op jit(solution)/shard_map/ppermute | solution.py:17
  114.1 3.3 %place.2 = bf16[8,128,1280]{2,1,0:T(8,128)(2,1)} custom-call(s32[10]{0:T(128)} %stack.40.me_ref.info_ref, bf16[8,32,1280]{2,1,0:T(8,128)(2,1)} %bitcast.71, bf16[8,32,1280]{2,1,0:T(8,128)(2,1)} %collective-permute-done.10.refs_1_, bf16[8,32,1280]{2,1,0:T(8,128)(2,1)} %collective-permute-done.11.refs_2_, bf16[8,32,1280]{2,1,0:T(8,128)(2,1)} %collective-permute-done.12.refs_3_), custom_call_target="tpu_custom_call" | custom-call | flops 1000 | bytes 1000 | tf_op jit(solution)/shard_map/place/pallas_call | solution.py:309
  118.0 3.4 %collective-permute-done.20 = f32[56,128]{1,0:T(8,128)S(1)} collective-permute-done((f32[56,128]{1,0:T(8,128)S(1)}, f32[56,128]{1,0:T(8,128)S(1)}, u32[]{:S(2)}, u32[]{:S(2)}) %collective-permute-start.20) | collective-permute-done | bytes 28704 | tf_op jit(solution)/shard_map/ppermute | solution.py:17
  122.1 1.8 %combine.7 = (f32[1,40,1280]{2,1,0:T(8,128)}, bf16[1,40,1280]{2,1,0:T(8,128)(2,1)}) custom-call(s32[10]{0:T(128)} %stack.40.me_ref.info_ref, f32[2,40,1280]{2,1,0:T(8,128)} %get-tuple-element.115.refs_0_, bf16[2,40,1280]{2,1,0:T(8,128)(2,1)} %copy-done.7), custom_call_target="tpu_custom_call" | custom-call | flops 1000 | bytes 1000 | tf_op jit(solution)/shard_map/combine/pallas_call | solution.py:372
  124.5 1.3 collective-permute-start.27
  126.4 2.4 %collective-permute-start.25 = (f32[56,128]{1,0:T(8,128)S(1)}, f32[56,128]{1,0:T(8,128)S(1)}, u32[]{:S(2)}, u32[]{:S(2)}) collective-permute-start(f32[56,128]{1,0:T(8,128)S(1)} %add.62.refs_0_), channel_id=1, source_target_pairs={{0,16},{4,20},{8,24},{12,28},{16,0},{20,4},{24,8},{28,12},{1,17},{... | collective-permute-start | bytes 86024 | tf_op jit(solution)/shard_map/ppermute | solution.py:17
  128.9 3.3 %place.3 = bf16[8,128,1280]{2,1,0:T(8,128)(2,1)} custom-call(s32[10]{0:T(128)} %stack.40.me_ref.info_ref, bf16[8,32,1280]{2,1,0:T(8,128)(2,1)} %get-tuple-element.117.refs_0_, bf16[8,32,1280]{2,1,0:T(8,128)(2,1)} %collective-permute-done.15.refs_1_, bf16[8,32,1280]{2,1,0:T(8,128)(2,1)} %collective-permute-done.22.refs_2_, ...), custom_call_target="tpu_custom_call" | custom-call | flops 1000 | bytes 1000 | tf_op jit(solution)/shard_map/place/pallas_call | solution.py:309
  132.9 1.7 %final.1 = (bf16[40,1280]{1,0:T(8,128)(2,1)}, f32[32,32]{1,0:T(8,128)}, f32[1,32]{1,0:T(1,128)}, f32[10,128]{1,0:T(8,128)}) custom-call(f32[40,1280]{1,0:T(8,128)} %bitcast.76, bf16[40,1280]{1,0:T(8,128)(2,1)} %bitcast.77, f32[56,128]{1,0:T(8,128)} %copy-done.9, f32[56,128]{1,0:T(8,128)} %copy-done.13, f32[56,128]{1,0:T(8,128)} %copy-done.12, ...), custom_call_target="tpu_custom_call" | custom-call | flops 1000 | bytes 1000 | tf_op jit(solution)/shard_map/final/pallas_call | solution.py:397
  (72 shorter events, 9.1 us)
Async XLA Ops:
  0.6 16.4 %copy-start = (bf16[1280,1280]{1,0:T(8,128)(2,1)S(1)}, bf16[1280,1280]{1,0:T(8,128)(2,1)}, u32[]{:S(2)}) copy-start(bf16[1280,1280]{1,0:T(8,128)(2,1)} %param.9) | copy-start | bytes 9830404
  2.8 32.4 %collective-permute-start.2 = (bf16[8,32,1280]{2,1,0:T(8,128)(2,1)}, bf16[8,32,1280]{2,1,0:T(8,128)(2,1)}, u32[]{:S(2)}, u32[]{:S(2)}) collective-permute-start(bf16[8,32,1280]{2,1,0:T(8,128)(2,1)} %dynamic-slice_bitcast_fusion), channel_id=1, source_target_pairs={{0,2},{1,3},{2,0},{3,1},{4,6},{5,7},{6,4},{7,5},{8,10},{9,11},{10,... | collective-permute-start | bytes 1966088 | tf_op jit(solution)/shard_map/ppermute | solution.py:17
  7.7 27.5 %collective-permute-start.3 = (bf16[8,32,1280]{2,1,0:T(8,128)(2,1)}, bf16[8,32,1280]{2,1,0:T(8,128)(2,1)}, u32[]{:S(2)}, u32[]{:S(2)}) collective-permute-start(bf16[8,32,1280]{2,1,0:T(8,128)(2,1)} %constant_dynamic-slice_fusion.6), channel_id=1, source_target_pairs={{0,3},{1,2},{2,1},{3,0},{4,7},{5,6},{6,5},{7,4},{8,11},{9,10},{10,... | collective-permute-start | bytes 1966088 | tf_op jit(solution)/shard_map/ppermute | solution.py:17
  7.7 4.2 %copy-start.1 = (bf16[1,8,128,1280]{3,2,1,0:T(8,128)(2,1)S(1)}, bf16[1,8,128,1280]{3,2,1,0:T(8,128)(2,1)}, u32[]{:S(2)}) copy-start(bf16[1,8,128,1280]{3,2,1,0:T(8,128)(2,1)} %param.11) | copy-start | bytes 7864324
  9.8 18.2 %collective-permute-start.1 = (bf16[8,32,1280]{2,1,0:T(8,128)(2,1)}, bf16[8,32,1280]{2,1,0:T(8,128)(2,1)}, u32[]{:S(2)}, u32[]{:S(2)}) collective-permute-start(bf16[8,32,1280]{2,1,0:T(8,128)(2,1)} %constant_dynamic-slice_fusion.5), channel_id=1, source_target_pairs={{0,1},{1,0},{2,3},{3,2},{4,5},{5,4},{6,7},{7,6},{8,9},{9,8},{10,11... | collective-permute-start | bytes 1966088 | tf_op jit(solution)/shard_map/ppermute | solution.py:17
  12.8 39.8 %collective-permute-start.5 = (bf16[8,32,1280]{2,1,0:T(8,128)(2,1)}, bf16[8,32,1280]{2,1,0:T(8,128)(2,1)}, u32[]{:S(2)}, u32[]{:S(2)}) collective-permute-start(bf16[8,32,1280]{2,1,0:T(8,128)(2,1)} %constant_dynamic-slice_fusion.3), channel_id=1, source_target_pairs={{0,3},{1,2},{2,1},{3,0},{4,7},{5,6},{6,5},{7,4},{8,11},{9,10},{10,... | collective-permute-start | bytes 1966088 | tf_op jit(solution)/shard_map/ppermute | solution.py:17
  15.4 9.5 %collective-permute-start = (bf16[8,32,1280]{2,1,0:T(8,128)(2,1)}, bf16[8,32,1280]{2,1,0:T(8,128)(2,1)}, u32[]{:S(2)}, u32[]{:S(2)}) collective-permute-start(bf16[8,32,1280]{2,1,0:T(8,128)(2,1)} %constant_dynamic-slice_fusion.2), channel_id=1, source_target_pairs={{0,1},{1,0},{2,3},{3,2},{4,5},{5,4},{6,7},{7,6},{8,9},{9,8},{10,11... | collective-permute-start | bytes 1966088 | tf_op jit(solution)/shard_map/ppermute | solution.py:17
  17.0 1.9 %copy-start.3 = (bf16[8,32,1280]{2,1,0:T(8,128)(2,1)}, bf16[8,32,1280]{2,1,0:T(8,128)(2,1)S(1)}, u32[]{:S(2)}) copy-start(bf16[8,32,1280]{2,1,0:T(8,128)(2,1)S(1)} %constant_dynamic-slice_fusion.1.refs_4_) | copy-start | bytes 1966084
  17.1 2.0 %copy-start.2 = (bf16[1,8,128,1280]{3,2,1,0:T(8,128)(2,1)S(1)}, bf16[1,8,128,1280]{3,2,1,0:T(8,128)(2,1)}, u32[]{:S(2)}) copy-start(bf16[1,8,128,1280]{3,2,1,0:T(8,128)(2,1)} %param.11) | copy-start | bytes 7864324
  24.9 38.8 %collective-permute-start.4 = (bf16[8,32,1280]{2,1,0:T(8,128)(2,1)}, bf16[8,32,1280]{2,1,0:T(8,128)(2,1)}, u32[]{:S(2)}, u32[]{:S(2)}) collective-permute-start(bf16[8,32,1280]{2,1,0:T(8,128)(2,1)} %constant_dynamic-slice_fusion.4), channel_id=1, source_target_pairs={{0,2},{1,3},{2,0},{3,1},{4,6},{5,7},{6,4},{7,5},{8,10},{9,11},{10,... | collective-permute-start | bytes 1966088 | tf_op jit(solution)/shard_map/ppermute | solution.py:17
  28.0 13.7 %copy-start.14 = (f32[1280]{0:T(1024)S(1)}, f32[1280]{0:T(1024)}, u32[]{:S(2)}) copy-start(f32[1280]{0:T(1024)} %param.10) | copy-start | bytes 15364
  41.7 3.0 %copy-start.6 = (bf16[8,32,1280]{2,1,0:T(8,128)(2,1)S(1)}, bf16[8,32,1280]{2,1,0:T(8,128)(2,1)}, u32[]{:S(2)}) copy-start(bf16[8,32,1280]{2,1,0:T(8,128)(2,1)} %get-tuple-element.78.refs_2_) | copy-start | bytes 1966084
  44.8 4.1 %copy-start.5 = (bf16[8,32,1280]{2,1,0:T(8,128)(2,1)S(1)}, bf16[8,32,1280]{2,1,0:T(8,128)(2,1)}, u32[]{:S(2)}) copy-start(bf16[8,32,1280]{2,1,0:T(8,128)(2,1)} %get-tuple-element.77.refs_1_) | copy-start | bytes 1966084
  46.6 37.6 %collective-permute-start.12 = (bf16[8,32,1280]{2,1,0:T(8,128)(2,1)}, bf16[8,32,1280]{2,1,0:T(8,128)(2,1)}, u32[]{:S(2)}, u32[]{:S(2)}) collective-permute-start(bf16[8,32,1280]{2,1,0:T(8,128)(2,1)} %bitcast.24), channel_id=1, source_target_pairs={{0,3},{1,2},{2,1},{3,0},{4,7},{5,6},{6,5},{7,4},{8,11},{9,10},{10,... | collective-permute-start | bytes 1966088 | tf_op jit(solution)/shard_map/ppermute | solution.py:17
  48.9 1.9 %copy-start.4 = (bf16[8,32,1280]{2,1,0:T(8,128)(2,1)S(1)}, bf16[8,32,1280]{2,1,0:T(8,128)(2,1)}, u32[]{:S(2)}) copy-start(bf16[8,32,1280]{2,1,0:T(8,128)(2,1)} %get-tuple-element.75.refs_0_) | copy-start | bytes 1966084
  72.2 2.2 %collective-permute-start.8 = (bf16[8,40,640]{2,1,0:T(8,128)(2,1)}, bf16[8,40,640]{2,1,0:T(8,128)(2,1)}, u32[]{:S(2)}, u32[]{:S(2)}) collective-permute-start(bf16[8,40,640]{2,1,0:T(8,128)(2,1)} %get-tuple-element.90), channel_id=1, source_target_pairs={{0,1},{1,0},{2,3},{3,2},{4,5},{5,4},{6,7},{7,6},{8,9},{9,8},{10,11... | collective-permute-start | bytes 1228808 | tf_op jit(solution)/shard_map/ppermute | solution.py:17
  72.3 2.7 %collective-permute-start.9 = (bf16[8,40,640]{2,1,0:T(8,128)(2,1)}, bf16[8,40,640]{2,1,0:T(8,128)(2,1)}, u32[]{:S(2)}, u32[]{:S(2)}) collective-permute-start(bf16[8,40,640]{2,1,0:T(8,128)(2,1)} %get-tuple-element.92), channel_id=1, source_target_pairs={{0,1},{1,0},{2,3},{3,2},{4,5},{5,4},{6,7},{7,6},{8,9},{9,8},{10,11... | collective-permute-start | bytes 1228808 | tf_op jit(solution)/shard_map/ppermute | solution.py:17
  72.8 4.2 %collective-permute-start.7 = (bf16[8,40,640]{2,1,0:T(8,128)(2,1)}, bf16[8,40,640]{2,1,0:T(8,128)(2,1)}, u32[]{:S(2)}, u32[]{:S(2)}) collective-permute-start(bf16[8,40,640]{2,1,0:T(8,128)(2,1)} %get-tuple-element.89), channel_id=1, source_target_pairs={{0,1},{1,0},{2,3},{3,2},{4,5},{5,4},{6,7},{7,6},{8,9},{9,8},{10,11... | collective-permute-start | bytes 1228808 | tf_op jit(solution)/shard_map/ppermute | solution.py:17
  72.9 4.2 %collective-permute-start.6 = (bf16[8,40,640]{2,1,0:T(8,128)(2,1)}, bf16[8,40,640]{2,1,0:T(8,128)(2,1)}, u32[]{:S(2)}, u32[]{:S(2)}) collective-permute-start(bf16[8,40,640]{2,1,0:T(8,128)(2,1)} %get-tuple-element.87), channel_id=1, source_target_pairs={{0,1},{1,0},{2,3},{3,2},{4,5},{5,4},{6,7},{7,6},{8,9},{9,8},{10,11... | collective-permute-start | bytes 1228808 | tf_op jit(solution)/shard_map/ppermute | solution.py:17
  74.4 18.1 %collective-permute-start.10 = (bf16[8,32,1280]{2,1,0:T(8,128)(2,1)}, bf16[8,32,1280]{2,1,0:T(8,128)(2,1)}, u32[]{:S(2)}, u32[]{:S(2)}) collective-permute-start(bf16[8,32,1280]{2,1,0:T(8,128)(2,1)} %bitcast.81), channel_id=1, source_target_pairs={{0,1},{1,0},{2,3},{3,2},{4,5},{5,4},{6,7},{7,6},{8,9},{9,8},{10,11... | collective-permute-start | bytes 1966088 | tf_op jit(solution)/shard_map/ppermute | solution.py:17
  75.0 18.8 %collective-permute-start.11 = (bf16[8,32,1280]{2,1,0:T(8,128)(2,1)}, bf16[8,32,1280]{2,1,0:T(8,128)(2,1)}, u32[]{:S(2)}, u32[]{:S(2)}) collective-permute-start(bf16[8,32,1280]{2,1,0:T(8,128)(2,1)} %bitcast.80), channel_id=1, source_target_pairs={{0,2},{1,3},{2,0},{3,1},{4,6},{5,7},{6,4},{7,5},{8,10},{9,11},{10,... | collective-permute-start | bytes 1966088 | tf_op jit(solution)/shard_map/ppermute | solution.py:17
  81.1 13.3 %collective-permute-start.13 = (bf16[8,40,640]{2,1,0:T(8,128)(2,1)}, bf16[8,40,640]{2,1,0:T(8,128)(2,1)}, u32[]{:S(2)}, u32[]{:S(2)}) collective-permute-start(bf16[8,40,640]{2,1,0:T(8,128)(2,1)} %get-tuple-element.95), channel_id=1, source_target_pairs={{0,4},{4,0},{8,12},{12,8},{16,20},{20,16},{24,28},{28,24},{1,5},{5... | collective-permute-start | bytes 1228808 | tf_op jit(solution)/shard_map/ppermute | solution.py:17
  82.7 11.7 %collective-permute-start.14 = (bf16[8,40,640]{2,1,0:T(8,128)(2,1)}, bf16[8,40,640]{2,1,0:T(8,128)(2,1)}, u32[]{:S(2)}, u32[]{:S(2)}) collective-permute-start(bf16[8,40,640]{2,1,0:T(8,128)(2,1)} %get-tuple-element.96), channel_id=1, source_target_pairs={{0,8},{4,12},{8,0},{12,4},{16,24},{20,28},{24,16},{28,20},{1,9},{5... | collective-permute-start | bytes 1228808 | tf_op jit(solution)/shard_map/ppermute | solution.py:17
  92.5 10.6 %collective-permute-start.15 = (bf16[8,32,1280]{2,1,0:T(8,128)(2,1)}, bf16[8,32,1280]{2,1,0:T(8,128)(2,1)}, u32[]{:S(2)}, u32[]{:S(2)}) collective-permute-start(bf16[8,32,1280]{2,1,0:T(8,128)(2,1)} %get-tuple-element.99), channel_id=1, source_target_pairs={{0,1},{1,0},{2,3},{3,2},{4,5},{5,4},{6,7},{7,6},{8,9},{9,8},{10,11... | collective-permute-start | bytes 1966088 | tf_op jit(solution)/shard_map/ppermute | solution.py:17
  92.5 33.9 %collective-permute-start.22 = (bf16[8,32,1280]{2,1,0:T(8,128)(2,1)}, bf16[8,32,1280]{2,1,0:T(8,128)(2,1)}, u32[]{:S(2)}, u32[]{:S(2)}) collective-permute-start(bf16[8,32,1280]{2,1,0:T(8,128)(2,1)} %get-tuple-element.100), channel_id=1, source_target_pairs={{0,2},{1,3},{2,0},{3,1},{4,6},{5,7},{6,4},{7,5},{8,10},{9,11},{10,... | collective-permute-start | bytes 1966088 | tf_op jit(solution)/shard_map/ppermute | solution.py:17
  93.8 35.1 %collective-permute-start.23 = (bf16[8,32,1280]{2,1,0:T(8,128)(2,1)}, bf16[8,32,1280]{2,1,0:T(8,128)(2,1)}, u32[]{:S(2)}, u32[]{:S(2)}) collective-permute-start(bf16[8,32,1280]{2,1,0:T(8,128)(2,1)} %get-tuple-element.101), channel_id=1, source_target_pairs={{0,3},{1,2},{2,1},{3,0},{4,7},{5,6},{6,5},{7,4},{8,11},{9,10},{10,... | collective-permute-start | bytes 1966088 | tf_op jit(solution)/shard_map/ppermute | solution.py:17
  97.2 7.5 %collective-permute-start.16 = (bf16[4,40,640]{2,1,0:T(8,128)(2,1)}, bf16[4,40,640]{2,1,0:T(8,128)(2,1)S(1)}, u32[]{:S(2)}, u32[]{:S(2)}) collective-permute-start(bf16[4,40,640]{2,1,0:T(8,128)(2,1)} %get-tuple-element.104), channel_id=1, source_target_pairs={{0,8},{4,12},{8,0},{12,4},{16,24},{20,28},{24,16},{28,20},{1,9},{5... | collective-permute-start | bytes 614408 | tf_op jit(solution)/shard_map/ppermute | solution.py:17
  98.4 7.3 %collective-permute-start.17 = (bf16[4,40,640]{2,1,0:T(8,128)(2,1)}, bf16[4,40,640]{2,1,0:T(8,128)(2,1)}, u32[]{:S(2)}, u32[]{:S(2)}) collective-permute-start(bf16[4,40,640]{2,1,0:T(8,128)(2,1)} %get-tuple-element.105), channel_id=1, source_target_pairs={{0,4},{4,0},{8,12},{12,8},{16,20},{20,16},{24,28},{28,24},{1,5},{5... | collective-permute-start | bytes 614408 | tf_op jit(solution)/shard_map/ppermute | solution.py:17
  104.8 0.9 copy-start.8
  107.9 13.6 %collective-permute-start.21 = (bf16[2,40,1280]{2,1,0:T(8,128)(2,1)}, bf16[2,40,1280]{2,1,0:T(8,128)(2,1)S(1)}, u32[]{:S(2)}, u32[]{:S(2)}) collective-permute-start(bf16[2,40,1280]{2,1,0:T(8,128)(2,1)} %get-tuple-element.110), channel_id=1, source_target_pairs={{0,16},{4,20},{8,24},{12,28},{16,0},{20,4},{24,8},{28,12},{1,17},{... | collective-permute-start | bytes 614408 | tf_op jit(solution)/shard_map/ppermute | solution.py:17
  110.4 1.4 %collective-permute-start.18 = (f32[56,128]{1,0:T(8,128)}, f32[56,128]{1,0:T(8,128)S(1)}, u32[]{:S(2)}, u32[]{:S(2)}) collective-permute-start(f32[56,128]{1,0:T(8,128)} %late_sums.1), channel_id=1, source_target_pairs={{0,1},{1,0},{2,3},{3,2},{4,5},{5,4},{6,7},{7,6},{8,9},{9,8},{10,11... | collective-permute-start | bytes 86024 | tf_op jit(solution)/shard_map/ppermute | solution.py:17
  112.6 4.8 %collective-permute-start.19 = (f32[56,128]{1,0:T(8,128)S(1)}, f32[56,128]{1,0:T(8,128)S(1)}, u32[]{:S(2)}, u32[]{:S(2)}) collective-permute-start(f32[56,128]{1,0:T(8,128)S(1)} %add.60), channel_id=1, source_target_pairs={{0,4},{4,0},{8,12},{12,8},{16,20},{20,16},{24,28},{28,24},{1,5},{5... | collective-permute-start | bytes 86024 | tf_op jit(solution)/shard_map/ppermute | solution.py:17
  117.5 3.9 %collective-permute-start.20 = (f32[56,128]{1,0:T(8,128)S(1)}, f32[56,128]{1,0:T(8,128)S(1)}, u32[]{:S(2)}, u32[]{:S(2)}) collective-permute-start(f32[56,128]{1,0:T(8,128)S(1)} %add.61), channel_id=1, source_target_pairs={{0,8},{4,12},{8,0},{12,4},{16,24},{20,28},{24,16},{28,20},{1,9},{5... | collective-permute-start | bytes 86024 | tf_op jit(solution)/shard_map/ppermute | solution.py:17
  121.4 10.8 %copy-start.9 = (f32[56,128]{1,0:T(8,128)}, f32[56,128]{1,0:T(8,128)S(1)}, u32[]{:S(2)}) copy-start(f32[56,128]{1,0:T(8,128)S(1)} %add.62.refs_0_) | copy-start | bytes 86020
  121.4 0.7 copy-start.7
  123.9 8.3 %collective-permute-start.24 = (bf16[1,40,1280]{2,1,0:T(8,128)(2,1)}, bf16[1,40,1280]{2,1,0:T(8,128)(2,1)S(1)}, u32[]{:S(2)}, u32[]{:S(2)}) collective-permute-start(bf16[1,40,1280]{2,1,0:T(8,128)(2,1)} %get-tuple-element.116), channel_id=1, source_target_pairs={{0,2},{1,3},{2,0},{3,1},{4,6},{5,7},{6,4},{7,5},{8,10},{9,11},{10,... | collective-permute-start | bytes 307208 | tf_op jit(solution)/shard_map/ppermute | solution.py:17
  124.5 7.7 %collective-permute-start.27 = (f32[56,128]{1,0:T(8,128)S(1)}, f32[56,128]{1,0:T(8,128)S(1)}, u32[]{:S(2)}, u32[]{:S(2)}) collective-permute-start(f32[56,128]{1,0:T(8,128)S(1)} %add.62.refs_0_), channel_id=1, source_target_pairs={{0,18},{1,19},{2,16},{3,17},{4,22},{5,23},{6,20},{7,21},{8,26},{9,... | collective-permute-start | bytes 86024 | tf_op jit(solution)/shard_map/ppermute | solution.py:17
  125.7 6.5 %collective-permute-start.26 = (f32[56,128]{1,0:T(8,128)S(1)}, f32[56,128]{1,0:T(8,128)S(1)}, u32[]{:S(2)}, u32[]{:S(2)}) collective-permute-start(f32[56,128]{1,0:T(8,128)S(1)} %add.62.refs_0_), channel_id=1, source_target_pairs={{0,2},{1,3},{2,0},{3,1},{4,6},{5,7},{6,4},{7,5},{8,10},{9,11},{10,... | collective-permute-start | bytes 86024 | tf_op jit(solution)/shard_map/ppermute | solution.py:17
  126.4 5.8 %collective-permute-start.25 = (f32[56,128]{1,0:T(8,128)S(1)}, f32[56,128]{1,0:T(8,128)S(1)}, u32[]{:S(2)}, u32[]{:S(2)}) collective-permute-start(f32[56,128]{1,0:T(8,128)S(1)} %add.62.refs_0_), channel_id=1, source_target_pairs={{0,16},{4,20},{8,24},{12,28},{16,0},{20,4},{24,8},{28,12},{1,17},{... | collective-permute-start | bytes 86024 | tf_op jit(solution)/shard_map/ppermute | solution.py:17
  132.2 0.6 copy-start.11
  132.2 0.6 copy-start.12
  132.2 0.6 copy-start.13
  132.2 0.7 copy-start.10

commit v6 on v5

--- a/solution.py
+++ b/solution.py
@@ -113,14 +113,29 @@
     return high, (mg - high.astype(jnp.float32)).astype(jnp.bfloat16)
 
 
-def backward_kernel(parts, kron_ref, surrogate_ref, *refs):
-    grads, outs = refs[:parts], refs[parts:]
-    steps, group, width = grads[0].shape
+def backward_kernel(parts, kron_ref, surrogate_ref, weight_ref, cot_ref, *refs):
+    others, outs, last_ref = refs[: parts - 1], refs[parts - 1 : -1], refs[-1]
+    steps, group, width = others[0].shape
     rows = steps * group
+
+    @pl.when(pl.program_id(0) == 0)
+    def _():
+        grad = lax.dot_general(
+            cot_ref[...].reshape(-1, width),
+            weight_ref[...],
+            (((1,), (1,)), ((), ())),
+            preferred_element_type=jnp.float32,
+        )
+        last_ref[...] = grad.astype(jnp.bfloat16).reshape(last_ref.shape)
+
+    here = pl.ds(pl.multiple_of(pl.program_id(0) * group, group), group)
     kron = kron_ref[...]
     tile = 256
     for at in range(0, width, tile):
-        mg = rows_of(grads, at, tile).astype(jnp.float32) * surrogate_ref[0, :, at : at + tile]
+        spike_grads = [r[:, :, at : at + tile].reshape(rows, tile) for r in others]
+        spike_grads.insert(2, last_ref[:, here, at : at + tile].reshape(rows, tile))
+        mg = jnp.concatenate(spike_grads, axis=0).astype(jnp.float32)
+        mg = mg * surrogate_ref[0, :, at : at + tile]
         grad = jnp.dot(kron, mg.astype(jnp.bfloat16), preferred_element_type=jnp.float32)
         grad = grad.astype(jnp.bfloat16)
         for k in range(parts):
@@ -129,28 +144,32 @@
             )
 
 
-def backward(kron, surrogate, grads):
-    parts = len(grads)
-    steps, tokens, width = grads[0].shape
+def backward(kron, surrogate, weight, cot, others):
+    parts = len(others) + 1
+    steps, tokens, width = cot.shape
     rows = parts * steps * GROUP
     piece = pl.BlockSpec((steps, GROUP, width), lambda g: (0, g, 0))
-    return pl.pallas_call(
+    fixed = pl.BlockSpec(cot.shape, lambda g: (0, 0, 0))
+    found = pl.pallas_call(
         functools.partial(backward_kernel, parts),
         grid=(tokens // GROUP,),
         in_specs=[
             pl.BlockSpec(kron.shape, lambda g: (0, 0)),
             pl.BlockSpec((1, rows, width), lambda g: (g, 0, 0)),
+            pl.BlockSpec(weight.shape, lambda g: (0, 0)),
+            fixed,
         ]
-        + [piece] * parts,
-        out_specs=[piece] * parts,
-        out_shape=[jax.ShapeDtypeStruct((steps, tokens, width), jnp.bfloat16)] * parts,
+        + [piece] * (parts - 1),
+        out_specs=[piece] * parts + [fixed],
+        out_shape=[jax.ShapeDtypeStruct((steps, tokens, width), jnp.bfloat16)] * (parts + 1),
         cost_estimate=pl.CostEstimate(
-            flops=2 * rows * rows * width * (tokens // GROUP),
+            flops=5 * rows * rows * width * (tokens // GROUP),
             bytes_accessed=2 * rows * width * (tokens // GROUP),
             transcendentals=0,
         ),
         name="backward",
-    )(kron, surrogate, *grads)
+    )(kron, surrogate, weight, cot, *others)
+    return list(found[:parts]), found[parts]
 
 
 def cross_of(grads, surrogate, sources, cross_ref, tsum_ref, both_ref):
@@ -558,8 +577,13 @@
     bits = [route[0] for route in routes]
     pairs, lefts = step(state, [left, left], bits)
     state = travel(pairs, bits)
-    grads[2] = spike_grad(after(cots[2], outs_in[-1], *[send for _, send in pairs]))
-    cgrads = list(backward(kron_bwd, surrogate, grads))
+    cgrads, grads[2] = backward(
+        kron_bwd,
+        surrogate,
+        weight,
+        after(cots[2], outs_in[-1], *[send for _, send in pairs]),
+        [grads[k] for k in others],
+    )
     cgrads_in = exchange(cgrads)
 
     def meet(sums, *bits):

time: 135 us -> 136 us (level)
  Pallas kernels: 52.7 us -> 54.9 us
  local copies, waits for them, and re-layouts: 15.1 us -> 13.1 us
  matrix products: 19.5 us -> 21 us
    dynamic_slice x8, local copies, waits for them, and re-layouts: 13.1 us -> 8.57 us  [cut(): found[k] = lax.dynamic_slice_in_dim(value, (me ^ k) * share, share, axis=1)]
    unnamed x30 -> x38, local copies, waits for them, and re-layouts: 1.41 us -> 3.94 us
    pallas_call x1, Pallas kernels: 5.29 us -> 7.68 us  [backward(): pl.pallas_call(functools.partial(backward_kernel, parts), grid=(tokens //...]
    dot_general x4 -> x3, matrix products: 10.9 us -> 11.1 us  [spike_grad(): jnp.einsum('re,de->rd', flat(cot), weight, preferred_element_type=jnp.flo...]
  transfers between devices with their start and end apart: 28 -> 28, of which waited for: 8 -> 7; matrix products, arithmetic and copies ran while one was open for 24% -> 23% of each run, Pallas kernels for 38% -> 39%
where the time goes in v6:
time: 136 us; the launch traced here: 135 us
  Pallas kernels  54.9 us (40%)
  starting transfers between devices  26.9 us (20%)
  matrix products  21 us (15%)
  waiting for transfers between devices  16.4 us (12%)
  local copies, waits for them, and re-layouts  13.1 us (10%)
  other arithmetic  1.79 us (1%)
    ppermute x28, starting transfers between devices, xor_permute(): return lax.ppermute(value, axis, [(i, i ^ mask) for i in range(size)])  26.9 us
    ppermute x28, waiting for transfers between devices, xor_permute(): return lax.ppermute(value, axis, [(i, i ^ mask) for i in range(size)])  16.4 us
    dot_general x3, matrix products, spike_grad(): jnp.einsum('re,de->rd', flat(cot), weight, preferred_element_type=jnp.flo...  11.1 us
    pallas_call x2, Pallas kernels, small_sums(): pl.pallas_call(functools.partial(late_kernel if late else early_kernel, p...  11 us
    pallas_call x4, Pallas kernels, combine(): pl.pallas_call(functools.partial(combine_kernel, tuple(shapes), counts, l...  10.9 us
    dot_general x4, matrix products, body(): jnp.dot(flat(spikes[k]), weight, preferred_element_type=jnp.float32) + bias  9.88 us
    dynamic_slice x8, local copies, waits for them, and re-layouts, cut(): found[k] = lax.dynamic_slice_in_dim(value, (me ^ k) * share, share, axis=1)  8.57 us
    pallas_call x1, Pallas kernels, weight_halves(): pl.pallas_call(functools.partial(weight_kernel, shard, len(spikes)), grid...  8.53 us
  transfers between devices with their start and end apart: 28, of which 7 were waited for; matrix products, arithmetic and copies ran while one was open for 23% of the time, Pallas kernels for 39%

profile of v6, /device:TPU:0, one launch (start us, length us, event | category | flops | bytes accessed | tf_op | source)
XLA Modules:
  0.0 135.0 jit_solution(9736250643582076805)
XLA Ops:
  0.7 1.7 %copy-done = bf16[1,8,128,1280]{3,2,1,0:T(8,128)(2,1)S(1)} copy-done((bf16[1,8,128,1280]{3,2,1,0:T(8,128)(2,1)S(1)}, bf16[1,8,128,1280]{3,2,1,0:T(8,128)(2,1)}, u32[]{:S(2)}) %copy-start) | copy-done | bytes 2621464
  2.4 0.9 dynamic-slice_bitcast_fusion
  3.3 2.9 %collective-permute-start.2 = (bf16[8,32,1280]{2,1,0:T(8,128)(2,1)}, bf16[8,32,1280]{2,1,0:T(8,128)(2,1)S(1)}, u32[]{:S(2)}, u32[]{:S(2)}) collective-permute-start(bf16[8,32,1280]{2,1,0:T(8,128)(2,1)} %dynamic-slice_bitcast_fusion), channel_id=1, source_target_pairs={{0,2},{1,3},{2,0},{3,1},{4,6},{5,7},{6,4},{7,5},{8,10},{9,11},{10,... | collective-permute-start | bytes 1966088 | tf_op jit(solution)/shard_map/ppermute | solution.py:17
  6.2 0.9 constant_dynamic-slice_fusion.6
  7.1 0.9 constant_dynamic-slice_fusion.5
  8.1 2.0 %constant_dynamic-slice_fusion.4 = bf16[8,32,1280]{2,1,0:T(8,128)(2,1)} fusion(bf16[8,128,1280]{2,1,0:T(8,128)(2,1)} %bitcast.52, s32[]{:T(128)S(6)} %select_n.16), kind=kLoop, calls=%fused_computation.17 | loop fusion | bytes 1310724 | tf_op jit(solution)/shard_map/dynamic_slice | solution.py:501
  10.2 0.9 constant_dynamic-slice_fusion.3
  11.1 1.7 %collective-permute-start.5 = (bf16[8,32,1280]{2,1,0:T(8,128)(2,1)}, bf16[8,32,1280]{2,1,0:T(8,128)(2,1)}, u32[]{:S(2)}, u32[]{:S(2)}) collective-permute-start(bf16[8,32,1280]{2,1,0:T(8,128)(2,1)} %constant_dynamic-slice_fusion.3), channel_id=1, source_target_pairs={{0,3},{1,2},{2,1},{3,0},{4,7},{5,6},{6,5},{7,4},{8,11},{9,10},{10,... | collective-permute-start | bytes 1966088 | tf_op jit(solution)/shard_map/ppermute | solution.py:17
  12.8 0.9 constant_dynamic-slice_fusion.2
  14.1 1.1 constant_dynamic-slice_fusion.1.refs_4_
  15.2 4.1 %convolution_convert_fusion.2 = bf16[256,1280]{1,0:T(8,128)(2,1)} fusion(bf16[256,1280]{1,0:T(8,128)(2,1)S(1)} %bitcast.58, bf16[1280,1280]{1,0:T(8,128)(2,1)} %weight_ref.1), kind=kOutput, calls=%fused_computation.11 | convolution fusion | flops 839188480 | bytes 4587520 | tf_op jit(solution)/shard_map/re,de->rd/dot_general | solution.py:512
  19.3 1.0 convert_reduce_fusion
  21.0 2.3 %build_krons.1 = (bf16[512,512]{1,0:T(8,128)(2,1)}, bf16[512,512]{1,0:T(8,128)(2,1)}, f32[512,1]{1,0:T(8,128)}) custom-call(s32[10]{0:T(128)} %stack.40.me_ref.info_ref, f32[32,32]{1,0:T(8,128)} %mixing_ref.1, f32[1,32]{1,0:T(1,128)} %bitcast.73), custom_call_target="tpu_custom_call" | custom-call | tf_op jit(solution)/shard_map/build_krons/pallas_call | solution.py:60
  23.3 0.9 constant_dynamic-slice_fusion.refs_0_
  24.3 4.1 %convolution_convert_fusion.1 = bf16[256,1280]{1,0:T(8,128)(2,1)} fusion(bf16[256,1280]{1,0:T(8,128)(2,1)} %bitcast.15, bf16[1280,1280]{1,0:T(8,128)(2,1)} %weight_ref.1), kind=kOutput, calls=%fused_computation.10 | convolution fusion | flops 839188480 | bytes 4587520 | tf_op jit(solution)/shard_map/re,de->rd/dot_general | solution.py:512
  28.3 7.4 %collective-permute-done.3.refs_3_ = bf16[8,32,1280]{2,1,0:T(8,128)(2,1)} collective-permute-done((bf16[8,32,1280]{2,1,0:T(8,128)(2,1)}, bf16[8,32,1280]{2,1,0:T(8,128)(2,1)}, u32[]{:S(2)}, u32[]{:S(2)}) %collective-permute-start.3) | collective-permute-done | bytes 655392 | tf_op jit(solution)/shard_map/ppermute | solution.py:17
  36.6 6.2 %forward.1 = (bf16[8,32,1280]{2,1,0:T(8,128)(2,1)}, bf16[8,32,1280]{2,1,0:T(8,128)(2,1)}, bf16[8,32,1280]{2,1,0:T(8,128)(2,1)}, bf16[8,32,1280]{2,1,0:T(8,128)(2,1)}, f32[2,512,1280]{2,1,0:T(8,128)}) custom-call(bf16[512,512]{1,0:T(8,128)(2,1)} %get-tuple-element.66.kron_ref, f32[512,1]{1,0:T(8,128)} %get-tuple-element.74.thr_ref, ...), custom_call_target="tpu_custom_call" | custom-call | tf_op jit(solution)/shard_map/forward/pallas_call | solution.py:99
  42.8 4.2 %fusion.3 = bf16[256,1280]{1,0:T(8,128)(2,1)} fusion(bf16[256,1280]{1,0:T(8,128)(2,1)} %bitcast.69, bf16[1280,1280]{1,0:T(8,128)(2,1)} %weight_ref.1, f32[1280]{0:T(1024)S(1)} %copy-done.18), kind=kOutput, calls=%fused_computation.8 | convolution fusion | flops 839516160 | bytes 4592640 | tf_op jit(solution)/shard_map/dot_general | solution.py:519
  47.0 1.9 %fusion.2 = bf16[256,1280]{1,0:T(8,128)(2,1)} fusion(bf16[256,1280]{1,0:T(8,128)(2,1)S(1)} %bitcast.68, bf16[1280,1280]{1,0:T(8,128)(2,1)S(1)} %copy-done.17, f32[1280]{0:T(1024)S(1)} %copy-done.18), kind=kOutput, calls=%fused_computation.7 | convolution fusion | flops 839516160 | bytes 4592640 | tf_op jit(solution)/shard_map/dot_general | solution.py:519
  48.9 2.2 %collective-permute-start.12 = (bf16[8,32,1280]{2,1,0:T(8,128)(2,1)}, bf16[8,32,1280]{2,1,0:T(8,128)(2,1)S(1)}, u32[]{:S(2)}, u32[]{:S(2)}) collective-permute-start(bf16[8,32,1280]{2,1,0:T(8,128)(2,1)} %bitcast.24), channel_id=1, source_target_pairs={{0,3},{1,2},{2,1},{3,0},{4,7},{5,6},{6,5},{7,4},{8,11},{9,10},{10,... | collective-permute-start | bytes 1966088 | tf_op jit(solution)/shard_map/ppermute | solution.py:17
  51.1 1.9 %fusion.1 = bf16[256,1280]{1,0:T(8,128)(2,1)} fusion(bf16[256,1280]{1,0:T(8,128)(2,1)S(1)} %bitcast.67, bf16[1280,1280]{1,0:T(8,128)(2,1)S(1)} %copy-done.17, f32[1280]{0:T(1024)S(1)} %copy-done.18), kind=kOutput, calls=%fused_computation.6 | convolution fusion | flops 839516160 | bytes 4592640 | tf_op jit(solution)/shard_map/dot_general | solution.py:519
  53.0 1.9 %fusion = bf16[256,1280]{1,0:T(8,128)(2,1)} fusion(bf16[256,1280]{1,0:T(8,128)(2,1)S(1)} %bitcast.66, bf16[1280,1280]{1,0:T(8,128)(2,1)S(1)} %copy-done.17, f32[1280]{0:T(1024)S(1)} %copy-done.18), kind=kOutput, calls=%fused_computation.5 | convolution fusion | flops 839516160 | bytes 4592640 | tf_op jit(solution)/shard_map/dot_general | solution.py:519
  54.9 3.0 %convolution_convert_fusion = bf16[256,1280]{1,0:T(8,128)(2,1)} fusion(bf16[256,1280]{1,0:T(8,128)(2,1)} %bitcast.26, bf16[1280,1280]{1,0:T(8,128)(2,1)S(1)} %copy-done.17), kind=kOutput, calls=%fused_computation.9 | convolution fusion | flops 839188480 | bytes 4587520 | tf_op jit(solution)/shard_map/re,de->rd/dot_general | solution.py:512
  57.9 6.9 %early_sums.1.early_ref = f32[56,128]{1,0:T(8,128)} custom-call(s32[10]{0:T(128)} %stack.40.me_ref.info_ref, f32[2,512,1280]{2,1,0:T(8,128)} %get-tuple-element.107.surrogate_ref, f32[10,128]{1,0:T(8,128)} %bitcast.72, bf16[8,32,1280]{2,1,0:T(8,128)(2,1)} %constant_dynamic-slice_fusion.refs_0_, bf16[8,32,1280]{2,1,0:T(8,128)(2,1)} %collective-permute-done.1.refs_1_, ...), custom_call_target="tpu_custom_call" | custom-call | flops 1000 | bytes 1000 | tf_op jit(solution)/shard_map/early_sums/pallas_call | solution.py:285
  64.8 8.5 %weight_halves.1 = (f32[16,40,640]{2,1,0:T(8,128)}, f32[16,40,640]{2,1,0:T(8,128)}, bf16[8,40,640]{2,1,0:T(8,128)(2,1)}, bf16[8,40,640]{2,1,0:T(8,128)(2,1)}, bf...) custom-call(s32[10]{0:T(128)} %stack.40.me_ref.info_ref, bf16[8,32,1280]{2,1,0:T(8,128)(2,1)} %get-tuple-element.76.refs_0_, ...), custom_call_target="tpu_custom_call" | custom-call | flops 1000 | bytes 1000 | tf_op jit(solution)/shard_map/weight_halves/pallas_call | solution.py:463
  74.4 1.1 collective-permute-done.8.refs_4_
  76.1 1.5 %collective-permute-start.11 = (bf16[8,32,1280]{2,1,0:T(8,128)(2,1)}, bf16[8,32,1280]{2,1,0:T(8,128)(2,1)}, u32[]{:S(2)}, u32[]{:S(2)}) collective-permute-start(bf16[8,32,1280]{2,1,0:T(8,128)(2,1)} %bitcast.74), channel_id=1, source_target_pairs={{0,2},{1,3},{2,0},{3,1},{4,6},{5,7},{6,4},{7,5},{8,10},{9,11},{10,... | collective-permute-start | bytes 1966088 | tf_op jit(solution)/shard_map/ppermute | solution.py:17
  77.5 4.1 %combine.4 = (f32[8,40,640]{2,1,0:T(8,128)}, bf16[8,40,640]{2,1,0:T(8,128)(2,1)}, f32[8,40,640]{2,1,0:T(8,128)}, bf16[8,40,640]{2,1,0:T(8,128)(2,1)}) custom-call(s32[10]{0:T(128)} %stack.40.me_ref.info_ref, f32[16,40,640]{2,1,0:T(8,128)} %get-tuple-element.84.refs_0_, f32[16,40,640]{2,1,0:T(8,128)} %get-tuple-element.85.refs_1_, ...), custom_call_target="tpu_custom_call" | custom-call | flops 1000 | bytes 1000 | tf_op jit(solution)/shard_map/combine/pallas_call | solution.py:391
  81.6 1.5 %collective-permute-start.13 = (bf16[8,40,640]{2,1,0:T(8,128)(2,1)}, bf16[8,40,640]{2,1,0:T(8,128)(2,1)}, u32[]{:S(2)}, u32[]{:S(2)}) collective-permute-start(bf16[8,40,640]{2,1,0:T(8,128)(2,1)} %get-tuple-element.96), channel_id=1, source_target_pairs={{0,4},{4,0},{8,12},{12,8},{16,20},{20,16},{24,28},{28,24},{1,5},{5... | collective-permute-start | bytes 1228808 | tf_op jit(solution)/shard_map/ppermute | solution.py:17
  83.2 1.6 %collective-permute-start.14 = (bf16[8,40,640]{2,1,0:T(8,128)(2,1)}, bf16[8,40,640]{2,1,0:T(8,128)(2,1)}, u32[]{:S(2)}, u32[]{:S(2)}) collective-permute-start(bf16[8,40,640]{2,1,0:T(8,128)(2,1)} %get-tuple-element.97), channel_id=1, source_target_pairs={{0,8},{4,12},{8,0},{12,4},{16,24},{20,28},{24,16},{28,20},{1,9},{5... | collective-permute-start | bytes 1228808 | tf_op jit(solution)/shard_map/ppermute | solution.py:17
  84.7 7.7 %backward.1 = (bf16[8,32,1280]{2,1,0:T(8,128)(2,1)}, bf16[8,32,1280]{2,1,0:T(8,128)(2,1)}, bf16[8,32,1280]{2,1,0:T(8,128)(2,1)}, bf16[8,32,1280]{2,1,0:T(8,128)(2,1)}, bf16[8,32,1280]{2,1,0:T(8,128)(2,1)}) custom-call(bf16[512,512]{1,0:T(8,128)(2,1)} %get-tuple-element.95.kron_ref, f32[2,512,1280]{2,1,0:T(8,128)} %get-tuple-element.107.surrogate_ref, ...), custom_call_target="tpu_custom_call" | custom-call | flops 3355443200 | bytes 2621440 | tf_op jit(solution)/shard_map/backward/pallas_call | solution.py:153
  92.5 1.2 collective-permute-start.22
  94.4 2.8 %combine.5 = (f32[4,40,640]{2,1,0:T(8,128)}, bf16[4,40,640]{2,1,0:T(8,128)(2,1)}, f32[4,40,640]{2,1,0:T(8,128)}, bf16[4,40,640]{2,1,0:T(8,128)(2,1)}) custom-call(s32[10]{0:T(128)} %stack.40.me_ref.info_ref, f32[8,40,640]{2,1,0:T(8,128)} %get-tuple-element.103.refs_0_, f32[8,40,640]{2,1,0:T(8,128)} %get-tuple-element.104.refs_1_, ...), custom_call_target="tpu_custom_call" | custom-call | flops 1000 | bytes 1000 | tf_op jit(solution)/shard_map/combine/pallas_call | solution.py:391
  97.2 1.6 %collective-permute-start.16 = (bf16[4,40,640]{2,1,0:T(8,128)(2,1)}, bf16[4,40,640]{2,1,0:T(8,128)(2,1)S(1)}, u32[]{:S(2)}, u32[]{:S(2)}) collective-permute-start(bf16[4,40,640]{2,1,0:T(8,128)(2,1)} %get-tuple-element.105), channel_id=1, source_target_pairs={{0,8},{4,12},{8,0},{12,4},{16,24},{20,28},{24,16},{28,20},{1,9},{5... | collective-permute-start | bytes 614408 | tf_op jit(solution)/shard_map/ppermute | solution.py:17
  99.5 4.1 %late_sums.1 = f32[56,128]{1,0:T(8,128)} custom-call(s32[10]{0:T(128)} %stack.40.me_ref.info_ref, f32[2,512,1280]{2,1,0:T(8,128)} %get-tuple-element.107.surrogate_ref, f32[56,128]{1,0:T(8,128)} %early_sums.1.early_ref, bf16[8,32,1280]{2,1,0:T(8,128)(2,1)} %constant_dynamic-slice_fusion.refs_0_, bf16[8,32,1280]{2,1,0:T(8,128)(2,1)} %collective-permute-done.1.refs_1_, ...), custom_call_target="tpu_custom_call" | custom-call | flops 5368709120 | bytes 10485760 | tf_op jit(solution)/shard_map/late_sums/pallas_call | solution.py:285
  103.6 1.2 collective-permute-done.16.refs_2_
  104.8 1.4 %collective-permute-done.17.refs_3_ = bf16[4,40,640]{2,1,0:T(8,128)(2,1)} collective-permute-done((bf16[4,40,640]{2,1,0:T(8,128)(2,1)}, bf16[4,40,640]{2,1,0:T(8,128)(2,1)}, u32[]{:S(2)}, u32[]{:S(2)}) %collective-permute-start.17) | collective-permute-done | bytes 204832 | tf_op jit(solution)/shard_map/ppermute | solution.py:17
  106.2 2.2 %combine.6 = (f32[2,40,1280]{2,1,0:T(8,128)}, bf16[2,40,1280]{2,1,0:T(8,128)(2,1)}) custom-call(s32[10]{0:T(128)} %stack.40.me_ref.info_ref, f32[4,40,640]{2,1,0:T(8,128)} %get-tuple-element.110.refs_0_, f32[4,40,640]{2,1,0:T(8,128)} %get-tuple-element.111.refs_1_, bf16[4,40,640]{2,1,0:T(8,128)(2,1)} %copy-done.11, ...), custom_call_target="tpu_custom_call" | custom-call | flops 1000 | bytes 1000 | tf_op jit(solution)/shard_map/combine/pallas_call | solution.py:391
  108.3 2.6 %collective-permute-start.21 = (bf16[2,40,1280]{2,1,0:T(8,128)(2,1)}, bf16[2,40,1280]{2,1,0:T(8,128)(2,1)S(1)}, u32[]{:S(2)}, u32[]{:S(2)}) collective-permute-start(bf16[2,40,1280]{2,1,0:T(8,128)(2,1)} %get-tuple-element.112), channel_id=1, source_target_pairs={{0,16},{4,20},{8,24},{12,28},{16,0},{20,4},{24,8},{28,12},{1,17},{... | collective-permute-start | bytes 614408 | tf_op jit(solution)/shard_map/ppermute | solution.py:17
  110.9 1.4 %collective-permute-done.18 = f32[56,128]{1,0:T(8,128)S(1)} collective-permute-done((f32[56,128]{1,0:T(8,128)}, f32[56,128]{1,0:T(8,128)S(1)}, u32[]{:S(2)}, u32[]{:S(2)}) %collective-permute-start.18) | collective-permute-done | bytes 28704 | tf_op jit(solution)/shard_map/ppermute | solution.py:17
  113.1 1.5 %collective-permute-start.19 = (f32[56,128]{1,0:T(8,128)S(1)}, f32[56,128]{1,0:T(8,128)S(1)}, u32[]{:S(2)}, u32[]{:S(2)}) collective-permute-start(f32[56,128]{1,0:T(8,128)S(1)} %add.60), channel_id=1, source_target_pairs={{0,4},{4,0},{8,12},{12,8},{16,20},{20,16},{24,28},{28,24},{1,5},{5... | collective-permute-start | bytes 86024 | tf_op jit(solution)/shard_map/ppermute | solution.py:17
  114.6 3.3 %place.2 = bf16[8,128,1280]{2,1,0:T(8,128)(2,1)} custom-call(s32[10]{0:T(128)} %stack.40.me_ref.info_ref, bf16[8,32,1280]{2,1,0:T(8,128)(2,1)} %bitcast.65, bf16[8,32,1280]{2,1,0:T(8,128)(2,1)} %collective-permute-done.10.refs_1_, bf16[8,32,1280]{2,1,0:T(8,128)(2,1)} %collective-permute-done.11.refs_2_, bf16[8,32,1280]{2,1,0:T(8,128)(2,1)} %copy-done.5), custom_call_target="tpu_custom_call" | custom-call | flops 1000 | bytes 1000 | tf_op jit(solution)/shard_map/place/pallas_call | solution.py:328
  118.5 3.4 %collective-permute-done.20 = f32[56,128]{1,0:T(8,128)S(1)} collective-permute-done((f32[56,128]{1,0:T(8,128)S(1)}, f32[56,128]{1,0:T(8,128)S(1)}, u32[]{:S(2)}, u32[]{:S(2)}) %collective-permute-start.20) | collective-permute-done | bytes 28704 | tf_op jit(solution)/shard_map/ppermute | solution.py:17
  122.6 1.8 %combine.7 = (f32[1,40,1280]{2,1,0:T(8,128)}, bf16[1,40,1280]{2,1,0:T(8,128)(2,1)}) custom-call(s32[10]{0:T(128)} %stack.40.me_ref.info_ref, f32[2,40,1280]{2,1,0:T(8,128)} %get-tuple-element.117.refs_0_, bf16[2,40,1280]{2,1,0:T(8,128)(2,1)} %copy-done.10), custom_call_target="tpu_custom_call" | custom-call | flops 1000 | bytes 1000 | tf_op jit(solution)/shard_map/combine/pallas_call | solution.py:391
  124.9 1.2 collective-permute-start.27
  126.8 2.6 %collective-permute-start.25 = (f32[56,128]{1,0:T(8,128)S(1)}, f32[56,128]{1,0:T(8,128)S(1)}, u32[]{:S(2)}, u32[]{:S(2)}) collective-permute-start(f32[56,128]{1,0:T(8,128)S(1)} %add.62.refs_0_), channel_id=1, source_target_pairs={{0,16},{4,20},{8,24},{12,28},{16,0},{20,4},{24,8},{28,12},{1,17},{... | collective-permute-start | bytes 86024 | tf_op jit(solution)/shard_map/ppermute | solution.py:17
  129.3 3.3 %place.3 = bf16[8,128,1280]{2,1,0:T(8,128)(2,1)} custom-call(s32[10]{0:T(128)} %stack.40.me_ref.info_ref, bf16[8,32,1280]{2,1,0:T(8,128)(2,1)} %get-tuple-element.119.refs_0_, bf16[8,32,1280]{2,1,0:T(8,128)(2,1)} %copy-done.6, bf16[8,32,1280]{2,1,0:T(8,128)(2,1)} %collective-permute-done.22.refs_2_, bf16[8,32,1280]{2,1,0:T(8,128)(2,1)} %collective-permute-done.23.refs_3_), custom_call_target="tpu_custom_call" | custom-call | flops 1000 | bytes 1000 | tf_op jit(solution)/shard_map/place/pallas_call | solution.py:328
  133.4 1.7 %final.1 = (bf16[40,1280]{1,0:T(8,128)(2,1)}, f32[32,32]{1,0:T(8,128)}, f32[1,32]{1,0:T(1,128)}, f32[10,128]{1,0:T(8,128)}) custom-call(f32[40,1280]{1,0:T(8,128)} %bitcast.70, bf16[40,1280]{1,0:T(8,128)(2,1)} %bitcast.71, f32[56,128]{1,0:T(8,128)} %copy-done.12, f32[56,128]{1,0:T(8,128)} %copy-done.16, f32[56,128]{1,0:T(8,128)} %copy-done.15, ...), custom_call_target="tpu_custom_call" | custom-call | flops 1000 | bytes 1000 | tf_op jit(solution)/shard_map/final/pallas_call | solution.py:416
  (79 shorter events, 8.8 us)
Async XLA Ops:
  0.6 1.7 %copy-start = (bf16[1,8,128,1280]{3,2,1,0:T(8,128)(2,1)S(1)}, bf16[1,8,128,1280]{3,2,1,0:T(8,128)(2,1)}, u32[]{:S(2)}) copy-start(bf16[1,8,128,1280]{3,2,1,0:T(8,128)(2,1)} %param.6) | copy-start | bytes 7864324
  3.3 32.4 %collective-permute-start.2 = (bf16[8,32,1280]{2,1,0:T(8,128)(2,1)}, bf16[8,32,1280]{2,1,0:T(8,128)(2,1)S(1)}, u32[]{:S(2)}, u32[]{:S(2)}) collective-permute-start(bf16[8,32,1280]{2,1,0:T(8,128)(2,1)} %dynamic-slice_bitcast_fusion), channel_id=1, source_target_pairs={{0,2},{1,3},{2,0},{3,1},{4,6},{5,7},{6,4},{7,5},{8,10},{9,11},{10,... | collective-permute-start | bytes 1966088 | tf_op jit(solution)/shard_map/ppermute | solution.py:17
  7.1 28.6 %collective-permute-start.3 = (bf16[8,32,1280]{2,1,0:T(8,128)(2,1)}, bf16[8,32,1280]{2,1,0:T(8,128)(2,1)}, u32[]{:S(2)}, u32[]{:S(2)}) collective-permute-start(bf16[8,32,1280]{2,1,0:T(8,128)(2,1)} %constant_dynamic-slice_fusion.6), channel_id=1, source_target_pairs={{0,3},{1,2},{2,1},{3,0},{4,7},{5,6},{6,5},{7,4},{8,11},{9,10},{10,... | collective-permute-start | bytes 1966088 | tf_op jit(solution)/shard_map/ppermute | solution.py:17
  7.1 3.0 %copy-start.1 = (bf16[1,8,128,1280]{3,2,1,0:T(8,128)(2,1)S(1)}, bf16[1,8,128,1280]{3,2,1,0:T(8,128)(2,1)}, u32[]{:S(2)}) copy-start(bf16[1,8,128,1280]{3,2,1,0:T(8,128)(2,1)} %param.11) | copy-start | bytes 7864324
  8.0 20.3 %collective-permute-start.1 = (bf16[8,32,1280]{2,1,0:T(8,128)(2,1)}, bf16[8,32,1280]{2,1,0:T(8,128)(2,1)}, u32[]{:S(2)}, u32[]{:S(2)}) collective-permute-start(bf16[8,32,1280]{2,1,0:T(8,128)(2,1)} %constant_dynamic-slice_fusion.5), channel_id=1, source_target_pairs={{0,1},{1,0},{2,3},{3,2},{4,5},{5,4},{6,7},{7,6},{8,9},{9,8},{10,11... | collective-permute-start | bytes 1966088 | tf_op jit(solution)/shard_map/ppermute | solution.py:17
  11.1 43.9 %collective-permute-start.5 = (bf16[8,32,1280]{2,1,0:T(8,128)(2,1)}, bf16[8,32,1280]{2,1,0:T(8,128)(2,1)}, u32[]{:S(2)}, u32[]{:S(2)}) collective-permute-start(bf16[8,32,1280]{2,1,0:T(8,128)(2,1)} %constant_dynamic-slice_fusion.3), channel_id=1, source_target_pairs={{0,3},{1,2},{2,1},{3,0},{4,7},{5,6},{6,5},{7,4},{8,11},{9,10},{10,... | collective-permute-start | bytes 1966088 | tf_op jit(solution)/shard_map/ppermute | solution.py:17
  13.7 10.5 %collective-permute-start = (bf16[8,32,1280]{2,1,0:T(8,128)(2,1)}, bf16[8,32,1280]{2,1,0:T(8,128)(2,1)}, u32[]{:S(2)}, u32[]{:S(2)}) collective-permute-start(bf16[8,32,1280]{2,1,0:T(8,128)(2,1)} %constant_dynamic-slice_fusion.2), channel_id=1, source_target_pairs={{0,1},{1,0},{2,3},{3,2},{4,5},{5,4},{6,7},{7,6},{8,9},{9,8},{10,11... | collective-permute-start | bytes 1966088 | tf_op jit(solution)/shard_map/ppermute | solution.py:17
  15.2 4.1 %copy-start.4 = (bf16[8,32,1280]{2,1,0:T(8,128)(2,1)}, bf16[8,32,1280]{2,1,0:T(8,128)(2,1)S(1)}, u32[]{:S(2)}) copy-start(bf16[8,32,1280]{2,1,0:T(8,128)(2,1)S(1)} %constant_dynamic-slice_fusion.1.refs_4_) | copy-start | bytes 1966084
  15.2 4.1 %copy-start.2 = (bf16[1,8,128,1280]{3,2,1,0:T(8,128)(2,1)S(1)}, bf16[1,8,128,1280]{3,2,1,0:T(8,128)(2,1)}, u32[]{:S(2)}) copy-start(bf16[1,8,128,1280]{3,2,1,0:T(8,128)(2,1)} %param.11) | copy-start | bytes 7864324
  24.2 40.6 %collective-permute-start.4 = (bf16[8,32,1280]{2,1,0:T(8,128)(2,1)}, bf16[8,32,1280]{2,1,0:T(8,128)(2,1)}, u32[]{:S(2)}, u32[]{:S(2)}) collective-permute-start(bf16[8,32,1280]{2,1,0:T(8,128)(2,1)} %constant_dynamic-slice_fusion.4), channel_id=1, source_target_pairs={{0,2},{1,3},{2,0},{3,1},{4,6},{5,7},{6,4},{7,5},{8,10},{9,11},{10,... | collective-permute-start | bytes 1966088 | tf_op jit(solution)/shard_map/ppermute | solution.py:17
  28.3 14.5 %copy-start.18 = (f32[1280]{0:T(1024)S(1)}, f32[1280]{0:T(1024)}, u32[]{:S(2)}) copy-start(f32[1280]{0:T(1024)} %param.10) | copy-start | bytes 15364
  35.7 0.9 copy-start.3
  42.8 4.2 %copy-start.9 = (bf16[8,32,1280]{2,1,0:T(8,128)(2,1)S(1)}, bf16[8,32,1280]{2,1,0:T(8,128)(2,1)}, u32[]{:S(2)}) copy-start(bf16[8,32,1280]{2,1,0:T(8,128)(2,1)} %get-tuple-element.79.refs_2_) | copy-start | bytes 1966084
  42.8 4.2 %copy-start.17 = (bf16[1280,1280]{1,0:T(8,128)(2,1)S(1)}, bf16[1280,1280]{1,0:T(8,128)(2,1)}, u32[]{:S(2)}) copy-start(bf16[1280,1280]{1,0:T(8,128)(2,1)} %weight_ref.1) | copy-start | bytes 9830404
  47.0 4.1 %copy-start.8 = (bf16[8,32,1280]{2,1,0:T(8,128)(2,1)S(1)}, bf16[8,32,1280]{2,1,0:T(8,128)(2,1)}, u32[]{:S(2)}) copy-start(bf16[8,32,1280]{2,1,0:T(8,128)(2,1)} %get-tuple-element.78.refs_1_) | copy-start | bytes 1966084
  48.9 35.8 %collective-permute-start.12 = (bf16[8,32,1280]{2,1,0:T(8,128)(2,1)}, bf16[8,32,1280]{2,1,0:T(8,128)(2,1)S(1)}, u32[]{:S(2)}, u32[]{:S(2)}) collective-permute-start(bf16[8,32,1280]{2,1,0:T(8,128)(2,1)} %bitcast.24), channel_id=1, source_target_pairs={{0,3},{1,2},{2,1},{3,0},{4,7},{5,6},{6,5},{7,4},{8,11},{9,10},{10,... | collective-permute-start | bytes 1966088 | tf_op jit(solution)/shard_map/ppermute | solution.py:17
  51.1 1.9 %copy-start.7 = (bf16[8,32,1280]{2,1,0:T(8,128)(2,1)S(1)}, bf16[8,32,1280]{2,1,0:T(8,128)(2,1)}, u32[]{:S(2)}) copy-start(bf16[8,32,1280]{2,1,0:T(8,128)(2,1)} %get-tuple-element.76.refs_0_) | copy-start | bytes 1966084
  73.3 2.2 %collective-permute-start.8 = (bf16[8,40,640]{2,1,0:T(8,128)(2,1)}, bf16[8,40,640]{2,1,0:T(8,128)(2,1)}, u32[]{:S(2)}, u32[]{:S(2)}) collective-permute-start(bf16[8,40,640]{2,1,0:T(8,128)(2,1)} %get-tuple-element.91), channel_id=1, source_target_pairs={{0,1},{1,0},{2,3},{3,2},{4,5},{5,4},{6,7},{7,6},{8,9},{9,8},{10,11... | collective-permute-start | bytes 1228808 | tf_op jit(solution)/shard_map/ppermute | solution.py:17
  73.4 2.7 %collective-permute-start.9 = (bf16[8,40,640]{2,1,0:T(8,128)(2,1)}, bf16[8,40,640]{2,1,0:T(8,128)(2,1)}, u32[]{:S(2)}, u32[]{:S(2)}) collective-permute-start(bf16[8,40,640]{2,1,0:T(8,128)(2,1)} %get-tuple-element.93), channel_id=1, source_target_pairs={{0,1},{1,0},{2,3},{3,2},{4,5},{5,4},{6,7},{7,6},{8,9},{9,8},{10,11... | collective-permute-start | bytes 1228808 | tf_op jit(solution)/shard_map/ppermute | solution.py:17
  73.9 3.6 %collective-permute-start.7 = (bf16[8,40,640]{2,1,0:T(8,128)(2,1)}, bf16[8,40,640]{2,1,0:T(8,128)(2,1)}, u32[]{:S(2)}, u32[]{:S(2)}) collective-permute-start(bf16[8,40,640]{2,1,0:T(8,128)(2,1)} %get-tuple-element.90), channel_id=1, source_target_pairs={{0,1},{1,0},{2,3},{3,2},{4,5},{5,4},{6,7},{7,6},{8,9},{9,8},{10,11... | collective-permute-start | bytes 1228808 | tf_op jit(solution)/shard_map/ppermute | solution.py:17
  74.0 3.6 %collective-permute-start.6 = (bf16[8,40,640]{2,1,0:T(8,128)(2,1)}, bf16[8,40,640]{2,1,0:T(8,128)(2,1)}, u32[]{:S(2)}, u32[]{:S(2)}) collective-permute-start(bf16[8,40,640]{2,1,0:T(8,128)(2,1)} %get-tuple-element.88), channel_id=1, source_target_pairs={{0,1},{1,0},{2,3},{3,2},{4,5},{5,4},{6,7},{7,6},{8,9},{9,8},{10,11... | collective-permute-start | bytes 1228808 | tf_op jit(solution)/shard_map/ppermute | solution.py:17
  75.5 17.0 %collective-permute-start.10 = (bf16[8,32,1280]{2,1,0:T(8,128)(2,1)}, bf16[8,32,1280]{2,1,0:T(8,128)(2,1)}, u32[]{:S(2)}, u32[]{:S(2)}) collective-permute-start(bf16[8,32,1280]{2,1,0:T(8,128)(2,1)} %bitcast.75), channel_id=1, source_target_pairs={{0,1},{1,0},{2,3},{3,2},{4,5},{5,4},{6,7},{7,6},{8,9},{9,8},{10,11... | collective-permute-start | bytes 1966088 | tf_op jit(solution)/shard_map/ppermute | solution.py:17
  76.1 17.7 %collective-permute-start.11 = (bf16[8,32,1280]{2,1,0:T(8,128)(2,1)}, bf16[8,32,1280]{2,1,0:T(8,128)(2,1)}, u32[]{:S(2)}, u32[]{:S(2)}) collective-permute-start(bf16[8,32,1280]{2,1,0:T(8,128)(2,1)} %bitcast.74), channel_id=1, source_target_pairs={{0,2},{1,3},{2,0},{3,1},{4,6},{5,7},{6,4},{7,5},{8,10},{9,11},{10,... | collective-permute-start | bytes 1966088 | tf_op jit(solution)/shard_map/ppermute | solution.py:17
  81.6 12.8 %collective-permute-start.13 = (bf16[8,40,640]{2,1,0:T(8,128)(2,1)}, bf16[8,40,640]{2,1,0:T(8,128)(2,1)}, u32[]{:S(2)}, u32[]{:S(2)}) collective-permute-start(bf16[8,40,640]{2,1,0:T(8,128)(2,1)} %get-tuple-element.96), channel_id=1, source_target_pairs={{0,4},{4,0},{8,12},{12,8},{16,20},{20,16},{24,28},{28,24},{1,5},{5... | collective-permute-start | bytes 1228808 | tf_op jit(solution)/shard_map/ppermute | solution.py:17
  83.2 11.3 %collective-permute-start.14 = (bf16[8,40,640]{2,1,0:T(8,128)(2,1)}, bf16[8,40,640]{2,1,0:T(8,128)(2,1)}, u32[]{:S(2)}, u32[]{:S(2)}) collective-permute-start(bf16[8,40,640]{2,1,0:T(8,128)(2,1)} %get-tuple-element.97), channel_id=1, source_target_pairs={{0,8},{4,12},{8,0},{12,4},{16,24},{20,28},{24,16},{28,20},{1,9},{5... | collective-permute-start | bytes 1228808 | tf_op jit(solution)/shard_map/ppermute | solution.py:17
  84.7 7.7 %copy-start.5 = (bf16[8,32,1280]{2,1,0:T(8,128)(2,1)}, bf16[8,32,1280]{2,1,0:T(8,128)(2,1)S(1)}, u32[]{:S(2)}) copy-start(bf16[8,32,1280]{2,1,0:T(8,128)(2,1)S(1)} %collective-permute-done.12.refs_3_) | copy-start | bytes 1966084
  92.4 11.1 %collective-permute-start.15 = (bf16[8,32,1280]{2,1,0:T(8,128)(2,1)}, bf16[8,32,1280]{2,1,0:T(8,128)(2,1)S(1)}, u32[]{:S(2)}, u32[]{:S(2)}) collective-permute-start(bf16[8,32,1280]{2,1,0:T(8,128)(2,1)} %get-tuple-element.100), channel_id=1, source_target_pairs={{0,1},{1,0},{2,3},{3,2},{4,5},{5,4},{6,7},{7,6},{8,9},{9,8},{10,11... | collective-permute-start | bytes 1966088 | tf_op jit(solution)/shard_map/ppermute | solution.py:17
  92.5 34.2 %collective-permute-start.22 = (bf16[8,32,1280]{2,1,0:T(8,128)(2,1)}, bf16[8,32,1280]{2,1,0:T(8,128)(2,1)}, u32[]{:S(2)}, u32[]{:S(2)}) collective-permute-start(bf16[8,32,1280]{2,1,0:T(8,128)(2,1)} %get-tuple-element.101), channel_id=1, source_target_pairs={{0,2},{1,3},{2,0},{3,1},{4,6},{5,7},{6,4},{7,5},{8,10},{9,11},{10,... | collective-permute-start | bytes 1966088 | tf_op jit(solution)/shard_map/ppermute | solution.py:17
  93.8 35.6 %collective-permute-start.23 = (bf16[8,32,1280]{2,1,0:T(8,128)(2,1)}, bf16[8,32,1280]{2,1,0:T(8,128)(2,1)}, u32[]{:S(2)}, u32[]{:S(2)}) collective-permute-start(bf16[8,32,1280]{2,1,0:T(8,128)(2,1)} %get-tuple-element.102), channel_id=1, source_target_pairs={{0,3},{1,2},{2,1},{3,0},{4,7},{5,6},{6,5},{7,4},{8,11},{9,10},{10,... | collective-permute-start | bytes 1966088 | tf_op jit(solution)/shard_map/ppermute | solution.py:17
  97.2 7.5 %collective-permute-start.16 = (bf16[4,40,640]{2,1,0:T(8,128)(2,1)}, bf16[4,40,640]{2,1,0:T(8,128)(2,1)S(1)}, u32[]{:S(2)}, u32[]{:S(2)}) collective-permute-start(bf16[4,40,640]{2,1,0:T(8,128)(2,1)} %get-tuple-element.105), channel_id=1, source_target_pairs={{0,8},{4,12},{8,0},{12,4},{16,24},{20,28},{24,16},{28,20},{1,9},{5... | collective-permute-start | bytes 614408 | tf_op jit(solution)/shard_map/ppermute | solution.py:17
  98.8 7.3 %collective-permute-start.17 = (bf16[4,40,640]{2,1,0:T(8,128)(2,1)}, bf16[4,40,640]{2,1,0:T(8,128)(2,1)}, u32[]{:S(2)}, u32[]{:S(2)}) collective-permute-start(bf16[4,40,640]{2,1,0:T(8,128)(2,1)} %get-tuple-element.106), channel_id=1, source_target_pairs={{0,4},{4,0},{8,12},{12,8},{16,20},{20,16},{24,28},{28,24},{1,5},{5... | collective-permute-start | bytes 614408 | tf_op jit(solution)/shard_map/ppermute | solution.py:17
  103.5 14.4 %copy-start.6 = (bf16[8,32,1280]{2,1,0:T(8,128)(2,1)}, bf16[8,32,1280]{2,1,0:T(8,128)(2,1)S(1)}, u32[]{:S(2)}) copy-start(bf16[8,32,1280]{2,1,0:T(8,128)(2,1)S(1)} %collective-permute-done.15.refs_1_) | copy-start | bytes 1966084
  104.7 1.4 %copy-start.11 = (bf16[4,40,640]{2,1,0:T(8,128)(2,1)}, bf16[4,40,640]{2,1,0:T(8,128)(2,1)S(1)}, u32[]{:S(2)}) copy-start(bf16[4,40,640]{2,1,0:T(8,128)(2,1)S(1)} %collective-permute-done.16.refs_2_) | copy-start | bytes 614404
  108.3 13.6 %collective-permute-start.21 = (bf16[2,40,1280]{2,1,0:T(8,128)(2,1)}, bf16[2,40,1280]{2,1,0:T(8,128)(2,1)S(1)}, u32[]{:S(2)}, u32[]{:S(2)}) collective-permute-start(bf16[2,40,1280]{2,1,0:T(8,128)(2,1)} %get-tuple-element.112), channel_id=1, source_target_pairs={{0,16},{4,20},{8,24},{12,28},{16,0},{20,4},{24,8},{28,12},{1,17},{... | collective-permute-start | bytes 614408 | tf_op jit(solution)/shard_map/ppermute | solution.py:17
  110.9 1.4 %collective-permute-start.18 = (f32[56,128]{1,0:T(8,128)}, f32[56,128]{1,0:T(8,128)S(1)}, u32[]{:S(2)}, u32[]{:S(2)}) collective-permute-start(f32[56,128]{1,0:T(8,128)} %late_sums.1), channel_id=1, source_target_pairs={{0,1},{1,0},{2,3},{3,2},{4,5},{5,4},{6,7},{7,6},{8,9},{9,8},{10,11... | collective-permute-start | bytes 86024 | tf_op jit(solution)/shard_map/ppermute | solution.py:17
  113.1 4.8 %collective-permute-start.19 = (f32[56,128]{1,0:T(8,128)S(1)}, f32[56,128]{1,0:T(8,128)S(1)}, u32[]{:S(2)}, u32[]{:S(2)}) collective-permute-start(f32[56,128]{1,0:T(8,128)S(1)} %add.60), channel_id=1, source_target_pairs={{0,4},{4,0},{8,12},{12,8},{16,20},{20,16},{24,28},{28,24},{1,5},{5... | collective-permute-start | bytes 86024 | tf_op jit(solution)/shard_map/ppermute | solution.py:17
  117.9 3.9 %collective-permute-start.20 = (f32[56,128]{1,0:T(8,128)S(1)}, f32[56,128]{1,0:T(8,128)S(1)}, u32[]{:S(2)}, u32[]{:S(2)}) collective-permute-start(f32[56,128]{1,0:T(8,128)S(1)} %add.61), channel_id=1, source_target_pairs={{0,8},{4,12},{8,0},{12,4},{16,24},{20,28},{24,16},{28,20},{1,9},{5... | collective-permute-start | bytes 86024 | tf_op jit(solution)/shard_map/ppermute | solution.py:17
  121.9 10.8 %copy-start.12 = (f32[56,128]{1,0:T(8,128)}, f32[56,128]{1,0:T(8,128)S(1)}, u32[]{:S(2)}) copy-start(f32[56,128]{1,0:T(8,128)S(1)} %add.62.refs_0_) | copy-start | bytes 86020
  121.9 0.7 copy-start.10
  124.4 8.3 %collective-permute-start.24 = (bf16[1,40,1280]{2,1,0:T(8,128)(2,1)}, bf16[1,40,1280]{2,1,0:T(8,128)(2,1)S(1)}, u32[]{:S(2)}, u32[]{:S(2)}) collective-permute-start(bf16[1,40,1280]{2,1,0:T(8,128)(2,1)} %get-tuple-element.118), channel_id=1, source_target_pairs={{0,2},{1,3},{2,0},{3,1},{4,6},{5,7},{6,4},{7,5},{8,10},{9,11},{10,... | collective-permute-start | bytes 307208 | tf_op jit(solution)/shard_map/ppermute | solution.py:17
  124.9 7.7 %collective-permute-start.27 = (f32[56,128]{1,0:T(8,128)S(1)}, f32[56,128]{1,0:T(8,128)S(1)}, u32[]{:S(2)}, u32[]{:S(2)}) collective-permute-start(f32[56,128]{1,0:T(8,128)S(1)} %add.62.refs_0_), channel_id=1, source_target_pairs={{0,18},{1,19},{2,16},{3,17},{4,22},{5,23},{6,20},{7,21},{8,26},{9,... | collective-permute-start | bytes 86024 | tf_op jit(solution)/shard_map/ppermute | solution.py:17
  126.2 6.5 %collective-permute-start.26 = (f32[56,128]{1,0:T(8,128)S(1)}, f32[56,128]{1,0:T(8,128)S(1)}, u32[]{:S(2)}, u32[]{:S(2)}) collective-permute-start(f32[56,128]{1,0:T(8,128)S(1)} %add.62.refs_0_), channel_id=1, source_target_pairs={{0,2},{1,3},{2,0},{3,1},{4,6},{5,7},{6,4},{7,5},{8,10},{9,11},{10,... | collective-permute-start | bytes 86024 | tf_op jit(solution)/shard_map/ppermute | solution.py:17
  126.8 5.9 %collective-permute-start.25 = (f32[56,128]{1,0:T(8,128)S(1)}, f32[56,128]{1,0:T(8,128)S(1)}, u32[]{:S(2)}, u32[]{:S(2)}) collective-permute-start(f32[56,128]{1,0:T(8,128)S(1)} %add.62.refs_0_), channel_id=1, source_target_pairs={{0,16},{4,20},{8,24},{12,28},{16,0},{20,4},{24,8},{28,12},{1,17},{... | collective-permute-start | bytes 86024 | tf_op jit(solution)/shard_map/ppermute | solution.py:17
  132.7 0.6 copy-start.14
  132.7 0.6 copy-start.15
  132.7 0.6 copy-start.16
  132.7 0.6 copy-start.13
